TPU v7x, 32 devices: a whole 2x2x4 slice. The times are simulated.
32 devices in a mesh: space: 16 (over z, y, core), frame: 2 (over x).
Axes of the slice: x: 2, y: 2, z: 4, core: 2. Of those that a mesh axis runs over, the one named last changes fastest.
Arguments:
- raw_sequence: bfloat16 [4, 256, 512], P('frame', 'space'), may hold values from -12 to 12
- tile_shifts_grid: int32 [4, 2, 16, 32], P('frame', None, 'space'), may hold values from -16 to 16, as said below
- color_layer_kernel: bfloat16 [32, 36], replicated, may hold values from -1 to 1
- color_layer_offset: float32 [32], replicated, may hold values from -0.5 to 0.5
- log_variance_spectrum: float32 [256], replicated, may hold values from 4 to 8
- goal_features: bfloat16 [32, 128, 256], P(None, 'space', 'frame'), may hold values from -3 to 3
Outputs:
- merged: float32 [256, 512], P('space', 'frame')
- grad_weight: float32 [32, 36], replicated
- grad_bias: float32 [32], replicated
- grad_log_noise: float32 [256], replicated
Inputs may be any that keep to these rules, and one draw needn't show every extreme that they name: tile_shifts_grid[0] (the reference frame) is zero; the other frames' displacements reach both ends of the range.
All inputs are finite; a program needn't handle non-finite values.
Results may differ from a plain program's by a relative error of at most 0.00033.
Values may be sent and summed in bfloat16 or wider, within the bound.
No kernel may reach another device: no remote copies, remote signals or barrier semaphores. Data moves between devices by JAX's collectives and lax.ppermute only.
A program may use at most 64 MiB of HBM per device.

v0:
```python
import functools
import math

import jax
import jax.numpy as jnp
import ml_dtypes
import numpy as np
from jax import lax
from jax.experimental import pallas as pl
from jax.experimental.pallas import tpu as pltpu
from jax.sharding import PartitionSpec as P


TILE = 16
LANES = 128
F32 = jnp.float32
BF16 = jnp.bfloat16


def dot(a, b, dims=((1,), (0,))):
    return lax.dot_general(a, b, (dims, ((), ())), preferred_element_type=F32)


def split(value, parts):
    terms = []
    for _ in range(parts):
        term = value.astype(BF16)
        terms.append(term)
        value = value - term.astype(F32)
    return terms


def split_table(value, parts):
    terms = []
    value = value.astype(np.float64)
    for _ in range(parts):
        term = value.astype(np.float32).astype(ml_dtypes.bfloat16)
        terms.append(term)
        value = value - term.astype(np.float64)
    return terms


def tables():
    angle = 2.0 * math.pi / TILE * (np.outer(np.arange(TILE), np.arange(TILE)) % TILE)
    cos16, sin16 = np.cos(angle), np.sin(angle)
    eye8, eye16 = np.eye(8), np.eye(16)
    bc, bs = np.kron(eye8, cos16), np.kron(eye8, sin16)
    fwd = split_table(np.concatenate([bc, bs], axis=1), 3)
    fwd_main = np.concatenate(fwd[:2], axis=0)
    inv = split_table(np.concatenate([bc, -bs], axis=0), 3)
    inv_main = np.concatenate(inv[:2], axis=1)
    part = np.zeros((256, 256))
    for x in range(256):
        part[x, (x % 2) * 128 + x // 2] = 1.0
    wide = np.concatenate([np.kron(eye16, cos16), np.kron(eye16, sin16)], axis=1)
    wide = split_table(part.T @ wide, 2)
    return fwd_main, fwd[2], inv_main, inv[2], part.astype(ml_dtypes.bfloat16), wide[0], wide[1]


def tap_tables():
    place = np.zeros((36, 10, 144))
    back = np.zeros((96, 10, 36))
    pick = np.zeros((256, 128))
    for a in range(3):
        for b in range(3):
            for p in range(2):
                for q in range(2):
                    tap = (3 * a + b) * 4 + 2 * p + q
                    pick[(q * 3 + b) * 24 + 2 * a + p, tap] = 1.0
                    for sy in range(10):
                        r = 2 * (sy + a) + p
                        place[tap, sy, (q * 3 + b) * 24 + r] = 1.0
                        if 4 <= r < 20:
                            back[(q * 3 + b) * 16 + r - 4, sy, tap] = 1.0
    return place, back, pick.astype(ml_dtypes.bfloat16)


def turn(re, im, k, n):
    if k == 0:
        return re, im
    if 4 * k == n:
        return im, -re
    if 8 * k == n:
        half = math.sqrt(0.5)
        return (re + im) * half, (im - re) * half
    if 8 * k == 3 * n:
        half = math.sqrt(0.5)
        return (im - re) * half, (re + im) * -half
    c, s = math.cos(2.0 * math.pi * k / n), math.sin(2.0 * math.pi * k / n)
    return re * c + im * s, im * c - re * s


def fft(re, im):
    n = len(re)
    if n == 1:
        return re, im
    er, ei = fft(re[0::2], im[0::2])
    our, oi = fft(re[1::2], im[1::2])
    half = n // 2
    xr, xi = [None] * n, [None] * n
    for k in range(half):
        tr, ti = turn(our[k], oi[k], k, n)
        xr[k], xi[k] = er[k] + tr, ei[k] + ti
        xr[k + half], xi[k + half] = er[k] - tr, ei[k] - ti
    return xr, xi


def tree(values):
    while len(values) > 1:
        half = len(values) // 2
        values = [a + b for a, b in zip(values[:half], values[half:])]
    return values[0]


def add_lists(a, b):
    return b if a is None else [x + y for x, y in zip(a, b)]


def merge_kernel(dims, *refs):
    nf, fl, G, T, nsc = dims
    F = nf * fl
    dy_refs, refs = refs[:nf], refs[nf:]
    dx_refs, refs = refs[:nf], refs[nf:]
    goal_refs, refs = refs[:nf], refs[nf:]
    y_ref, yc_ref, yf_ref, fwd_ref, fwdl_ref, inv_ref, invl_ref, var_ref = refs[:8]
    merged_ref, pack_ref, pc_ref, pf_ref, h_ref = refs[8:13]
    x_ref, idx_ref, p_ref, q_ref, xs_ref, mm_ref, goal_ref = refs[13:]
    s = lax.axis_index("space")
    fr = lax.axis_index("frame")
    odd = lax.rem(s, 2)

    slots = ((y_ref, 1), (yc_ref, 2 - 2 * odd), (yf_ref, 2 * odd))

    def fill(f, carry):
        for ref, slot in slots:
            rows = ref[f].astype(F32)
            for g in range(G):
                block = rows[:, g * LANES : (g + 1) * LANES]
                x_ref[f * G + g, pl.ds(pl.multiple_of(slot * TILE, TILE), TILE), :] = block
        return carry

    lax.fori_loop(0, F, fill, 0, unroll=min(F, 4))

    spot = lax.broadcasted_iota(jnp.int32, (8, LANES), 1)
    for j in range(nf):
        for l in range(fl):
            row = dx_refs[j][l, 1]
            if T < LANES:
                row = jnp.concatenate([row, jnp.zeros((1, LANES - T), jnp.int32)], axis=1)
            row = jnp.broadcast_to(row, (8, LANES))
            for g in range(G):
                moved = jnp.take_along_axis(row, 8 * g + spot // TILE, axis=1)
                idx_ref[(j * fl + l) * G + g] = (moved + (spot - TILE)) & (LANES - 1)

    lead = G * 4
    for j in range(nf):
        for c in range(nsc):
            cols = slice(c * LANES, (c + 1) * LANES)
            goal_ref[j * nsc + c] = goal_refs[j][:, :, cols].astype(F32).reshape(256, LANES)
    for k in range(nf * nsc):
        rows = slice(lead + k * 32, lead + k * 32 + 32)
        pc_ref[rows, :] = goal_ref[k, pl.ds(7 - 7 * odd, 32, stride=8), :].astype(BF16)
        pf_ref[rows, :] = goal_ref[k, pl.ds(7 * odd, 32, stride=8), :].astype(BF16)

    lane = lax.broadcasted_iota(jnp.int32, (TILE, LANES), 1)
    kind = (lane // TILE) % 4
    per = 16 // G
    chunks = F * G // 16
    rows_out = max(G, 8)
    fold = TILE // rows_out
    zero = jnp.zeros((TILE, LANES), F32)

    def place(f):
        if nf == 2:
            return f
        return lax.rem(f // fl + nf - fr, nf) * fl + f % fl

    def row_shift(f, t):
        if isinstance(f, int):
            return dy_refs[f // fl][f % fl, 0, 0, t]
        j = lax.div(f, fl)
        l = lax.rem(f, fl)
        value = dy_refs[0][l, 0, 0, t]
        for k in range(1, nf):
            value = jnp.where(j == k, dy_refs[k][l, 0, 0, t], value)
        return value

    first = lax.rem(nf - fr, nf) * fl
    log_var = var_ref[...]
    variances = []
    for k in range(16):
        row = jnp.broadcast_to(log_var[k // 8 : k // 8 + 1], (8, LANES))
        row = jnp.take_along_axis(row, (k % 8) * TILE + spot % TILE, axis=1)
        variances.append(jnp.concatenate([row, row], axis=0))

    def chunk_step(c, carry):
        sums = carry[0] if carry is not None else None
        blocks = []
        for q in range(16):
            g = q % G
            f = place(c * per + q // G)

            def load(t, group):
                if group < 0 or group >= G:
                    return zero
                start = row_shift(f, 8 * g + t)
                return x_ref[f * G + group, pl.ds(start, TILE), :]

            idx = idx_ref[f * G + g]
            idx = jnp.concatenate([idx, idx], axis=0)
            mixes = (
                jnp.where(
                    lane < 40,
                    load(0, g),
                    jnp.where(lane < 104, load(4, g), load(0, g - 1)),
                ),
                jnp.where(lane < 56, load(1, g), load(5, g)),
                jnp.where(lane < 72, load(2, g), load(6, g)),
                jnp.where(
                    lane < 24,
                    load(7, g + 1),
                    jnp.where(lane < 88, load(3, g), load(7, g)),
                ),
            )
            moved = [jnp.take_along_axis(m, idx, axis=1) for m in mixes]
            blocks.append(
                jnp.where(
                    kind < 2,
                    jnp.where(kind == 0, moved[0], moved[1]),
                    jnp.where(kind == 2, moved[2], moved[3]),
                )
            )
        part = [tree(blocks[g::G]) for g in range(G)]
        sums = add_lists(sums, part)
        base = [x_ref[first * G + g, TILE : 2 * TILE, :] for g in range(G)]
        both = jnp.concatenate(blocks + base, axis=0).astype(BF16)
        pq = dot(jnp.concatenate([both, both], axis=1), fwd_ref[...]) + dot(both, fwdl_ref[...])
        for q in range(16):
            rows = slice(q * TILE, (q + 1) * TILE)
            ref_rows = slice(256 + (q % G) * TILE, 256 + (q % G + 1) * TILE)
            diff = pq[ref_rows] - pq[rows]
            p_ref[rows, :] = diff[:, :LANES]
            q_ref[rows, :] = -diff[:, LANES:]
        re, im = fft(
            [p_ref[pl.ds(n, 16, stride=16), :] for n in range(16)],
            [q_ref[pl.ds(n, 16, stride=16), :] for n in range(16)],
        )
        out = [[], [], [], []]
        for k in range(16):
            energy = re[k] * re[k] + im[k] * im[k]
            weight = energy / (energy + variances[k])
            wr = weight * re[k]
            wi = weight * im[k]
            rest = 1.0 - weight
            for store, val in zip(out, (wr, wi, wr * rest, wi * rest)):
                if fold == 2:
                    val = val[:8] + val[8:]
                store.append(val)
        flat = out[0] + out[1] + out[2] + out[3]
        return sums, add_lists(carry[1] if carry is not None else None, flat)

    carry = chunk_step(0, None)
    if chunks > 1:
        carry = lax.fori_loop(1, chunks, chunk_step, carry)
    sums, flat = carry
    for k in range(32):
        h_ref[k * rows_out : (k + 1) * rows_out, :] = flat[32 + k]

    vi, ur = fft(flat[16:32], flat[:16])
    uv = jnp.concatenate(
        [jnp.concatenate(ur, axis=0), jnp.concatenate(vi, axis=0)], axis=1
    )
    m = 16 * rows_out
    terms = split(uv, 3)
    wide = dot(jnp.concatenate(terms, axis=0), inv_ref[...])
    pix = wide[:m, :LANES] + (wide[m : 2 * m, :LANES] + wide[:m, LANES:])
    pix = pix + (wide[2 * m :, :LANES] + wide[m : 2 * m, LANES:] + dot(terms[0], invl_ref[...]))
    xs_ref[...] = pix
    for g in range(G):
        val = xs_ref[pl.ds(g, 16, stride=rows_out), :]
        for other in range(g + G, rows_out, G):
            val = val + xs_ref[pl.ds(other, 16, stride=rows_out), :]
        val = (sums[g] + val / 256.0) / F
        mm_ref[g] = val
        pack_ref[g] = val
    own = G // nf
    for k in range(own):
        merged_ref[:, k * LANES : (k + 1) * LANES] = mm_ref[fr * own + k]
    low = jnp.concatenate([mm_ref[g, 0:4, :] for g in range(G)], axis=0)
    high = jnp.concatenate([mm_ref[g, 12:16, :] for g in range(G)], axis=0)
    pc_ref[0:lead, :] = jnp.where(odd == 1, low, high).astype(BF16)
    pf_ref[0:lead, :] = jnp.where(odd == 1, high, low).astype(BF16)


def demosaic_kernel(dims, pack_ref, pc_ref, pf_ref, h_ref, *refs):
    nf, fl, G, nsc, n_space, inv_pixels = dims
    F = nf * fl
    W = G * LANES
    half = W // 2
    goal_refs = refs[:nf]
    part_ref, wideh_ref, widel_ref, pick_ref, big_ref, bigt_ref, offs_ref = refs[nf : nf + 7]
    out_ref, goal_ref, raw_ref, mm_ref, p_ref, q_ref, ns_ref = refs[nf + 7 :]
    s = lax.axis_index("space")
    fr = lax.axis_index("frame")
    odd = lax.rem(s, 2)
    rows_out = max(G, 8)

    lead = G * 4
    for j in range(nf):
        at = pl.multiple_of(lax.rem(fr + j, nf) * (nsc * LANES), LANES)
        for c in range(nsc):
            cols = slice(c * LANES, (c + 1) * LANES)
            raw_ref[...] = goal_refs[j][:, :, cols].astype(F32).reshape(256, LANES)
            to = pl.ds(pl.multiple_of(at + c * LANES, LANES), LANES)
            for r in range(8):
                goal_ref[r + 1, :, to] = raw_ref[pl.ds(r, 32, stride=8), :]
        for ref, row in ((pc_ref, 9 - 9 * odd), (pf_ref, 9 * odd)):
            for c in range(nsc):
                first = lead + (j * nsc + c) * 32
                val = ref[first : first + 32, :].astype(F32)
                goal_ref[row, :, pl.ds(pl.multiple_of(at + c * LANES, LANES), LANES)] = val

    near = pc_ref[0:lead, :].astype(F32)
    far = pf_ref[0:lead, :].astype(F32)
    low = jnp.where(odd == 1, near, far)
    high = jnp.where(odd == 1, far, near)
    for g in range(G):
        mm_ref[g, 0:4, :] = low[4 * g : 4 * g + 4]
        mm_ref[g, 4:20, :] = pack_ref[g]
        mm_ref[g, 20:24, :] = high[4 * g : 4 * g + 4]
    pairs = jnp.concatenate(
        [jnp.concatenate([mm_ref[2 * h], mm_ref[2 * h + 1]], axis=1) for h in range(G // 2)],
        axis=0,
    )
    parted = dot(pairs.astype(BF16), part_ref[...])
    site = lax.broadcasted_iota(jnp.int32, (24, half), 1)
    pieces = []
    for q in range(2):
        plane = jnp.concatenate(
            [parted[24 * h : 24 * h + 24, q * 128 : (q + 1) * 128] for h in range(G // 2)], axis=1
        )
        pieces.append(jnp.where(site == 0, 0.0, pltpu.roll(plane, 1, 1)))
        pieces.append(plane)
        pieces.append(jnp.where(site == half - 1, 0.0, pltpu.roll(plane, half - 1, 1)))
    pieces.append(jnp.zeros((112, half), F32))
    taps = jnp.concatenate(pieces, axis=0).astype(BF16)

    preact = dot(big_ref[...], taps[:144])
    diag = lax.broadcasted_iota(jnp.int32, (32, LANES), 0) == lax.broadcasted_iota(
        jnp.int32, (32, LANES), 1
    )
    offs = jnp.concatenate([offs_ref[...], jnp.zeros((1, LANES - 32), F32)], axis=1)
    offs = jnp.where(diag, jnp.broadcast_to(offs, (32, LANES)), 0.0)
    offs = jnp.broadcast_to(jnp.sum(offs, axis=1, keepdims=True), (32, half))
    bias = jnp.zeros((32, half), F32)
    slopes = []
    for sy in range(10):
        v = preact[sy * 32 : sy * 32 + 32] + offs
        sig = jax.nn.sigmoid(v)
        slope = (v * sig - goal_ref[sy]) * inv_pixels * (sig * (1.0 + v * (1.0 - sig)))
        if sy == 0:
            slope = jnp.where(s == 0, 0.0, slope)
        elif sy == 9:
            slope = jnp.where(s == n_space - 1, 0.0, slope)
        else:
            bias = bias + slope
        slopes.append(slope)
    slope_bf = jnp.concatenate(slopes, axis=0).astype(BF16)

    gt = dot(bigt_ref[...], slope_bf)
    site16 = lax.broadcasted_iota(jnp.int32, (TILE, half), 1)
    planes = []
    for q in range(2):
        left, mid, right = (gt[(q * 3 + b) * 16 : (q * 3 + b) * 16 + 16] for b in range(3))
        planes.append(
            mid
            + jnp.where(site16 == half - 1, 0.0, pltpu.roll(left, half - 1, 1))
            + jnp.where(site16 == 0, 0.0, pltpu.roll(right, 1, 1))
        )
    grad = jnp.concatenate(
        [
            jnp.concatenate([p[:, h * 128 : (h + 1) * 128] for p in planes], axis=1)
            for h in range(G // 2)
        ],
        axis=0,
    )
    m = grad.shape[0]
    terms = split(grad, 2)
    pq = dot(jnp.concatenate(terms, axis=0), wideh_ref[...])
    pq = pq[:m] + (pq[m:] + dot(terms[0], widel_ref[...]))
    for r in range(rows_out):
        g = r % G
        rows = slice((g // 2) * TILE, (g // 2 + 1) * TILE)
        c0 = (g % 2) * LANES
        p_ref[r * TILE : (r + 1) * TILE, :] = pq[rows, c0 : c0 + LANES]
        q_ref[r * TILE : (r + 1) * TILE, :] = -pq[rows, 256 + c0 : 256 + c0 + LANES]
    gre, gim = fft(
        [p_ref[pl.ds(n, rows_out, stride=16), :] for n in range(16)],
        [q_ref[pl.ds(n, rows_out, stride=16), :] for n in range(16)],
    )
    for k in range(16):
        rows = slice(k * rows_out, (k + 1) * rows_out)
        rows_im = slice((16 + k) * rows_out, (17 + k) * rows_out)
        ns_ref[rows, :] = gre[k] * h_ref[rows, :] + gim[k] * h_ref[rows_im, :]
    noise = ns_ref[pl.ds(0, 16, stride=rows_out), :]
    for r in range(1, rows_out):
        noise = noise + ns_ref[pl.ds(r, 16, stride=rows_out), :]
    noise = noise * (-1.0 / (256.0 * F))
    for step in (64, 32, 16):
        noise = noise + pltpu.roll(noise, step, 1)
    lane_tile = lax.broadcasted_iota(jnp.int32, (TILE, LANES), 1) // TILE
    spot = lax.broadcasted_iota(jnp.int32, (TILE, LANES), 0) % 8
    noise = jnp.where(lane_tile == spot, noise, 0.0)
    upper = jnp.sum(noise[:8], axis=0, keepdims=True)
    lower = jnp.sum(noise[8:], axis=0, keepdims=True)

    prod = dot(slope_bf[32:288], taps, ((1,), (1,)))
    gw = jnp.zeros((32, 256), F32)
    for sy in range(1, 9):
        gw = gw + pltpu.roll(prod[(sy - 1) * 32 : sy * 32], 256 - 2 * sy, 1)
    picked = dot(jnp.concatenate(split(gw, 3), axis=0), pick_ref[...])
    out_ref[0:32, :] = picked[0:32] + (picked[32:64] + picked[64:96])
    bias = jnp.broadcast_to(jnp.sum(bias, axis=1, keepdims=True), (32, LANES))
    bias = jnp.sum(jnp.where(diag, bias, 0.0), axis=0, keepdims=True)
    row = lax.broadcasted_iota(jnp.int32, (8, LANES), 0)
    tail = jnp.where(row == 0, bias, jnp.where(row == 1, upper, jnp.where(row == 2, lower, 0.0)))
    out_ref[32:40, :] = tail


def last_sum(own_ref, got_ref, weight_ref, bias_ref, noise_ref):
    total = own_ref[...] + got_ref[...]
    weight_ref[...] = total[:32, :36]
    bias_ref[...] = total[32:33, :32]
    noise_ref[...] = total[33:35]


def involution(value, count, step, first):
    pairs = []
    for i in range(first, count):
        j = ((i - first) ^ step) + first
        if j < count:
            pairs.append((i, j))
    return lax.ppermute(value, "space", pairs)


def sum_space(value, count):
    bits = count.bit_length() - 1
    assert 1 << bits == count
    stages = []
    at = 0
    while at < bits:
        width = 2 if at == 1 and bits - at >= 3 else 1
        stages.append([m << at for m in range(1, 1 << width)])
        at += width
    for masks in stages[:-1]:
        got = [lax.ppermute(value, "space", [(i, i ^ m) for i in range(count)]) for m in masks]
        value = value + got[0]
        if len(got) == 3:
            value = value + (got[1] + got[2])
    (mask,) = stages[-1]
    got = lax.ppermute(value, "space", [(i, i ^ mask) for i in range(count)])
    return value, got


def call(body, args, smem, outs, scratch):
    vm = pl.BlockSpec(memory_space=pltpu.VMEM)
    sm = pl.BlockSpec(memory_space=pltpu.SMEM)
    sizes = [int(np.prod(a.shape)) * a.dtype.itemsize for a in list(args) + list(outs)]
    sizes += [int(np.prod(a.shape)) * 4 for a in scratch]
    return pl.pallas_call(
        body,
        out_shape=tuple(outs),
        in_specs=[sm] * smem + [vm] * (len(args) - smem),
        out_specs=(vm,) * len(outs),
        scratch_shapes=scratch,
        compiler_params=pltpu.CompilerParams(vmem_limit_bytes=sum(sizes) + (12 << 20)),
    )(*args)


def shards(raw, shifts, weight, offset, log_var, goal):
    nf = lax.axis_size("frame")
    n_space = lax.axis_size("space")
    fl, band_rows, W = raw.shape
    T = shifts.shape[3]
    channels, _, ws = goal.shape
    G = W // LANES
    F = nf * fl
    nsc = ws // LANES
    inv_pixels = 1.0 / (band_rows * n_space * W // 4)
    rows_out = max(G, 8)

    def from_frame(value, j):
        return lax.ppermute(value, "frame", [(i, (i - j) % nf) for i in range(nf)])

    def pieces(value):
        return [value] + [from_frame(value, j) for j in range(1, nf)]

    raws = pieces(raw)
    shift_parts = pieces(shifts)
    shift_parts = [v + TILE for v in shift_parts]
    y = jnp.concatenate(raws, axis=0)
    yf = involution(y, n_space, 1, 1)
    yc = involution(y, n_space, 1, 0)
    goals = pieces(goal)

    fwd, fwd_low, inv, inv_low, part, wide, wide_low = (jnp.asarray(t) for t in tables())
    place, place_t, pick = tap_tables()
    side = 4 * G + nf * nsc * channels
    shape = jax.ShapeDtypeStruct
    merged, pack, pc, pf, moments = call(
        functools.partial(merge_kernel, (nf, fl, G, T, nsc)),
        [*shift_parts, *shift_parts, *goals, y, yc, yf]
        + [fwd, fwd_low, inv, inv_low, jnp.exp(log_var).reshape(2, LANES)],
        nf,
        [
            shape((TILE, W // nf), F32),
            shape((G, TILE, LANES), F32),
            shape((side, LANES), BF16),
            shape((side, LANES), BF16),
            shape((32 * rows_out, LANES), F32),
        ],
        [
            pltpu.VMEM((F * G, 3 * TILE, LANES), F32),
            pltpu.VMEM((F * G, 8, LANES), jnp.int32),
            pltpu.VMEM((256, LANES), F32),
            pltpu.VMEM((256, LANES), F32),
            pltpu.VMEM((16 * rows_out, LANES), F32),
            pltpu.VMEM((G, TILE, LANES), F32),
            pltpu.VMEM((nf * nsc, 256, LANES), F32),
        ],
    )
    pc, pf, weight = lax.optimization_barrier((pc, pf, weight))
    pf = involution(pf, n_space, 1, 1)
    pc = involution(pc, n_space, 1, 0)
    big = dot(weight, jnp.asarray(place.reshape(36, -1), BF16))
    big = big.reshape(channels, 10, 144).transpose(1, 0, 2).reshape(320, 144).astype(BF16)
    bigt = dot(jnp.asarray(place_t.reshape(-1, 36), BF16), weight.T)
    bigt = bigt.reshape(96, 320).astype(BF16)
    (partial,) = call(
        functools.partial(demosaic_kernel, (nf, fl, G, nsc, n_space, inv_pixels)),
        [pack, pc, pf, moments, *goals, part, wide, wide_low, jnp.asarray(pick), big, bigt]
        + [offset.reshape(1, channels)],
        0,
        [shape((40, LANES), F32)],
        [
            pltpu.VMEM((10, channels, W // 2), F32),
            pltpu.VMEM((256, LANES), F32),
            pltpu.VMEM((G, 24, LANES), F32),
            pltpu.VMEM((rows_out * TILE, LANES), F32),
            pltpu.VMEM((rows_out * TILE, LANES), F32),
            pltpu.VMEM((rows_out * TILE, LANES), F32),
        ],
    )
    grad_weight, grad_bias, grad_noise = call(
        last_sum,
        sum_space(partial, n_space),
        0,
        [shape((channels, 36), F32), shape((1, channels), F32), shape((2, LANES), F32)],
        [],
    )
    return merged, grad_weight, grad_bias.reshape(channels), grad_noise.reshape(256)


def solution(mesh):
    placed = (
        P("frame", "space", None),
        P("frame", None, "space", None),
        P(),
        P(),
        P(),
        P(None, "space", "frame"),
    )

    return jax.shard_map(
        shards,
        mesh=mesh,
        in_specs=placed,
        out_specs=(P("space", "frame"), P(), P(), P()),
        check_vma=False,
    )
```

profile of v0, /device:TPU:0, one launch (start us, length us, event | category | flops | bytes accessed | tf_op | source)
XLA Modules:
  0.0 41.5 jit_solution(493336254625337210)
XLA Ops:
  0.7 3.0 %collective-permute-start = (s32[2,2,1,32]{3,2,1,0:T(1,128)}, s32[2,2,1,32]{3,2,1,0:T(1,128)S(1)}, u32[]{:S(2)}, u32[]{:S(2)}) collective-permute-start(s32[2,2,1,32]{3,2,1,0:T(1,128)} %param.17), channel_id=1, source_target_pairs={{0,1},{1,0},{2,3},{3,2},{4,5},{5,4},{6,7},{7,6},{8,9},{9,8},{10,11... | collective-permute-start | bytes 1544 | tf_op jit(solution)/shard_map/ppermute | solution.py:493
  3.8 1.9 %collective-permute-start.2 = (bf16[2,16,512]{2,1,0:T(8,128)(2,1)}, bf16[2,16,512]{2,1,0:T(8,128)(2,1)S(1)}, u32[]{:S(2)}, u32[]{:S(2)}) collective-permute-start(bf16[2,16,512]{2,1,0:T(8,128)(2,1)} %param.16), channel_id=1, source_target_pairs={{0,1},{1,0},{2,3},{3,2},{4,5},{5,4},{6,7},{7,6},{8,9},{9,8},{10,11... | collective-permute-start | bytes 98312 | tf_op jit(solution)/shard_map/ppermute | solution.py:493
  5.7 0.7 %broadcast_add_fusion.1.refs_0_.refs_2_ = s32[2,2,1,32]{3,2,1,0:T(1,128)S(1)} fusion(s32[2,2,1,32]{3,2,1,0:T(1,128)} %param.17), kind=kLoop, calls=%fused_computation.8 | loop fusion | flops 128 | bytes 1024 | tf_op jit(solution)/shard_map/add | solution.py:500
  6.4 0.8 %constant_dynamic-update-slice_fusion.1 = bf16[4,16,512]{2,1,0:T(8,128)(2,1)S(1)} fusion(bf16[2,16,512]{2,1,0:T(8,128)(2,1)} %param.16), kind=kLoop, calls=%fused_computation.5 | loop fusion | bytes 65536
  7.2 1.3 %collective-permute-done.2 = bf16[2,16,512]{2,1,0:T(8,128)(2,1)S(1)} collective-permute-done((bf16[2,16,512]{2,1,0:T(8,128)(2,1)}, bf16[2,16,512]{2,1,0:T(8,128)(2,1)S(1)}, u32[]{:S(2)}, u32[]{:S(2)}) %collective-permute-start.2) | collective-permute-done | bytes 32800 | tf_op jit(solution)/shard_map/ppermute | solution.py:493
  8.5 0.7 %collective-permute-start.4 = (bf16[4,16,512]{2,1,0:T(8,128)(2,1)S(1)}, bf16[4,16,512]{2,1,0:T(8,128)(2,1)S(1)}, u32[]{:S(2)}, u32[]{:S(2)}) collective-permute-start(bf16[4,16,512]{2,1,0:T(8,128)(2,1)S(1)} %constant_dynamic-update-slice_fusion.refs_6_), channel_id=1, source_target_pairs={{2,4},{4,2},{6,8},{8,6},{10,12},{12,10},{14,16},{16,14},{18,20},{2... | collective-permute-start | bytes 196616 | tf_op jit(solution)/shard_map/ppermute | solution.py:443
  9.2 0.6 %collective-permute-done.3.refs_7_ = bf16[4,16,512]{2,1,0:T(8,128)(2,1)S(1)} collective-permute-done((bf16[4,16,512]{2,1,0:T(8,128)(2,1)S(1)}, bf16[4,16,512]{2,1,0:T(8,128)(2,1)S(1)}, u32[]{:S(2)}, u32[]{:S(2)}) %collective-permute-start.3) | collective-permute-done | bytes 65568 | tf_op jit(solution)/shard_map/ppermute | solution.py:443
  9.8 0.9 %copy-done.5 = bf16[256,256]{1,0:T(8,128)(2,1)S(1)} copy-done((bf16[256,256]{1,0:T(8,128)(2,1)S(1)}, bf16[256,256]{1,0:T(8,128)(2,1)}, u32[]{:S(2)}) %copy-start.5) | copy-done | bytes 131096
  10.7 0.9 %copy-done.6 = bf16[256,256]{1,0:T(8,128)(2,1)S(1)} copy-done((bf16[256,256]{1,0:T(8,128)(2,1)S(1)}, bf16[256,256]{1,0:T(8,128)(2,1)}, u32[]{:S(2)}) %copy-start.6) | copy-done | bytes 131096
  11.6 0.8 %copy-done.9 = bf16[256,128]{1,0:T(8,128)(2,1)S(1)} copy-done((bf16[256,128]{1,0:T(8,128)(2,1)S(1)}, bf16[256,128]{1,0:T(8,128)(2,1)}, u32[]{:S(2)}) %copy-start.9) | copy-done | bytes 65560
  12.4 2.2 %shard_map.183 = (f32[16,256]{1,0:T(8,128)}, f32[4,16,128]{2,1,0:T(8,128)S(1)}, bf16[80,128]{1,0:T(8,128)(2,1)S(1)}, bf16[80,128]{1,0:T(8,128)(2,1)S(1)}, f32[256,128]{1,0:T(8,128)S(1)}) custom-call(s32[2,2,1,32]{3,2,1,0:T(1,128)S(1)} %broadcast_add_fusion.1.refs_0_.refs_2_, s32[2,2,1,32]{3,2,1,0:T(1,128)S(1)} %broadcast_add_fusion.refs_1_.refs_3_, ...), custom_call_target="tpu_custom_call" | custom-call | tf_op jit(solution)/shard_map/pallas_call | solution.py:470
  14.7 4.8 %collective-permute-start.5 = (bf16[80,128]{1,0:T(8,128)(2,1)S(1)}, bf16[80,128]{1,0:T(8,128)(2,1)S(1)}, u32[]{:S(2)}, u32[]{:S(2)}) collective-permute-start(bf16[80,128]{1,0:T(8,128)(2,1)S(1)} %get-tuple-element.19), channel_id=1, source_target_pairs={{0,2},{2,0},{4,6},{6,4},{8,10},{10,8},{12,14},{14,12},{16,18},{18,... | collective-permute-start | bytes 61448 | tf_op jit(solution)/shard_map/ppermute | solution.py:443
  19.5 0.7 %collective-permute-start.6 = (bf16[80,128]{1,0:T(8,128)(2,1)S(1)}, bf16[80,128]{1,0:T(8,128)(2,1)S(1)}, u32[]{:S(2)}, u32[]{:S(2)}) collective-permute-start(bf16[80,128]{1,0:T(8,128)(2,1)S(1)} %get-tuple-element.20), channel_id=1, source_target_pairs={{2,4},{4,2},{6,8},{8,6},{10,12},{12,10},{14,16},{16,14},{18,20},{2... | collective-permute-start | bytes 61448 | tf_op jit(solution)/shard_map/ppermute | solution.py:443
  20.2 0.2 fusion
  20.4 0.1 convolution_convert_fusion
  20.6 0.4 convert_element_type.17
  21.1 0.2 copy.23
  21.3 0.2 convert_element_type.22.refs_7_
  21.5 0.4 copy-done.4
  21.9 0.1 copy-done.1
  22.2 1.2 %shard_map.184 = f32[40,128]{1,0:T(8,128)S(1)} custom-call(f32[4,16,128]{2,1,0:T(8,128)S(1)} %get-tuple-element.16.pack_ref, bf16[80,128]{1,0:T(8,128)(2,1)S(1)} %collective-permute-done.5.pc_ref, bf16[80,128]{1,0:T(8,128)(2,1)S(1)} %collective-permute-done.6.pf_ref, f32[256,128]{1,0:T(8,128)S(1)} %get-tuple-element.21.h_ref, ...), custom_call_target="tpu_custom_call" | custom-call | tf_op jit(solution)/shard_map/pallas_call | solution.py:470
  23.4 4.0 %collective-permute-start.7 = (f32[40,128]{1,0:T(8,128)S(1)}, f32[40,128]{1,0:T(8,128)S(1)}, u32[]{:S(2)}, u32[]{:S(2)}) collective-permute-start(f32[40,128]{1,0:T(8,128)S(1)} %shard_map.184), channel_id=1, source_target_pairs={{0,2},{2,0},{4,6},{6,4},{8,10},{10,8},{12,14},{14,12},{16,18},{18,... | collective-permute-start | bytes 61448 | tf_op jit(solution)/shard_map/ppermute | solution.py:456
  27.4 0.8 %collective-permute-done.7 = f32[40,128]{1,0:T(8,128)S(1)} collective-permute-done((f32[40,128]{1,0:T(8,128)S(1)}, f32[40,128]{1,0:T(8,128)S(1)}, u32[]{:S(2)}, u32[]{:S(2)}) %collective-permute-start.7) | collective-permute-done | bytes 20512 | tf_op jit(solution)/shard_map/ppermute | solution.py:456
  28.3 2.7 %collective-permute-start.9 = (f32[40,128]{1,0:T(8,128)S(1)}, f32[40,128]{1,0:T(8,128)S(1)}, u32[]{:S(2)}, u32[]{:S(2)}) collective-permute-start(f32[40,128]{1,0:T(8,128)S(1)} %add.20), channel_id=1, source_target_pairs={{0,8},{2,10},{4,12},{6,14},{8,0},{10,2},{12,4},{14,6},{16,24},{18,... | collective-permute-start | bytes 61448 | tf_op jit(solution)/shard_map/ppermute | solution.py:456
  30.9 1.4 %collective-permute-start.10 = (f32[40,128]{1,0:T(8,128)S(1)}, f32[40,128]{1,0:T(8,128)S(1)}, u32[]{:S(2)}, u32[]{:S(2)}) collective-permute-start(f32[40,128]{1,0:T(8,128)S(1)} %add.20), channel_id=1, source_target_pairs={{0,12},{2,14},{4,8},{6,10},{8,4},{10,6},{12,0},{14,2},{16,28},{18,... | collective-permute-start | bytes 61448 | tf_op jit(solution)/shard_map/ppermute | solution.py:456
  32.3 0.1 collective-permute-start.8
  32.5 0.2 collective-permute-done.9
  32.7 2.9 %collective-permute-done.10 = f32[40,128]{1,0:T(8,128)S(1)} collective-permute-done((f32[40,128]{1,0:T(8,128)S(1)}, f32[40,128]{1,0:T(8,128)S(1)}, u32[]{:S(2)}, u32[]{:S(2)}) %collective-permute-start.10) | collective-permute-done | bytes 20512 | tf_op jit(solution)/shard_map/ppermute | solution.py:456
  35.6 0.5 %collective-permute-done.8 = f32[40,128]{1,0:T(8,128)S(1)} collective-permute-done((f32[40,128]{1,0:T(8,128)S(1)}, f32[40,128]{1,0:T(8,128)S(1)}, u32[]{:S(2)}, u32[]{:S(2)}) %collective-permute-start.8) | collective-permute-done | bytes 20512 | tf_op jit(solution)/shard_map/ppermute | solution.py:456
  36.1 2.6 %collective-permute-start.11 = (f32[40,128]{1,0:T(8,128)S(1)}, f32[40,128]{1,0:T(8,128)S(1)}, u32[]{:S(2)}, u32[]{:S(2)}) collective-permute-start(f32[40,128]{1,0:T(8,128)S(1)} %add_add_fusion.own_ref), channel_id=1, source_target_pairs={{0,16},{2,18},{4,20},{6,22},{8,24},{10,26},{12,28},{14,30},{16,0},... | collective-permute-start | bytes 61448 | tf_op jit(solution)/shard_map/ppermute | solution.py:461
  38.8 2.1 %collective-permute-done.11.got_ref = f32[40,128]{1,0:T(8,128)S(1)} collective-permute-done((f32[40,128]{1,0:T(8,128)S(1)}, f32[40,128]{1,0:T(8,128)S(1)}, u32[]{:S(2)}, u32[]{:S(2)}) %collective-permute-start.11) | collective-permute-done | bytes 20512 | tf_op jit(solution)/shard_map/ppermute | solution.py:461
  40.9 0.6 %shard_map.185 = (f32[32,36]{1,0:T(8,128)}, f32[1,32]{1,0:T(1,128)}, f32[2,128]{1,0:T(2,128)}) custom-call(f32[40,128]{1,0:T(8,128)S(1)} %add_add_fusion.own_ref, f32[40,128]{1,0:T(8,128)S(1)} %collective-permute-done.11.got_ref), custom_call_target="tpu_custom_call" | custom-call | tf_op jit(solution)/shard_map/pallas_call | solution.py:470
  (36 shorter events, 0.4 us)
Async XLA Ops:
  0.6 19.5 %copy-start = (bf16[32,36]{1,0:T(8,128)(2,1)S(1)}, bf16[32,36]{1,0:T(8,128)(2,1)}, u32[]{:S(2)}) copy-start(bf16[32,36]{1,0:T(8,128)(2,1)} %param.18) | copy-start | bytes 6916
  0.6 5.8 %copy-start.13 = (f32[256]{0:T(256)S(1)}, f32[256]{0:T(256)}, u32[]{:S(2)}) copy-start(f32[256]{0:T(256)} %param.20) | copy-start | bytes 3076
  0.7 8.5 %collective-permute-start = (s32[2,2,1,32]{3,2,1,0:T(1,128)}, s32[2,2,1,32]{3,2,1,0:T(1,128)S(1)}, u32[]{:S(2)}, u32[]{:S(2)}) collective-permute-start(s32[2,2,1,32]{3,2,1,0:T(1,128)} %param.17), channel_id=1, source_target_pairs={{0,1},{1,0},{2,3},{3,2},{4,5},{5,4},{6,7},{7,6},{8,9},{9,8},{10,11... | collective-permute-start | bytes 1544 | tf_op jit(solution)/shard_map/ppermute | solution.py:493
  3.7 5.5 %collective-permute-start.1 = (bf16[32,8,128]{2,1,0:T(8,128)(2,1)}, bf16[32,8,128]{2,1,0:T(8,128)(2,1)S(1)}, u32[]{:S(2)}, u32[]{:S(2)}) collective-permute-start(bf16[32,8,128]{2,1,0:T(8,128)(2,1)} %refs_0_.1), channel_id=1, source_target_pairs={{0,1},{1,0},{2,3},{3,2},{4,5},{5,4},{6,7},{7,6},{8,9},{9,8},{10,11... | collective-permute-start | bytes 196616 | tf_op jit(solution)/shard_map/ppermute | solution.py:493
  3.8 4.7 %collective-permute-start.2 = (bf16[2,16,512]{2,1,0:T(8,128)(2,1)}, bf16[2,16,512]{2,1,0:T(8,128)(2,1)S(1)}, u32[]{:S(2)}, u32[]{:S(2)}) collective-permute-start(bf16[2,16,512]{2,1,0:T(8,128)(2,1)} %param.16), channel_id=1, source_target_pairs={{0,1},{1,0},{2,3},{3,2},{4,5},{5,4},{6,7},{7,6},{8,9},{9,8},{10,11... | collective-permute-start | bytes 98312 | tf_op jit(solution)/shard_map/ppermute | solution.py:493
  6.4 3.4 %copy-start.3 = (bf16[32,8,128]{2,1,0:T(8,128)(2,1)S(1)}, bf16[32,8,128]{2,1,0:T(8,128)(2,1)}, u32[]{:S(2)}) copy-start(bf16[32,8,128]{2,1,0:T(8,128)(2,1)} %refs_0_.1) | copy-start | bytes 196612
  6.4 3.4 %copy-start.8 = (bf16[128,256]{1,0:T(8,128)(2,1)S(1)}, bf16[128,256]{1,0:T(8,128)(2,1)}, u32[]{:S(2)}) copy-start(bf16[128,256]{1,0:T(8,128)(2,1)} %constant.23.clone.refs_10_) | copy-start | bytes 196612
  8.5 1.3 %collective-permute-start.3 = (bf16[4,16,512]{2,1,0:T(8,128)(2,1)S(1)}, bf16[4,16,512]{2,1,0:T(8,128)(2,1)S(1)}, u32[]{:S(2)}, u32[]{:S(2)}) collective-permute-start(bf16[4,16,512]{2,1,0:T(8,128)(2,1)S(1)} %constant_dynamic-update-slice_fusion.refs_6_), channel_id=1, source_target_pairs={{0,2},{2,0},{4,6},{6,4},{8,10},{10,8},{12,14},{14,12},{16,18},{18,... | collective-permute-start | bytes 196616 | tf_op jit(solution)/shard_map/ppermute | solution.py:443
  8.5 1.3 %collective-permute-start.4 = (bf16[4,16,512]{2,1,0:T(8,128)(2,1)S(1)}, bf16[4,16,512]{2,1,0:T(8,128)(2,1)S(1)}, u32[]{:S(2)}, u32[]{:S(2)}) collective-permute-start(bf16[4,16,512]{2,1,0:T(8,128)(2,1)S(1)} %constant_dynamic-update-slice_fusion.refs_6_), channel_id=1, source_target_pairs={{2,4},{4,2},{6,8},{8,6},{10,12},{12,10},{14,16},{16,14},{18,20},{2... | collective-permute-start | bytes 196616 | tf_op jit(solution)/shard_map/ppermute | solution.py:443
  9.8 0.9 %copy-start.5 = (bf16[256,256]{1,0:T(8,128)(2,1)S(1)}, bf16[256,256]{1,0:T(8,128)(2,1)}, u32[]{:S(2)}) copy-start(bf16[256,256]{1,0:T(8,128)(2,1)} %constant.22.clone.refs_9_) | copy-start | bytes 393220
  10.7 0.9 %copy-start.6 = (bf16[256,256]{1,0:T(8,128)(2,1)S(1)}, bf16[256,256]{1,0:T(8,128)(2,1)}, u32[]{:S(2)}) copy-start(bf16[256,256]{1,0:T(8,128)(2,1)} %constant.24.clone.refs_11_) | copy-start | bytes 393220
  11.6 0.8 %copy-start.9 = (bf16[256,128]{1,0:T(8,128)(2,1)S(1)}, bf16[256,128]{1,0:T(8,128)(2,1)}, u32[]{:S(2)}) copy-start(bf16[256,128]{1,0:T(8,128)(2,1)} %constant.25.clone.refs_12_) | copy-start | bytes 196612
  12.4 7.7 %copy-start.11 = (bf16[960,36]{1,0:T(8,128)(2,1)S(1)}, bf16[960,36]{1,0:T(8,128)(2,1)}, u32[]{:S(2)}) copy-start(bf16[960,36]{1,0:T(8,128)(2,1)} %constant.30.clone) | copy-start | bytes 207364
  14.7 5.7 %copy-start.12 = (bf16[36,1440]{1,0:T(8,128)(2,1)S(1)}, bf16[36,1440]{1,0:T(8,128)(2,1)}, u32[]{:S(2)}) copy-start(bf16[36,1440]{1,0:T(8,128)(2,1)} %constant.29.clone) | copy-start | bytes 311044
  14.7 6.8 %collective-permute-start.5 = (bf16[80,128]{1,0:T(8,128)(2,1)S(1)}, bf16[80,128]{1,0:T(8,128)(2,1)S(1)}, u32[]{:S(2)}, u32[]{:S(2)}) collective-permute-start(bf16[80,128]{1,0:T(8,128)(2,1)S(1)} %get-tuple-element.19), channel_id=1, source_target_pairs={{0,2},{2,0},{4,6},{6,4},{8,10},{10,8},{12,14},{14,12},{16,18},{18,... | collective-permute-start | bytes 61448 | tf_op jit(solution)/shard_map/ppermute | solution.py:443
  19.5 2.0 %collective-permute-start.6 = (bf16[80,128]{1,0:T(8,128)(2,1)S(1)}, bf16[80,128]{1,0:T(8,128)(2,1)S(1)}, u32[]{:S(2)}, u32[]{:S(2)}) collective-permute-start(bf16[80,128]{1,0:T(8,128)(2,1)S(1)} %get-tuple-element.20), channel_id=1, source_target_pairs={{2,4},{4,2},{6,8},{8,6},{10,12},{12,10},{14,16},{16,14},{18,20},{2... | collective-permute-start | bytes 61448 | tf_op jit(solution)/shard_map/ppermute | solution.py:443
  21.0 0.9 %copy-start.4 = (bf16[256,256]{1,0:T(8,128)(2,1)S(1)}, bf16[256,256]{1,0:T(8,128)(2,1)}, u32[]{:S(2)}) copy-start(bf16[256,256]{1,0:T(8,128)(2,1)} %constant.26.clone.refs_2_) | copy-start | bytes 393220
  21.0 1.0 %copy-start.1 = (bf16[256,512]{1,0:T(8,128)(2,1)S(1)}, bf16[256,512]{1,0:T(8,128)(2,1)}, u32[]{:S(2)}) copy-start(bf16[256,512]{1,0:T(8,128)(2,1)} %constant.27.clone.refs_3_) | copy-start | bytes 786436
  21.1 1.0 %copy-start.2 = (bf16[256,512]{1,0:T(8,128)(2,1)S(1)}, bf16[256,512]{1,0:T(8,128)(2,1)}, u32[]{:S(2)}) copy-start(bf16[256,512]{1,0:T(8,128)(2,1)} %constant.28.clone.refs_4_) | copy-start | bytes 786436
  21.3 0.9 %copy-start.7 = (bf16[256,128]{1,0:T(8,128)(2,1)S(1)}, bf16[256,128]{1,0:T(8,128)(2,1)}, u32[]{:S(2)}) copy-start(bf16[256,128]{1,0:T(8,128)(2,1)} %constant.31.clone.refs_5_) | copy-start | bytes 196612
  21.5 0.7 %copy-start.10 = (f32[32]{0:T(128)S(1)}, f32[32]{0:T(128)}, u32[]{:S(2)}) copy-start(f32[32]{0:T(128)} %param.19) | copy-start | bytes 388
  23.4 4.8 %collective-permute-start.7 = (f32[40,128]{1,0:T(8,128)S(1)}, f32[40,128]{1,0:T(8,128)S(1)}, u32[]{:S(2)}, u32[]{:S(2)}) collective-permute-start(f32[40,128]{1,0:T(8,128)S(1)} %shard_map.184), channel_id=1, source_target_pairs={{0,2},{2,0},{4,6},{6,4},{8,10},{10,8},{12,14},{14,12},{16,18},{18,... | collective-permute-start | bytes 61448 | tf_op jit(solution)/shard_map/ppermute | solution.py:456
  28.3 4.4 %collective-permute-start.9 = (f32[40,128]{1,0:T(8,128)S(1)}, f32[40,128]{1,0:T(8,128)S(1)}, u32[]{:S(2)}, u32[]{:S(2)}) collective-permute-start(f32[40,128]{1,0:T(8,128)S(1)} %add.20), channel_id=1, source_target_pairs={{0,8},{2,10},{4,12},{6,14},{8,0},{10,2},{12,4},{14,6},{16,24},{18,... | collective-permute-start | bytes 61448 | tf_op jit(solution)/shard_map/ppermute | solution.py:456
  30.9 4.7 %collective-permute-start.10 = (f32[40,128]{1,0:T(8,128)S(1)}, f32[40,128]{1,0:T(8,128)S(1)}, u32[]{:S(2)}, u32[]{:S(2)}) collective-permute-start(f32[40,128]{1,0:T(8,128)S(1)} %add.20), channel_id=1, source_target_pairs={{0,12},{2,14},{4,8},{6,10},{8,4},{10,6},{12,0},{14,2},{16,28},{18,... | collective-permute-start | bytes 61448 | tf_op jit(solution)/shard_map/ppermute | solution.py:456
  32.3 3.8 %collective-permute-start.8 = (f32[40,128]{1,0:T(8,128)S(1)}, f32[40,128]{1,0:T(8,128)S(1)}, u32[]{:S(2)}, u32[]{:S(2)}) collective-permute-start(f32[40,128]{1,0:T(8,128)S(1)} %add.20), channel_id=1, source_target_pairs={{0,4},{2,6},{4,0},{6,2},{8,12},{10,14},{12,8},{14,10},{16,20},{18,... | collective-permute-start | bytes 61448 | tf_op jit(solution)/shard_map/ppermute | solution.py:456
  36.1 4.7 %collective-permute-start.11 = (f32[40,128]{1,0:T(8,128)S(1)}, f32[40,128]{1,0:T(8,128)S(1)}, u32[]{:S(2)}, u32[]{:S(2)}) collective-permute-start(f32[40,128]{1,0:T(8,128)S(1)} %add_add_fusion.own_ref), channel_id=1, source_target_pairs={{0,16},{2,18},{4,20},{6,22},{8,24},{10,26},{12,28},{14,30},{16,0},... | collective-permute-start | bytes 61448 | tf_op jit(solution)/shard_map/ppermute | solution.py:461
where the time goes:
time: 41.8 us; the launch traced here: 41.5 us
  starting transfers between devices  22 us (53%)
  waiting for transfers between devices  8.43 us (20%)
  local copies, waits for them, and re-layouts  5.05 us (12%)
  Pallas kernels  4.1 us (10%)
  between operations  0.85 us (2%)
  other arithmetic  0.7 us (2%)
    ppermute x4, starting transfers between devices, sum_space(): lax.ppermute(value, 'space', [(i, i ^ m) for i in range(count)])  8.16 us
    ppermute x4, starting transfers between devices, involution(): return lax.ppermute(value, 'space', pairs)  6.12 us
    ppermute x3, starting transfers between devices, from_frame(): return lax.ppermute(value, 'frame', [(i, (i - j) % nf) for i in range(nf)])  5.06 us
    ppermute x4, waiting for transfers between devices, sum_space(): lax.ppermute(value, 'space', [(i, i ^ m) for i in range(count)])  4.49 us
    unnamed x29, local copies, waits for them, and re-layouts  4.2 us
    pallas_call x3, Pallas kernels, call(): pl.pallas_call(body, out_shape=tuple(outs), in_specs=[sm] * smem + [vm] *...  4.1 us
    ppermute x1, starting transfers between devices, sum_space(): got = lax.ppermute(value, 'space', [(i, i ^ mask) for i in range(count)])  2.65 us
    ppermute x1, waiting for transfers between devices, sum_space(): got = lax.ppermute(value, 'space', [(i, i ^ mask) for i in range(count)])  2.09 us
  transfers between devices with their start and end apart: 12, of which 7 were waited for; matrix products, arithmetic and copies ran while one was open for 6% of the time, Pallas kernels for 0%

commit v1 on v0

--- a/solution.py
+++ b/solution.py
@@ -124,7 +124,15 @@
     goal_refs, refs = refs[:nf], refs[nf:]
     y_ref, yc_ref, yf_ref, fwd_ref, fwdl_ref, inv_ref, invl_ref, var_ref = refs[:8]
     merged_ref, pack_ref, pc_ref, pf_ref, h_ref = refs[8:13]
-    x_ref, idx_ref, p_ref, q_ref, xs_ref, mm_ref, goal_ref = refs[13:]
+    x_ref, idx_ref, p_ref, q_ref, xs_ref, mm_ref, goal_ref = refs[13:20]
+    held, sems = refs[20:24], refs[24]
+    loads = [
+        pltpu.make_async_copy(src, dst, sems.at[k])
+        for k, (src, dst) in enumerate(zip((fwd_ref, fwdl_ref, inv_ref, invl_ref), held))
+    ]
+    for copy in loads:
+        copy.start()
+    fwd_ref, fwdl_ref, inv_ref, invl_ref = held
     s = lax.axis_index("space")
     fr = lax.axis_index("frame")
     odd = lax.rem(s, 2)
@@ -234,6 +242,9 @@
         sums = add_lists(sums, part)
         base = [x_ref[first * G + g, TILE : 2 * TILE, :] for g in range(G)]
         both = jnp.concatenate(blocks + base, axis=0).astype(BF16)
+        if carry is None:
+            loads[0].wait()
+            loads[1].wait()
         pq = dot(jnp.concatenate([both, both], axis=1), fwd_ref[...]) + dot(both, fwdl_ref[...])
         for q in range(16):
             rows = slice(q * TILE, (q + 1) * TILE)
@@ -272,6 +283,8 @@
     )
     m = 16 * rows_out
     terms = split(uv, 3)
+    loads[2].wait()
+    loads[3].wait()
     wide = dot(jnp.concatenate(terms, axis=0), inv_ref[...])
     pix = wide[:m, :LANES] + (wide[m : 2 * m, :LANES] + wide[:m, LANES:])
     pix = pix + (wide[2 * m :, :LANES] + wide[m : 2 * m, LANES:] + dot(terms[0], invl_ref[...]))
@@ -299,7 +312,15 @@
     half = W // 2
     goal_refs = refs[:nf]
     part_ref, wideh_ref, widel_ref, pick_ref, big_ref, bigt_ref, offs_ref = refs[nf : nf + 7]
-    out_ref, goal_ref, raw_ref, mm_ref, p_ref, q_ref, ns_ref = refs[nf + 7 :]
+    out_ref, goal_ref, raw_ref, mm_ref, p_ref, q_ref, ns_ref = refs[nf + 7 : nf + 14]
+    held, sems = refs[nf + 14 : nf + 17], refs[nf + 17]
+    loads = [
+        pltpu.make_async_copy(src, dst, sems.at[k])
+        for k, (src, dst) in enumerate(zip((wideh_ref, widel_ref, pick_ref), held))
+    ]
+    for copy in loads:
+        copy.start()
+    wideh_ref, widel_ref, pick_ref = held
     s = lax.axis_index("space")
     fr = lax.axis_index("frame")
     odd = lax.rem(s, 2)
@@ -386,6 +407,8 @@
     )
     m = grad.shape[0]
     terms = split(grad, 2)
+    for copy in loads:
+        copy.wait()
     pq = dot(jnp.concatenate(terms, axis=0), wideh_ref[...])
     pq = pq[:m] + (pq[m:] + dot(terms[0], widel_ref[...]))
     for r in range(rows_out):
@@ -453,7 +476,9 @@
         stages.append([m << at for m in range(1, 1 << width)])
         at += width
     for masks in stages[:-1]:
-        got = [lax.ppermute(value, "space", [(i, i ^ m) for i in range(count)]) for m in masks]
+        got = []
+        for m in masks:
+            got.append(lax.ppermute(value, "space", [(i, i ^ m) for i in range(count)]))
         value = value + got[0]
         if len(got) == 3:
             value = value + (got[1] + got[2])
@@ -462,15 +487,21 @@
     return value, got
 
 
-def call(body, args, smem, outs, scratch):
+def call(body, args, smem, outs, scratch, far=()):
     vm = pl.BlockSpec(memory_space=pltpu.VMEM)
     sm = pl.BlockSpec(memory_space=pltpu.SMEM)
     sizes = [int(np.prod(a.shape)) * a.dtype.itemsize for a in list(args) + list(outs)]
     sizes += [int(np.prod(a.shape)) * 4 for a in scratch]
+    hbm = pl.BlockSpec(memory_space=pltpu.HBM)
+    specs = [sm if k < smem else hbm if k in far else vm for k in range(len(args))]
+    args = [
+        pltpu.with_memory_space_constraint(a, pltpu.HBM) if k in far else a
+        for k, a in enumerate(args)
+    ]
     return pl.pallas_call(
         body,
         out_shape=tuple(outs),
-        in_specs=[sm] * smem + [vm] * (len(args) - smem),
+        in_specs=specs,
         out_specs=(vm,) * len(outs),
         scratch_shapes=scratch,
         compiler_params=pltpu.CompilerParams(vmem_limit_bytes=sum(sizes) + (12 << 20)),
@@ -496,13 +527,16 @@
         return [value] + [from_frame(value, j) for j in range(1, nf)]
 
     raws = pieces(raw)
+    goals = pieces(goal)
     shift_parts = pieces(shifts)
-    shift_parts = [v + TILE for v in shift_parts]
-    y = jnp.concatenate(raws, axis=0)
+    y = jnp.pad(raw, ((0, F - fl), (0, 0), (0, 0)))
+    y = lax.optimization_barrier(y)
+    for j in range(1, nf):
+        y = lax.dynamic_update_slice(y, raws[j], (j * fl, 0, 0))
+    y, shifts, log_var = lax.optimization_barrier((y, shifts, log_var))
+    shift_parts = [v + TILE for v in [shifts] + shift_parts[1:]]
     yf = involution(y, n_space, 1, 1)
     yc = involution(y, n_space, 1, 0)
-    goals = pieces(goal)
-
     fwd, fwd_low, inv, inv_low, part, wide, wide_low = (jnp.asarray(t) for t in tables())
     place, place_t, pick = tap_tables()
     side = 4 * G + nf * nsc * channels
@@ -527,7 +561,10 @@
             pltpu.VMEM((16 * rows_out, LANES), F32),
             pltpu.VMEM((G, TILE, LANES), F32),
             pltpu.VMEM((nf * nsc, 256, LANES), F32),
+            *[pltpu.VMEM(t.shape, BF16) for t in (fwd, fwd_low, inv, inv_low)],
+            pltpu.SemaphoreType.DMA((4,)),
         ],
+        {3 * nf + 3, 3 * nf + 4, 3 * nf + 5, 3 * nf + 6},
     )
     pc, pf, weight = lax.optimization_barrier((pc, pf, weight))
     pf = involution(pf, n_space, 1, 1)
@@ -549,7 +586,10 @@
             pltpu.VMEM((rows_out * TILE, LANES), F32),
             pltpu.VMEM((rows_out * TILE, LANES), F32),
             pltpu.VMEM((rows_out * TILE, LANES), F32),
+            *[pltpu.VMEM(t.shape, BF16) for t in (wide, wide_low, pick)],
+            pltpu.SemaphoreType.DMA((3,)),
         ],
+        {5 + nf, 6 + nf, 7 + nf},
     )
     grad_weight, grad_bias, grad_noise = call(
         last_sum,

time: 41.8 us -> 40.4 us (0.967)
  local copies, waits for them, and re-layouts: 5.05 us -> 2.33 us
  Pallas kernels: 4.1 us -> 6.15 us
  other arithmetic: 0.7 us -> 0.02 us
    unnamed x29 -> x16, local copies, waits for them, and re-layouts: 4.2 us -> 0.72 us
    pallas_call x3, Pallas kernels: 4.1 us -> 6.15 us  [call(): pl.pallas_call(body, out_shape=tuple(outs), in_specs=specs, out_specs=(vm...]
    pad x0 -> x1, local copies, waits for them, and re-layouts: none -> 0.76 us  [shards(): y = jnp.pad(raw, ((0, F - fl), (0, 0), (0, 0)))]
    add x2, other arithmetic: 0.69 us -> 0.01 us  [shards(): shift_parts = [v + TILE for v in [shifts] + shift_parts[1:]]]
  transfers between devices with their start and end apart: 12 -> 12, of which waited for: 7 -> 7; matrix products, arithmetic and copies ran while one was open for 6% -> 5% of each run, Pallas kernels for 0% -> 0%
where the time goes in v1:
time: 40.4 us; the launch traced here: 40.1 us
  starting transfers between devices  22.1 us (55%)
  waiting for transfers between devices  8.3 us (21%)
  Pallas kernels  6.15 us (15%)
  local copies, waits for them, and re-layouts  2.33 us (6%)
  between operations  0.86 us (2%)
    ppermute x4, starting transfers between devices, sum_space(): got.append(lax.ppermute(value, 'space', [(i, i ^ m) for i in range(count)]))  8.23 us
    ppermute x4, starting transfers between devices, involution(): return lax.ppermute(value, 'space', pairs)  6.21 us
    pallas_call x3, Pallas kernels, call(): pl.pallas_call(body, out_shape=tuple(outs), in_specs=specs, out_specs=(vm...  6.15 us
    ppermute x3, starting transfers between devices, from_frame(): return lax.ppermute(value, 'frame', [(i, (i - j) % nf) for i in range(nf)])  5.06 us
    ppermute x4, waiting for transfers between devices, sum_space(): got.append(lax.ppermute(value, 'space', [(i, i ^ m) for i in range(count)]))  4.37 us
    ppermute x1, starting transfers between devices, sum_space(): got = lax.ppermute(value, 'space', [(i, i ^ mask) for i in range(count)])  2.65 us
    ppermute x1, waiting for transfers between devices, sum_space(): got = lax.ppermute(value, 'space', [(i, i ^ mask) for i in range(count)])  2.09 us
    ppermute x3, waiting for transfers between devices, from_frame(): return lax.ppermute(value, 'frame', [(i, (i - j) % nf) for i in range(nf)])  1.32 us
  transfers between devices with their start and end apart: 12, of which 7 were waited for; matrix products, arithmetic and copies ran while one was open for 5% of the time, Pallas kernels for 0%

profile of v1, /device:TPU:0, one launch (start us, length us, event | category | flops | bytes accessed | tf_op | source)
XLA Modules:
  0.0 40.1 jit_solution(1123807891031758331)
XLA Ops:
  0.6 0.0 copy-start
  0.7 3.0 %collective-permute-start.1 = (s32[2,2,1,32]{3,2,1,0:T(1,128)}, s32[2,2,1,32]{3,2,1,0:T(1,128)S(1)}, u32[]{:S(2)}, u32[]{:S(2)}) collective-permute-start(s32[2,2,1,32]{3,2,1,0:T(1,128)} %param.17), channel_id=1, source_target_pairs={{0,1},{1,0},{2,3},{3,2},{4,5},{5,4},{6,7},{7,6},{8,9},{9,8},{10,11... | collective-permute-start | bytes 1544 | tf_op jit(solution)/shard_map/ppermute | solution.py:524
  3.7 0.1 collective-permute-start
  3.8 1.9 %collective-permute-start.2 = (bf16[32,8,128]{2,1,0:T(8,128)(2,1)}, bf16[32,8,128]{2,1,0:T(8,128)(2,1)S(1)}, u32[]{:S(2)}, u32[]{:S(2)}) collective-permute-start(bf16[32,8,128]{2,1,0:T(8,128)(2,1)} %refs_0_.1), channel_id=1, source_target_pairs={{0,1},{1,0},{2,3},{3,2},{4,5},{5,4},{6,7},{7,6},{8,9},{9,8},{10,11... | collective-permute-start | bytes 196616 | tf_op jit(solution)/shard_map/ppermute | solution.py:524
  5.7 0.8 %pad.4 = bf16[4,16,512]{2,1,0:T(8,128)(2,1)S(1)} pad(bf16[2,16,512]{2,1,0:T(8,128)(2,1)} %param.16, bf16[]{:T(256)} %constant.11.clone.1), padding=0_2x0_0x0_0 | pad | bytes 98306 | tf_op jit(solution)/shard_map/jit(_pad)/pad | solution.py:532
  6.5 1.3 %collective-permute-done = bf16[2,16,512]{2,1,0:T(8,128)(2,1)S(1)} collective-permute-done((bf16[2,16,512]{2,1,0:T(8,128)(2,1)}, bf16[2,16,512]{2,1,0:T(8,128)(2,1)S(1)}, u32[]{:S(2)}, u32[]{:S(2)}) %collective-permute-start) | collective-permute-done | bytes 32800 | tf_op jit(solution)/shard_map/ppermute | solution.py:524
  7.8 0.7 %collective-permute-start.4 = (bf16[4,16,512]{2,1,0:T(8,128)(2,1)S(1)}, bf16[4,16,512]{2,1,0:T(8,128)(2,1)S(1)}, u32[]{:S(2)}, u32[]{:S(2)}) collective-permute-start(bf16[4,16,512]{2,1,0:T(8,128)(2,1)S(1)} %constant_dynamic-update-slice_fusion.refs_6_), channel_id=1, source_target_pairs={{2,4},{4,2},{6,8},{8,6},{10,12},{12,10},{14,16},{16,14},{18,20},{2... | collective-permute-start | bytes 196616 | tf_op jit(solution)/shard_map/ppermute | solution.py:466
  8.5 0.0 copy-start.4
  8.6 0.5 %collective-permute-done.3.refs_7_ = bf16[4,16,512]{2,1,0:T(8,128)(2,1)S(1)} collective-permute-done((bf16[4,16,512]{2,1,0:T(8,128)(2,1)S(1)}, bf16[4,16,512]{2,1,0:T(8,128)(2,1)S(1)}, u32[]{:S(2)}, u32[]{:S(2)}) %collective-permute-start.3) | collective-permute-done | bytes 65568 | tf_op jit(solution)/shard_map/ppermute | solution.py:466
  9.1 3.3 %shard_map.183 = (f32[16,256]{1,0:T(8,128)}, f32[4,16,128]{2,1,0:T(8,128)S(1)}, bf16[80,128]{1,0:T(8,128)(2,1)S(1)}, bf16[80,128]{1,0:T(8,128)(2,1)S(1)}, f32[256,128]{1,0:T(8,128)S(1)}) custom-call(s32[2,2,1,32]{3,2,1,0:T(1,128)S(1)} %broadcast_add_fusion.1.refs_0_.refs_2_, s32[2,2,1,32]{3,2,1,0:T(1,128)S(1)} %broadcast_add_fusion.refs_1_.refs_3_, ...), custom_call_target="tpu_custom_call" | custom-call | tf_op jit(solution)/shard_map/pallas_call | solution.py:501
  12.4 0.0 copy-start.5
  12.4 4.9 %collective-permute-start.5 = (bf16[80,128]{1,0:T(8,128)(2,1)S(1)}, bf16[80,128]{1,0:T(8,128)(2,1)S(1)}, u32[]{:S(2)}, u32[]{:S(2)}) collective-permute-start(bf16[80,128]{1,0:T(8,128)(2,1)S(1)} %get-tuple-element.25), channel_id=1, source_target_pairs={{0,2},{2,0},{4,6},{6,4},{8,10},{10,8},{12,14},{14,12},{16,18},{18,... | collective-permute-start | bytes 61448 | tf_op jit(solution)/shard_map/ppermute | solution.py:466
  17.3 0.7 %collective-permute-start.6 = (bf16[80,128]{1,0:T(8,128)(2,1)S(1)}, bf16[80,128]{1,0:T(8,128)(2,1)S(1)}, u32[]{:S(2)}, u32[]{:S(2)}) collective-permute-start(bf16[80,128]{1,0:T(8,128)(2,1)S(1)} %get-tuple-element.26), channel_id=1, source_target_pairs={{2,4},{4,2},{6,8},{8,6},{10,12},{12,10},{14,16},{16,14},{18,20},{2... | collective-permute-start | bytes 61448 | tf_op jit(solution)/shard_map/ppermute | solution.py:466
  18.0 0.2 fusion
  18.2 0.1 convolution_convert_fusion
  18.3 0.4 %convert_element_type.19 = bf16[32,10,144]{2,1,0:T(8,128)(2,1)S(1)} reshape(bf16[32,1440]{1,0:T(8,128)(2,1)S(1)} %convolution_convert_fusion) | data formatting | bytes 184320 | tf_op jit(solution)/shard_map/convert_element_type | solution.py:573
  18.7 0.1 copy.22
  18.8 0.2 copy.23
  19.0 0.2 convert_element_type.24.refs_7_
  19.2 0.7 %copy-done.2 = bf16[256,256]{1,0:T(8,128)(2,1)S(1)} copy-done((bf16[256,256]{1,0:T(8,128)(2,1)S(1)}, bf16[256,256]{1,0:T(8,128)(2,1)}, u32[]{:S(2)}) %copy-start.2) | copy-done | bytes 131096
  19.9 2.3 %shard_map.184 = f32[40,128]{1,0:T(8,128)S(1)} custom-call(f32[4,16,128]{2,1,0:T(8,128)S(1)} %get-tuple-element.22.pack_ref, bf16[80,128]{1,0:T(8,128)(2,1)S(1)} %collective-permute-done.5.pc_ref, bf16[80,128]{1,0:T(8,128)(2,1)S(1)} %collective-permute-done.6.pf_ref, f32[256,128]{1,0:T(8,128)S(1)} %get-tuple-element.27.h_ref, ...), custom_call_target="tpu_custom_call" | custom-call | tf_op jit(solution)/shard_map/pallas_call | solution.py:501
  22.2 4.0 %collective-permute-start.7 = (f32[40,128]{1,0:T(8,128)S(1)}, f32[40,128]{1,0:T(8,128)S(1)}, u32[]{:S(2)}, u32[]{:S(2)}) collective-permute-start(f32[40,128]{1,0:T(8,128)S(1)} %shard_map.184), channel_id=1, source_target_pairs={{0,2},{2,0},{4,6},{6,4},{8,10},{10,8},{12,14},{14,12},{16,18},{18,... | collective-permute-start | bytes 61448 | tf_op jit(solution)/shard_map/ppermute | solution.py:481
  26.2 0.8 %collective-permute-done.7 = f32[40,128]{1,0:T(8,128)S(1)} collective-permute-done((f32[40,128]{1,0:T(8,128)S(1)}, f32[40,128]{1,0:T(8,128)S(1)}, u32[]{:S(2)}, u32[]{:S(2)}) %collective-permute-start.7) | collective-permute-done | bytes 20512 | tf_op jit(solution)/shard_map/ppermute | solution.py:481
  27.0 2.7 %collective-permute-start.9 = (f32[40,128]{1,0:T(8,128)S(1)}, f32[40,128]{1,0:T(8,128)S(1)}, u32[]{:S(2)}, u32[]{:S(2)}) collective-permute-start(f32[40,128]{1,0:T(8,128)S(1)} %add.22), channel_id=1, source_target_pairs={{0,8},{2,10},{4,12},{6,14},{8,0},{10,2},{12,4},{14,6},{16,24},{18,... | collective-permute-start | bytes 61448 | tf_op jit(solution)/shard_map/ppermute | solution.py:481
  29.7 1.3 %collective-permute-start.10 = (f32[40,128]{1,0:T(8,128)S(1)}, f32[40,128]{1,0:T(8,128)S(1)}, u32[]{:S(2)}, u32[]{:S(2)}) collective-permute-start(f32[40,128]{1,0:T(8,128)S(1)} %add.22), channel_id=1, source_target_pairs={{0,12},{2,14},{4,8},{6,10},{8,4},{10,6},{12,0},{14,2},{16,28},{18,... | collective-permute-start | bytes 61448 | tf_op jit(solution)/shard_map/ppermute | solution.py:481
  31.0 0.3 collective-permute-start.8
  31.3 0.2 collective-permute-done.9
  31.5 2.9 %collective-permute-done.10 = f32[40,128]{1,0:T(8,128)S(1)} collective-permute-done((f32[40,128]{1,0:T(8,128)S(1)}, f32[40,128]{1,0:T(8,128)S(1)}, u32[]{:S(2)}, u32[]{:S(2)}) %collective-permute-start.10) | collective-permute-done | bytes 20512 | tf_op jit(solution)/shard_map/ppermute | solution.py:481
  34.4 0.4 collective-permute-done.8
  34.8 2.7 %collective-permute-start.11 = (f32[40,128]{1,0:T(8,128)S(1)}, f32[40,128]{1,0:T(8,128)S(1)}, u32[]{:S(2)}, u32[]{:S(2)}) collective-permute-start(f32[40,128]{1,0:T(8,128)S(1)} %add_add_fusion.own_ref), channel_id=1, source_target_pairs={{0,16},{2,18},{4,20},{6,22},{8,24},{10,26},{12,28},{14,30},{16,0},... | collective-permute-start | bytes 61448 | tf_op jit(solution)/shard_map/ppermute | solution.py:486
  37.4 2.1 %collective-permute-done.11.got_ref = f32[40,128]{1,0:T(8,128)S(1)} collective-permute-done((f32[40,128]{1,0:T(8,128)S(1)}, f32[40,128]{1,0:T(8,128)S(1)}, u32[]{:S(2)}, u32[]{:S(2)}) %collective-permute-start.11) | collective-permute-done | bytes 20512 | tf_op jit(solution)/shard_map/ppermute | solution.py:486
  39.5 0.6 %shard_map.185 = (f32[32,36]{1,0:T(8,128)}, f32[1,32]{1,0:T(1,128)}, f32[2,128]{1,0:T(2,128)}) custom-call(f32[40,128]{1,0:T(8,128)S(1)} %add_add_fusion.own_ref, f32[40,128]{1,0:T(8,128)S(1)} %collective-permute-done.11.got_ref), custom_call_target="tpu_custom_call" | custom-call | tf_op jit(solution)/shard_map/pallas_call | solution.py:501
  (24 shorter events, 0.1 us)
Async XLA Ops:
  0.6 17.3 %copy-start = (bf16[32,36]{1,0:T(8,128)(2,1)S(1)}, bf16[32,36]{1,0:T(8,128)(2,1)}, u32[]{:S(2)}) copy-start(bf16[32,36]{1,0:T(8,128)(2,1)} %param.18) | copy-start | bytes 6916
  0.6 8.4 %copy-start.1 = (bf16[32,8,128]{2,1,0:T(8,128)(2,1)S(1)}, bf16[32,8,128]{2,1,0:T(8,128)(2,1)}, u32[]{:S(2)}) copy-start(bf16[32,8,128]{2,1,0:T(8,128)(2,1)} %refs_0_.1) | copy-start | bytes 196612
  0.7 5.8 %collective-permute-start.1 = (s32[2,2,1,32]{3,2,1,0:T(1,128)}, s32[2,2,1,32]{3,2,1,0:T(1,128)S(1)}, u32[]{:S(2)}, u32[]{:S(2)}) collective-permute-start(s32[2,2,1,32]{3,2,1,0:T(1,128)} %param.17), channel_id=1, source_target_pairs={{0,1},{1,0},{2,3},{3,2},{4,5},{5,4},{6,7},{7,6},{8,9},{9,8},{10,11... | collective-permute-start | bytes 1544 | tf_op jit(solution)/shard_map/ppermute | solution.py:524
  3.7 4.1 %collective-permute-start = (bf16[2,16,512]{2,1,0:T(8,128)(2,1)}, bf16[2,16,512]{2,1,0:T(8,128)(2,1)S(1)}, u32[]{:S(2)}, u32[]{:S(2)}) collective-permute-start(bf16[2,16,512]{2,1,0:T(8,128)(2,1)} %param.16), channel_id=1, source_target_pairs={{0,1},{1,0},{2,3},{3,2},{4,5},{5,4},{6,7},{7,6},{8,9},{9,8},{10,11... | collective-permute-start | bytes 98312 | tf_op jit(solution)/shard_map/ppermute | solution.py:524
  3.8 4.8 %collective-permute-start.2 = (bf16[32,8,128]{2,1,0:T(8,128)(2,1)}, bf16[32,8,128]{2,1,0:T(8,128)(2,1)S(1)}, u32[]{:S(2)}, u32[]{:S(2)}) collective-permute-start(bf16[32,8,128]{2,1,0:T(8,128)(2,1)} %refs_0_.1), channel_id=1, source_target_pairs={{0,1},{1,0},{2,3},{3,2},{4,5},{5,4},{6,7},{7,6},{8,9},{9,8},{10,11... | collective-permute-start | bytes 196616 | tf_op jit(solution)/shard_map/ppermute | solution.py:524
  6.5 2.0 %copy-start.6 = (s32[2,2,1,32]{3,2,1,0:T(1,128)S(1)}, s32[2,2,1,32]{3,2,1,0:T(1,128)}, u32[]{:S(2)}) copy-start(s32[2,2,1,32]{3,2,1,0:T(1,128)} %param.17) | copy-start | bytes 1540
  7.8 0.7 %copy-start.7 = (f32[256]{0:T(256)S(1)}, f32[256]{0:T(256)}, u32[]{:S(2)}) copy-start(f32[256]{0:T(256)} %param.20) | copy-start | bytes 3076
  7.8 1.3 %collective-permute-start.3 = (bf16[4,16,512]{2,1,0:T(8,128)(2,1)S(1)}, bf16[4,16,512]{2,1,0:T(8,128)(2,1)S(1)}, u32[]{:S(2)}, u32[]{:S(2)}) collective-permute-start(bf16[4,16,512]{2,1,0:T(8,128)(2,1)S(1)} %constant_dynamic-update-slice_fusion.refs_6_), channel_id=1, source_target_pairs={{0,2},{2,0},{4,6},{6,4},{8,10},{10,8},{12,14},{14,12},{16,18},{18,... | collective-permute-start | bytes 196616 | tf_op jit(solution)/shard_map/ppermute | solution.py:466
  7.8 1.2 %collective-permute-start.4 = (bf16[4,16,512]{2,1,0:T(8,128)(2,1)S(1)}, bf16[4,16,512]{2,1,0:T(8,128)(2,1)S(1)}, u32[]{:S(2)}, u32[]{:S(2)}) collective-permute-start(bf16[4,16,512]{2,1,0:T(8,128)(2,1)S(1)} %constant_dynamic-update-slice_fusion.refs_6_), channel_id=1, source_target_pairs={{2,4},{4,2},{6,8},{8,6},{10,12},{12,10},{14,16},{16,14},{18,20},{2... | collective-permute-start | bytes 196616 | tf_op jit(solution)/shard_map/ppermute | solution.py:466
  8.5 9.4 %copy-start.4 = (bf16[960,36]{1,0:T(8,128)(2,1)S(1)}, bf16[960,36]{1,0:T(8,128)(2,1)}, u32[]{:S(2)}) copy-start(bf16[960,36]{1,0:T(8,128)(2,1)} %constant.36.clone) | copy-start | bytes 207364
  12.4 5.8 %copy-start.5 = (bf16[36,1440]{1,0:T(8,128)(2,1)S(1)}, bf16[36,1440]{1,0:T(8,128)(2,1)}, u32[]{:S(2)}) copy-start(bf16[36,1440]{1,0:T(8,128)(2,1)} %constant.35.clone) | copy-start | bytes 311044
  12.4 6.8 %collective-permute-start.5 = (bf16[80,128]{1,0:T(8,128)(2,1)S(1)}, bf16[80,128]{1,0:T(8,128)(2,1)S(1)}, u32[]{:S(2)}, u32[]{:S(2)}) collective-permute-start(bf16[80,128]{1,0:T(8,128)(2,1)S(1)} %get-tuple-element.25), channel_id=1, source_target_pairs={{0,2},{2,0},{4,6},{6,4},{8,10},{10,8},{12,14},{14,12},{16,18},{18,... | collective-permute-start | bytes 61448 | tf_op jit(solution)/shard_map/ppermute | solution.py:466
  17.3 1.9 %collective-permute-start.6 = (bf16[80,128]{1,0:T(8,128)(2,1)S(1)}, bf16[80,128]{1,0:T(8,128)(2,1)S(1)}, u32[]{:S(2)}, u32[]{:S(2)}) collective-permute-start(bf16[80,128]{1,0:T(8,128)(2,1)S(1)} %get-tuple-element.26), channel_id=1, source_target_pairs={{2,4},{4,2},{6,8},{8,6},{10,12},{12,10},{14,16},{16,14},{18,20},{2... | collective-permute-start | bytes 61448 | tf_op jit(solution)/shard_map/ppermute | solution.py:466
  19.0 0.9 %copy-start.2 = (bf16[256,256]{1,0:T(8,128)(2,1)S(1)}, bf16[256,256]{1,0:T(8,128)(2,1)}, u32[]{:S(2)}) copy-start(bf16[256,256]{1,0:T(8,128)(2,1)} %constant.32.clone.refs_2_) | copy-start | bytes 393220
  19.2 0.7 %copy-start.3 = (f32[32]{0:T(128)S(1)}, f32[32]{0:T(128)}, u32[]{:S(2)}) copy-start(f32[32]{0:T(128)} %param.19) | copy-start | bytes 388
  22.2 4.8 %collective-permute-start.7 = (f32[40,128]{1,0:T(8,128)S(1)}, f32[40,128]{1,0:T(8,128)S(1)}, u32[]{:S(2)}, u32[]{:S(2)}) collective-permute-start(f32[40,128]{1,0:T(8,128)S(1)} %shard_map.184), channel_id=1, source_target_pairs={{0,2},{2,0},{4,6},{6,4},{8,10},{10,8},{12,14},{14,12},{16,18},{18,... | collective-permute-start | bytes 61448 | tf_op jit(solution)/shard_map/ppermute | solution.py:481
  27.0 4.5 %collective-permute-start.9 = (f32[40,128]{1,0:T(8,128)S(1)}, f32[40,128]{1,0:T(8,128)S(1)}, u32[]{:S(2)}, u32[]{:S(2)}) collective-permute-start(f32[40,128]{1,0:T(8,128)S(1)} %add.22), channel_id=1, source_target_pairs={{0,8},{2,10},{4,12},{6,14},{8,0},{10,2},{12,4},{14,6},{16,24},{18,... | collective-permute-start | bytes 61448 | tf_op jit(solution)/shard_map/ppermute | solution.py:481
  29.7 4.7 %collective-permute-start.10 = (f32[40,128]{1,0:T(8,128)S(1)}, f32[40,128]{1,0:T(8,128)S(1)}, u32[]{:S(2)}, u32[]{:S(2)}) collective-permute-start(f32[40,128]{1,0:T(8,128)S(1)} %add.22), channel_id=1, source_target_pairs={{0,12},{2,14},{4,8},{6,10},{8,4},{10,6},{12,0},{14,2},{16,28},{18,... | collective-permute-start | bytes 61448 | tf_op jit(solution)/shard_map/ppermute | solution.py:481
  31.0 3.8 %collective-permute-start.8 = (f32[40,128]{1,0:T(8,128)S(1)}, f32[40,128]{1,0:T(8,128)S(1)}, u32[]{:S(2)}, u32[]{:S(2)}) collective-permute-start(f32[40,128]{1,0:T(8,128)S(1)} %add.22), channel_id=1, source_target_pairs={{0,4},{2,6},{4,0},{6,2},{8,12},{10,14},{12,8},{14,10},{16,20},{18,... | collective-permute-start | bytes 61448 | tf_op jit(solution)/shard_map/ppermute | solution.py:481
  34.8 4.7 %collective-permute-start.11 = (f32[40,128]{1,0:T(8,128)S(1)}, f32[40,128]{1,0:T(8,128)S(1)}, u32[]{:S(2)}, u32[]{:S(2)}) collective-permute-start(f32[40,128]{1,0:T(8,128)S(1)} %add_add_fusion.own_ref), channel_id=1, source_target_pairs={{0,16},{2,18},{4,20},{6,22},{8,24},{10,26},{12,28},{14,30},{16,0},... | collective-permute-start | bytes 61448 | tf_op jit(solution)/shard_map/ppermute | solution.py:486

commit v2 on v0

--- a/solution.py
+++ b/solution.py
@@ -32,47 +32,46 @@
 
 def split_table(value, parts):
     terms = []
-    value = value.astype(np.float64)
     for _ in range(parts):
-        term = value.astype(np.float32).astype(ml_dtypes.bfloat16)
+        term = float(np.float32(value).astype(ml_dtypes.bfloat16))
         terms.append(term)
-        value = value - term.astype(np.float64)
+        value = value - term
     return terms
 
 
-def tables():
-    angle = 2.0 * math.pi / TILE * (np.outer(np.arange(TILE), np.arange(TILE)) % TILE)
-    cos16, sin16 = np.cos(angle), np.sin(angle)
-    eye8, eye16 = np.eye(8), np.eye(16)
-    bc, bs = np.kron(eye8, cos16), np.kron(eye8, sin16)
-    fwd = split_table(np.concatenate([bc, bs], axis=1), 3)
-    fwd_main = np.concatenate(fwd[:2], axis=0)
-    inv = split_table(np.concatenate([bc, -bs], axis=0), 3)
-    inv_main = np.concatenate(inv[:2], axis=1)
-    part = np.zeros((256, 256))
-    for x in range(256):
-        part[x, (x % 2) * 128 + x // 2] = 1.0
-    wide = np.concatenate([np.kron(eye16, cos16), np.kron(eye16, sin16)], axis=1)
-    wide = split_table(part.T @ wide, 2)
-    return fwd_main, fwd[2], inv_main, inv[2], part.astype(ml_dtypes.bfloat16), wide[0], wide[1]
+def wave(phase, parts):
+    near = jnp.minimum(phase, 16 - phase)
+    step = jnp.minimum(near, 8 - near)
+    flip = near > 4
+    steps = [split_table(math.cos(2.0 * math.pi * k / 16.0), parts) for k in range(4)]
+    terms = []
+    for p in range(parts):
+        value = jnp.zeros(phase.shape, F32)
+        for k in range(4):
+            value = jnp.where(step == k, float(steps[k][p]), value)
+        terms.append(jnp.where(flip, -value, value))
+    return terms
+
+
+def waves(phase, parts):
+    phase = phase & 15
+    return wave(phase, parts), wave((phase + 12) & 15, parts)
 
 
 def tap_tables():
     place = np.zeros((36, 10, 144))
     back = np.zeros((96, 10, 36))
-    pick = np.zeros((256, 128))
     for a in range(3):
         for b in range(3):
             for p in range(2):
                 for q in range(2):
                     tap = (3 * a + b) * 4 + 2 * p + q
-                    pick[(q * 3 + b) * 24 + 2 * a + p, tap] = 1.0
                     for sy in range(10):
                         r = 2 * (sy + a) + p
                         place[tap, sy, (q * 3 + b) * 24 + r] = 1.0
                         if 4 <= r < 20:
                             back[(q * 3 + b) * 16 + r - 4, sy, tap] = 1.0
-    return place, back, pick.astype(ml_dtypes.bfloat16)
+    return place, back
 
 
 def turn(re, im, k, n):
@@ -122,9 +121,10 @@
     dy_refs, refs = refs[:nf], refs[nf:]
     dx_refs, refs = refs[:nf], refs[nf:]
     goal_refs, refs = refs[:nf], refs[nf:]
-    y_ref, yc_ref, yf_ref, fwd_ref, fwdl_ref, inv_ref, invl_ref, var_ref = refs[:8]
-    merged_ref, pack_ref, pc_ref, pf_ref, h_ref = refs[8:13]
-    x_ref, idx_ref, p_ref, q_ref, xs_ref, mm_ref, goal_ref = refs[13:]
+    y_ref, yc_ref, yf_ref, var_ref = refs[:4]
+    merged_ref, pack_ref, pc_ref, pf_ref, h_ref = refs[4:9]
+    x_ref, idx_ref, p_ref, q_ref, xs_ref, mm_ref, goal_ref = refs[9:16]
+    fwd_ref, fwdl_ref, inv_ref, invl_ref = refs[16:20]
     s = lax.axis_index("space")
     fr = lax.axis_index("frame")
     odd = lax.rem(s, 2)
@@ -164,6 +164,22 @@
 
     lane = lax.broadcasted_iota(jnp.int32, (TILE, LANES), 1)
     kind = (lane // TILE) % 4
+
+    line = lax.broadcasted_iota(jnp.int32, (TILE, LANES), 0)
+    cos, sin = waves(line * (lane & 15), 3)
+    for k in range(8):
+        at = slice(k * TILE, (k + 1) * TILE)
+        mid = slice(128 + k * TILE, 128 + (k + 1) * TILE)
+        here = (lane // TILE) == k
+        c = [jnp.where(here, v, 0.0).astype(BF16) for v in cos]
+        d = [jnp.where(here, v, 0.0).astype(BF16) for v in sin]
+        fwd_ref[at, :] = jnp.concatenate([c[0], d[0]], axis=1)
+        fwd_ref[mid, :] = jnp.concatenate([c[1], d[1]], axis=1)
+        fwdl_ref[at, :] = jnp.concatenate([c[2], d[2]], axis=1)
+        inv_ref[at, :] = jnp.concatenate([c[0], c[1]], axis=1)
+        inv_ref[mid, :] = jnp.concatenate([-d[0], -d[1]], axis=1)
+        invl_ref[at, :] = c[2]
+        invl_ref[mid, :] = -d[2]
     per = 16 // G
     chunks = F * G // 16
     rows_out = max(G, 8)
@@ -298,8 +314,9 @@
     W = G * LANES
     half = W // 2
     goal_refs = refs[:nf]
-    part_ref, wideh_ref, widel_ref, pick_ref, big_ref, bigt_ref, offs_ref = refs[nf : nf + 7]
-    out_ref, goal_ref, raw_ref, mm_ref, p_ref, q_ref, ns_ref = refs[nf + 7 :]
+    big_ref, bigt_ref, offs_ref = refs[nf : nf + 3]
+    out_ref, goal_ref, raw_ref, mm_ref, p_ref, q_ref, ns_ref = refs[nf + 3 : nf + 10]
+    part_ref, wideh_ref, widel_ref = refs[nf + 10 :]
     s = lax.axis_index("space")
     fr = lax.axis_index("frame")
     odd = lax.rem(s, 2)
@@ -320,6 +337,28 @@
                 val = ref[first : first + 32, :].astype(F32)
                 goal_ref[row, :, pl.ds(pl.multiple_of(at + c * LANES, LANES), LANES)] = val
 
+    line = lax.broadcasted_iota(jnp.int32, (256, 256), 0)
+    column = lax.broadcasted_iota(jnp.int32, (256, 256), 1)
+    source = 2 * (column & 127) + (column >> 7)
+    part_ref[...] = jnp.where(line == source, 1.0, 0.0).astype(BF16)
+    lane8 = lax.broadcasted_iota(jnp.int32, (8, LANES), 1)
+    line8 = lax.broadcasted_iota(jnp.int32, (8, LANES), 0)
+    empty = jnp.zeros((8, LANES), F32)
+    for q in range(2):
+        cos, sin = waves((2 * line8 + q) * (lane8 & 15), 2)
+        for t in range(0, 16, 2):
+            for ref, c, d in ((wideh_ref, cos[0], sin[0]), (widel_ref, cos[1], sin[1])):
+                rows = []
+                for u in (t, t + 1):
+                    here = lane8 // TILE == u % 8
+                    row = []
+                    for v in (c, d):
+                        v = jnp.where(here, v, 0.0)
+                        row += [v, empty] if u < 8 else [empty, v]
+                    rows.append(jnp.concatenate(row, axis=1))
+                at = q * 128 + t * 8
+                ref[at : at + 16, :] = jnp.concatenate(rows, axis=0).astype(BF16)
+
     near = pc_ref[0:lead, :].astype(F32)
     far = pf_ref[0:lead, :].astype(F32)
     low = jnp.where(odd == 1, near, far)
@@ -349,8 +388,7 @@
     diag = lax.broadcasted_iota(jnp.int32, (32, LANES), 0) == lax.broadcasted_iota(
         jnp.int32, (32, LANES), 1
     )
-    offs = jnp.concatenate([offs_ref[...], jnp.zeros((1, LANES - 32), F32)], axis=1)
-    offs = jnp.where(diag, jnp.broadcast_to(offs, (32, LANES)), 0.0)
+    offs = jnp.where(diag, jnp.broadcast_to(offs_ref[2:3, :], (32, LANES)), 0.0)
     offs = jnp.broadcast_to(jnp.sum(offs, axis=1, keepdims=True), (32, half))
     bias = jnp.zeros((32, half), F32)
     slopes = []
@@ -418,8 +456,14 @@
     gw = jnp.zeros((32, 256), F32)
     for sy in range(1, 9):
         gw = gw + pltpu.roll(prod[(sy - 1) * 32 : sy * 32], 256 - 2 * sy, 1)
-    picked = dot(jnp.concatenate(split(gw, 3), axis=0), pick_ref[...])
-    out_ref[0:32, :] = picked[0:32] + (picked[32:64] + picked[64:96])
+    tap = lax.broadcasted_iota(jnp.int32, (32, LANES), 1)
+    pair = tap >> 2
+    a = (pair * 11) >> 5
+    source = ((tap & 1) * 3 + pair - 3 * a) * 24 + 2 * a + ((tap >> 1) & 1)
+    source = jnp.where(tap < 36, source, 0)
+    lower_part = jnp.take_along_axis(gw[:, :LANES], source & 127, axis=1)
+    upper_part = jnp.take_along_axis(gw[:, LANES:], source & 127, axis=1)
+    out_ref[0:32, :] = jnp.where(source < LANES, lower_part, upper_part)
     bias = jnp.broadcast_to(jnp.sum(bias, axis=1, keepdims=True), (32, LANES))
     bias = jnp.sum(jnp.where(diag, bias, 0.0), axis=0, keepdims=True)
     row = lax.broadcasted_iota(jnp.int32, (8, LANES), 0)
@@ -453,7 +497,9 @@
         stages.append([m << at for m in range(1, 1 << width)])
         at += width
     for masks in stages[:-1]:
-        got = [lax.ppermute(value, "space", [(i, i ^ m) for i in range(count)]) for m in masks]
+        got = []
+        for m in masks:
+            got.append(lax.ppermute(value, "space", [(i, i ^ m) for i in range(count)]))
         value = value + got[0]
         if len(got) == 3:
             value = value + (got[1] + got[2])
@@ -496,21 +542,24 @@
         return [value] + [from_frame(value, j) for j in range(1, nf)]
 
     raws = pieces(raw)
+    goals = pieces(goal)
     shift_parts = pieces(shifts)
+    y = jnp.pad(raw, ((0, F - fl), (0, 0), (0, 0)))
+    y = lax.optimization_barrier(y)
+    for j in range(1, nf):
+        y = lax.dynamic_update_slice(y, raws[j], (j * fl, 0, 0))
     shift_parts = [v + TILE for v in shift_parts]
-    y = jnp.concatenate(raws, axis=0)
+    small = jnp.concatenate(
+        [jnp.exp(log_var), offset, jnp.zeros((6 * LANES - channels,), F32)]
+    ).reshape(8, LANES)
     yf = involution(y, n_space, 1, 1)
     yc = involution(y, n_space, 1, 0)
-    goals = pieces(goal)
-
-    fwd, fwd_low, inv, inv_low, part, wide, wide_low = (jnp.asarray(t) for t in tables())
-    place, place_t, pick = tap_tables()
+    place, place_t = tap_tables()
     side = 4 * G + nf * nsc * channels
     shape = jax.ShapeDtypeStruct
     merged, pack, pc, pf, moments = call(
         functools.partial(merge_kernel, (nf, fl, G, T, nsc)),
-        [*shift_parts, *shift_parts, *goals, y, yc, yf]
-        + [fwd, fwd_low, inv, inv_low, jnp.exp(log_var).reshape(2, LANES)],
+        [*shift_parts, *shift_parts, *goals, y, yc, yf, small],
         nf,
         [
             shape((TILE, W // nf), F32),
@@ -527,6 +576,10 @@
             pltpu.VMEM((16 * rows_out, LANES), F32),
             pltpu.VMEM((G, TILE, LANES), F32),
             pltpu.VMEM((nf * nsc, 256, LANES), F32),
+            pltpu.VMEM((256, 256), BF16),
+            pltpu.VMEM((128, 256), BF16),
+            pltpu.VMEM((256, 256), BF16),
+            pltpu.VMEM((256, 128), BF16),
         ],
     )
     pc, pf, weight = lax.optimization_barrier((pc, pf, weight))
@@ -538,8 +591,7 @@
     bigt = bigt.reshape(96, 320).astype(BF16)
     (partial,) = call(
         functools.partial(demosaic_kernel, (nf, fl, G, nsc, n_space, inv_pixels)),
-        [pack, pc, pf, moments, *goals, part, wide, wide_low, jnp.asarray(pick), big, bigt]
-        + [offset.reshape(1, channels)],
+        [pack, pc, pf, moments, *goals, big, bigt, small],
         0,
         [shape((40, LANES), F32)],
         [
@@ -549,6 +601,9 @@
             pltpu.VMEM((rows_out * TILE, LANES), F32),
             pltpu.VMEM((rows_out * TILE, LANES), F32),
             pltpu.VMEM((rows_out * TILE, LANES), F32),
+            pltpu.VMEM((256, 256), BF16),
+            pltpu.VMEM((256, 512), BF16),
+            pltpu.VMEM((256, 512), BF16),
         ],
     )
     grad_weight, grad_bias, grad_noise = call(

time: 41.8 us -> 38.4 us (0.919)
  local copies, waits for them, and re-layouts: 5.05 us -> 2.35 us
  waiting for transfers between devices: 8.43 us -> 7.7 us
    unnamed x29 -> x12, local copies, waits for them, and re-layouts: 4.2 us -> 0.66 us
    pad x0 -> x1, local copies, waits for them, and re-layouts: none -> 0.81 us  [shards(): y = jnp.pad(raw, ((0, F - fl), (0, 0), (0, 0)))]
    ppermute x3, waiting for transfers between devices: 1.29 us -> 0.56 us  [from_frame(): return lax.ppermute(value, 'frame', [(i, (i - j) % nf) for i in range(nf)])]
  transfers between devices with their start and end apart: 12 -> 12, of which waited for: 7 -> 7; matrix products, arithmetic and copies ran while one was open for 6% -> 7% of each run, Pallas kernels for 0% -> 0%
where the time goes in v2:
time: 38.4 us; the launch traced here: 38.2 us
  starting transfers between devices  22.1 us (58%)
  waiting for transfers between devices  7.7 us (20%)
  Pallas kernels  4.13 us (11%)
  local copies, waits for them, and re-layouts  2.35 us (6%)
  between operations  0.8 us (2%)
  other arithmetic  0.77 us (2%)
    ppermute x4, starting transfers between devices, sum_space(): got.append(lax.ppermute(value, 'space', [(i, i ^ m) for i in range(count)]))  8.23 us
    ppermute x4, starting transfers between devices, involution(): return lax.ppermute(value, 'space', pairs)  6.13 us
    ppermute x3, starting transfers between devices, from_frame(): return lax.ppermute(value, 'frame', [(i, (i - j) % nf) for i in range(nf)])  5.06 us
    ppermute x4, waiting for transfers between devices, sum_space(): got.append(lax.ppermute(value, 'space', [(i, i ^ m) for i in range(count)]))  4.48 us
    pallas_call x3, Pallas kernels, call(): pl.pallas_call(body, out_shape=tuple(outs), in_specs=[sm] * smem + [vm] *...  4.13 us
    ppermute x1, starting transfers between devices, sum_space(): got = lax.ppermute(value, 'space', [(i, i ^ mask) for i in range(count)])  2.66 us
    ppermute x1, waiting for transfers between devices, sum_space(): got = lax.ppermute(value, 'space', [(i, i ^ mask) for i in range(count)])  2.08 us
    pad x1, local copies, waits for them, and re-layouts, shards(): y = jnp.pad(raw, ((0, F - fl), (0, 0), (0, 0)))  0.81 us
  transfers between devices with their start and end apart: 12, of which 7 were waited for; matrix products, arithmetic and copies ran while one was open for 7% of the time, Pallas kernels for 0%

profile of v2, /device:TPU:0, one launch (start us, length us, event | category | flops | bytes accessed | tf_op | source)
XLA Modules:
  0.0 38.2 jit_solution(3250454495798205754)
XLA Ops:
  0.6 0.0 copy-start
  0.7 3.0 %collective-permute-start = (s32[2,2,1,32]{3,2,1,0:T(1,128)}, s32[2,2,1,32]{3,2,1,0:T(1,128)S(1)}, u32[]{:S(2)}, u32[]{:S(2)}) collective-permute-start(s32[2,2,1,32]{3,2,1,0:T(1,128)} %param.9), channel_id=1, source_target_pairs={{0,1},{1,0},{2,3},{3,2},{4,5},{5,4},{6,7},{7,6},{8,9},{9,8},{10,11... | collective-permute-start | bytes 1544 | tf_op jit(solution)/shard_map/ppermute | solution.py:539
  3.7 0.1 collective-permute-start.1
  3.8 1.9 %collective-permute-start.2 = (bf16[2,16,512]{2,1,0:T(8,128)(2,1)}, bf16[2,16,512]{2,1,0:T(8,128)(2,1)S(1)}, u32[]{:S(2)}, u32[]{:S(2)}) collective-permute-start(bf16[2,16,512]{2,1,0:T(8,128)(2,1)} %param.8), channel_id=1, source_target_pairs={{0,1},{1,0},{2,3},{3,2},{4,5},{5,4},{6,7},{7,6},{8,9},{9,8},{10,11... | collective-permute-start | bytes 98312 | tf_op jit(solution)/shard_map/ppermute | solution.py:539
  5.7 0.7 %broadcast_add_fusion.1.refs_0_.refs_2_ = s32[2,2,1,32]{3,2,1,0:T(1,128)S(1)} fusion(s32[2,2,1,32]{3,2,1,0:T(1,128)} %param.9), kind=kLoop, calls=%fused_computation.6 | loop fusion | flops 128 | bytes 1024 | tf_op jit(solution)/shard_map/add | solution.py:551
  6.4 0.6 %copy-done.5 = f32[32]{0:T(128)S(1)} copy-done((f32[32]{0:T(128)S(1)}, f32[32]{0:T(128)}, u32[]{:S(2)}) %copy-start.5) | copy-done | bytes 152
  7.1 0.1 maximum_bitcast_fusion.refs_9_.refs_4_
  7.1 0.8 %pad.4 = bf16[4,16,512]{2,1,0:T(8,128)(2,1)S(1)} pad(bf16[2,16,512]{2,1,0:T(8,128)(2,1)} %param.8, bf16[]{:T(256)} %constant.4.clone.1), padding=0_2x0_0x0_0 | pad | bytes 98306 | tf_op jit(solution)/shard_map/jit(_pad)/pad | solution.py:547
  8.0 0.6 %collective-permute-done.2 = bf16[2,16,512]{2,1,0:T(8,128)(2,1)S(1)} collective-permute-done((bf16[2,16,512]{2,1,0:T(8,128)(2,1)}, bf16[2,16,512]{2,1,0:T(8,128)(2,1)S(1)}, u32[]{:S(2)}, u32[]{:S(2)}) %collective-permute-start.2) | collective-permute-done | bytes 32800 | tf_op jit(solution)/shard_map/ppermute | solution.py:539
  8.5 0.7 %collective-permute-start.4 = (bf16[4,16,512]{2,1,0:T(8,128)(2,1)S(1)}, bf16[4,16,512]{2,1,0:T(8,128)(2,1)S(1)}, u32[]{:S(2)}, u32[]{:S(2)}) collective-permute-start(bf16[4,16,512]{2,1,0:T(8,128)(2,1)S(1)} %constant_dynamic-update-slice_fusion.refs_6_), channel_id=1, source_target_pairs={{2,4},{4,2},{6,8},{8,6},{10,12},{12,10},{14,16},{16,14},{18,20},{2... | collective-permute-start | bytes 196616 | tf_op jit(solution)/shard_map/ppermute | solution.py:487
  9.2 0.6 %collective-permute-done.3.refs_7_ = bf16[4,16,512]{2,1,0:T(8,128)(2,1)S(1)} collective-permute-done((bf16[4,16,512]{2,1,0:T(8,128)(2,1)S(1)}, bf16[4,16,512]{2,1,0:T(8,128)(2,1)S(1)}, u32[]{:S(2)}, u32[]{:S(2)}) %collective-permute-start.3) | collective-permute-done | bytes 65568 | tf_op jit(solution)/shard_map/ppermute | solution.py:487
  9.8 2.3 %shard_map.111 = (f32[16,256]{1,0:T(8,128)}, f32[4,16,128]{2,1,0:T(8,128)S(1)}, bf16[80,128]{1,0:T(8,128)(2,1)S(1)}, bf16[80,128]{1,0:T(8,128)(2,1)S(1)}, f32[256,128]{1,0:T(8,128)S(1)}) custom-call(s32[2,2,1,32]{3,2,1,0:T(1,128)S(1)} %broadcast_add_fusion.1.refs_0_.refs_2_, s32[2,2,1,32]{3,2,1,0:T(1,128)S(1)} %broadcast_add_fusion.refs_1_.refs_3_, ...), custom_call_target="tpu_custom_call" | custom-call | tf_op jit(solution)/shard_map/pallas_call | solution.py:516
  12.0 4.8 %collective-permute-start.5 = (bf16[80,128]{1,0:T(8,128)(2,1)S(1)}, bf16[80,128]{1,0:T(8,128)(2,1)S(1)}, u32[]{:S(2)}, u32[]{:S(2)}) collective-permute-start(bf16[80,128]{1,0:T(8,128)(2,1)S(1)} %get-tuple-element.19), channel_id=1, source_target_pairs={{0,2},{2,0},{4,6},{6,4},{8,10},{10,8},{12,14},{14,12},{16,18},{18,... | collective-permute-start | bytes 61448 | tf_op jit(solution)/shard_map/ppermute | solution.py:487
  16.9 0.7 %collective-permute-start.6 = (bf16[80,128]{1,0:T(8,128)(2,1)S(1)}, bf16[80,128]{1,0:T(8,128)(2,1)S(1)}, u32[]{:S(2)}, u32[]{:S(2)}) collective-permute-start(bf16[80,128]{1,0:T(8,128)(2,1)S(1)} %get-tuple-element.20), channel_id=1, source_target_pairs={{2,4},{4,2},{6,8},{8,6},{10,12},{12,10},{14,16},{16,14},{18,20},{2... | collective-permute-start | bytes 61448 | tf_op jit(solution)/shard_map/ppermute | solution.py:487
  17.5 0.2 fusion
  17.8 0.1 convolution_convert_fusion
  17.9 0.4 %convert_element_type.19 = bf16[32,10,144]{2,1,0:T(8,128)(2,1)S(1)} reshape(bf16[32,1440]{1,0:T(8,128)(2,1)S(1)} %convolution_convert_fusion) | data formatting | bytes 184320 | tf_op jit(solution)/shard_map/convert_element_type | solution.py:589
  18.3 0.1 copy.14
  18.4 0.2 copy.15
  18.6 0.2 convert_element_type.24.refs_3_
  18.8 1.3 %shard_map.112 = f32[40,128]{1,0:T(8,128)S(1)} custom-call(f32[4,16,128]{2,1,0:T(8,128)S(1)} %get-tuple-element.16.pack_ref, bf16[80,128]{1,0:T(8,128)(2,1)S(1)} %collective-permute-done.5.pc_ref, bf16[80,128]{1,0:T(8,128)(2,1)S(1)} %collective-permute-done.6.pf_ref, f32[256,128]{1,0:T(8,128)S(1)} %get-tuple-element.21.h_ref, ...), custom_call_target="tpu_custom_call" | custom-call | tf_op jit(solution)/shard_map/pallas_call | solution.py:516
  20.1 4.0 %collective-permute-start.7 = (f32[40,128]{1,0:T(8,128)S(1)}, f32[40,128]{1,0:T(8,128)S(1)}, u32[]{:S(2)}, u32[]{:S(2)}) collective-permute-start(f32[40,128]{1,0:T(8,128)S(1)} %shard_map.112), channel_id=1, source_target_pairs={{0,2},{2,0},{4,6},{6,4},{8,10},{10,8},{12,14},{14,12},{16,18},{18,... | collective-permute-start | bytes 61448 | tf_op jit(solution)/shard_map/ppermute | solution.py:502
  24.1 0.8 %collective-permute-done.7 = f32[40,128]{1,0:T(8,128)S(1)} collective-permute-done((f32[40,128]{1,0:T(8,128)S(1)}, f32[40,128]{1,0:T(8,128)S(1)}, u32[]{:S(2)}, u32[]{:S(2)}) %collective-permute-start.7) | collective-permute-done | bytes 20512 | tf_op jit(solution)/shard_map/ppermute | solution.py:502
  24.9 2.7 %collective-permute-start.9 = (f32[40,128]{1,0:T(8,128)S(1)}, f32[40,128]{1,0:T(8,128)S(1)}, u32[]{:S(2)}, u32[]{:S(2)}) collective-permute-start(f32[40,128]{1,0:T(8,128)S(1)} %add.22), channel_id=1, source_target_pairs={{0,8},{2,10},{4,12},{6,14},{8,0},{10,2},{12,4},{14,6},{16,24},{18,... | collective-permute-start | bytes 61448 | tf_op jit(solution)/shard_map/ppermute | solution.py:502
  27.6 1.4 %collective-permute-start.10 = (f32[40,128]{1,0:T(8,128)S(1)}, f32[40,128]{1,0:T(8,128)S(1)}, u32[]{:S(2)}, u32[]{:S(2)}) collective-permute-start(f32[40,128]{1,0:T(8,128)S(1)} %add.22), channel_id=1, source_target_pairs={{0,12},{2,14},{4,8},{6,10},{8,4},{10,6},{12,0},{14,2},{16,28},{18,... | collective-permute-start | bytes 61448 | tf_op jit(solution)/shard_map/ppermute | solution.py:502
  29.0 0.1 collective-permute-start.8
  29.2 0.2 collective-permute-done.9
  29.4 2.9 %collective-permute-done.10 = f32[40,128]{1,0:T(8,128)S(1)} collective-permute-done((f32[40,128]{1,0:T(8,128)S(1)}, f32[40,128]{1,0:T(8,128)S(1)}, u32[]{:S(2)}, u32[]{:S(2)}) %collective-permute-start.10) | collective-permute-done | bytes 20512 | tf_op jit(solution)/shard_map/ppermute | solution.py:502
  32.3 0.5 %collective-permute-done.8 = f32[40,128]{1,0:T(8,128)S(1)} collective-permute-done((f32[40,128]{1,0:T(8,128)S(1)}, f32[40,128]{1,0:T(8,128)S(1)}, u32[]{:S(2)}, u32[]{:S(2)}) %collective-permute-start.8) | collective-permute-done | bytes 20512 | tf_op jit(solution)/shard_map/ppermute | solution.py:502
  32.8 2.7 %collective-permute-start.11 = (f32[40,128]{1,0:T(8,128)S(1)}, f32[40,128]{1,0:T(8,128)S(1)}, u32[]{:S(2)}, u32[]{:S(2)}) collective-permute-start(f32[40,128]{1,0:T(8,128)S(1)} %add_add_fusion.own_ref), channel_id=1, source_target_pairs={{0,16},{2,18},{4,20},{6,22},{8,24},{10,26},{12,28},{14,30},{16,0},... | collective-permute-start | bytes 61448 | tf_op jit(solution)/shard_map/ppermute | solution.py:507
  35.5 2.1 %collective-permute-done.11.got_ref = f32[40,128]{1,0:T(8,128)S(1)} collective-permute-done((f32[40,128]{1,0:T(8,128)S(1)}, f32[40,128]{1,0:T(8,128)S(1)}, u32[]{:S(2)}, u32[]{:S(2)}) %collective-permute-start.11) | collective-permute-done | bytes 20512 | tf_op jit(solution)/shard_map/ppermute | solution.py:507
  37.6 0.6 %shard_map.113 = (f32[32,36]{1,0:T(8,128)}, f32[1,32]{1,0:T(1,128)}, f32[2,128]{1,0:T(2,128)}) custom-call(f32[40,128]{1,0:T(8,128)S(1)} %add_add_fusion.own_ref, f32[40,128]{1,0:T(8,128)S(1)} %collective-permute-done.11.got_ref), custom_call_target="tpu_custom_call" | custom-call | tf_op jit(solution)/shard_map/pallas_call | solution.py:516
  (22 shorter events, 0.1 us)
Async XLA Ops:
  0.6 16.9 %copy-start = (bf16[32,36]{1,0:T(8,128)(2,1)S(1)}, bf16[32,36]{1,0:T(8,128)(2,1)}, u32[]{:S(2)}) copy-start(bf16[32,36]{1,0:T(8,128)(2,1)} %param.10) | copy-start | bytes 6916
  0.6 5.8 %copy-start.4 = (f32[256]{0:T(256)S(1)}, f32[256]{0:T(256)}, u32[]{:S(2)}) copy-start(f32[256]{0:T(256)} %param.12) | copy-start | bytes 3076
  0.7 8.5 %collective-permute-start = (s32[2,2,1,32]{3,2,1,0:T(1,128)}, s32[2,2,1,32]{3,2,1,0:T(1,128)S(1)}, u32[]{:S(2)}, u32[]{:S(2)}) collective-permute-start(s32[2,2,1,32]{3,2,1,0:T(1,128)} %param.9), channel_id=1, source_target_pairs={{0,1},{1,0},{2,3},{3,2},{4,5},{5,4},{6,7},{7,6},{8,9},{9,8},{10,11... | collective-permute-start | bytes 1544 | tf_op jit(solution)/shard_map/ppermute | solution.py:539
  3.7 5.5 %collective-permute-start.1 = (bf16[32,8,128]{2,1,0:T(8,128)(2,1)}, bf16[32,8,128]{2,1,0:T(8,128)(2,1)S(1)}, u32[]{:S(2)}, u32[]{:S(2)}) collective-permute-start(bf16[32,8,128]{2,1,0:T(8,128)(2,1)} %refs_0_.1), channel_id=1, source_target_pairs={{0,1},{1,0},{2,3},{3,2},{4,5},{5,4},{6,7},{7,6},{8,9},{9,8},{10,11... | collective-permute-start | bytes 196616 | tf_op jit(solution)/shard_map/ppermute | solution.py:539
  3.8 4.7 %collective-permute-start.2 = (bf16[2,16,512]{2,1,0:T(8,128)(2,1)}, bf16[2,16,512]{2,1,0:T(8,128)(2,1)S(1)}, u32[]{:S(2)}, u32[]{:S(2)}) collective-permute-start(bf16[2,16,512]{2,1,0:T(8,128)(2,1)} %param.8), channel_id=1, source_target_pairs={{0,1},{1,0},{2,3},{3,2},{4,5},{5,4},{6,7},{7,6},{8,9},{9,8},{10,11... | collective-permute-start | bytes 98312 | tf_op jit(solution)/shard_map/ppermute | solution.py:539
  6.4 0.7 %copy-start.5 = (f32[32]{0:T(128)S(1)}, f32[32]{0:T(128)}, u32[]{:S(2)}) copy-start(f32[32]{0:T(128)} %param.11) | copy-start | bytes 388
  7.1 2.6 %copy-start.1 = (bf16[32,8,128]{2,1,0:T(8,128)(2,1)S(1)}, bf16[32,8,128]{2,1,0:T(8,128)(2,1)}, u32[]{:S(2)}) copy-start(bf16[32,8,128]{2,1,0:T(8,128)(2,1)} %refs_0_.1) | copy-start | bytes 196612
  7.1 10.4 %copy-start.2 = (bf16[960,36]{1,0:T(8,128)(2,1)S(1)}, bf16[960,36]{1,0:T(8,128)(2,1)}, u32[]{:S(2)}) copy-start(bf16[960,36]{1,0:T(8,128)(2,1)} %constant.15.clone) | copy-start | bytes 207364
  8.5 1.3 %collective-permute-start.3 = (bf16[4,16,512]{2,1,0:T(8,128)(2,1)S(1)}, bf16[4,16,512]{2,1,0:T(8,128)(2,1)S(1)}, u32[]{:S(2)}, u32[]{:S(2)}) collective-permute-start(bf16[4,16,512]{2,1,0:T(8,128)(2,1)S(1)} %constant_dynamic-update-slice_fusion.refs_6_), channel_id=1, source_target_pairs={{0,2},{2,0},{4,6},{6,4},{8,10},{10,8},{12,14},{14,12},{16,18},{18,... | collective-permute-start | bytes 196616 | tf_op jit(solution)/shard_map/ppermute | solution.py:487
  8.5 1.3 %collective-permute-start.4 = (bf16[4,16,512]{2,1,0:T(8,128)(2,1)S(1)}, bf16[4,16,512]{2,1,0:T(8,128)(2,1)S(1)}, u32[]{:S(2)}, u32[]{:S(2)}) collective-permute-start(bf16[4,16,512]{2,1,0:T(8,128)(2,1)S(1)} %constant_dynamic-update-slice_fusion.refs_6_), channel_id=1, source_target_pairs={{2,4},{4,2},{6,8},{8,6},{10,12},{12,10},{14,16},{16,14},{18,20},{2... | collective-permute-start | bytes 196616 | tf_op jit(solution)/shard_map/ppermute | solution.py:487
  12.0 5.7 %copy-start.3 = (bf16[36,1440]{1,0:T(8,128)(2,1)S(1)}, bf16[36,1440]{1,0:T(8,128)(2,1)}, u32[]{:S(2)}) copy-start(bf16[36,1440]{1,0:T(8,128)(2,1)} %constant.14.clone) | copy-start | bytes 311044
  12.0 6.8 %collective-permute-start.5 = (bf16[80,128]{1,0:T(8,128)(2,1)S(1)}, bf16[80,128]{1,0:T(8,128)(2,1)S(1)}, u32[]{:S(2)}, u32[]{:S(2)}) collective-permute-start(bf16[80,128]{1,0:T(8,128)(2,1)S(1)} %get-tuple-element.19), channel_id=1, source_target_pairs={{0,2},{2,0},{4,6},{6,4},{8,10},{10,8},{12,14},{14,12},{16,18},{18,... | collective-permute-start | bytes 61448 | tf_op jit(solution)/shard_map/ppermute | solution.py:487
  16.9 2.0 %collective-permute-start.6 = (bf16[80,128]{1,0:T(8,128)(2,1)S(1)}, bf16[80,128]{1,0:T(8,128)(2,1)S(1)}, u32[]{:S(2)}, u32[]{:S(2)}) collective-permute-start(bf16[80,128]{1,0:T(8,128)(2,1)S(1)} %get-tuple-element.20), channel_id=1, source_target_pairs={{2,4},{4,2},{6,8},{8,6},{10,12},{12,10},{14,16},{16,14},{18,20},{2... | collective-permute-start | bytes 61448 | tf_op jit(solution)/shard_map/ppermute | solution.py:487
  20.1 4.8 %collective-permute-start.7 = (f32[40,128]{1,0:T(8,128)S(1)}, f32[40,128]{1,0:T(8,128)S(1)}, u32[]{:S(2)}, u32[]{:S(2)}) collective-permute-start(f32[40,128]{1,0:T(8,128)S(1)} %shard_map.112), channel_id=1, source_target_pairs={{0,2},{2,0},{4,6},{6,4},{8,10},{10,8},{12,14},{14,12},{16,18},{18,... | collective-permute-start | bytes 61448 | tf_op jit(solution)/shard_map/ppermute | solution.py:502
  24.9 4.5 %collective-permute-start.9 = (f32[40,128]{1,0:T(8,128)S(1)}, f32[40,128]{1,0:T(8,128)S(1)}, u32[]{:S(2)}, u32[]{:S(2)}) collective-permute-start(f32[40,128]{1,0:T(8,128)S(1)} %add.22), channel_id=1, source_target_pairs={{0,8},{2,10},{4,12},{6,14},{8,0},{10,2},{12,4},{14,6},{16,24},{18,... | collective-permute-start | bytes 61448 | tf_op jit(solution)/shard_map/ppermute | solution.py:502
  27.6 4.7 %collective-permute-start.10 = (f32[40,128]{1,0:T(8,128)S(1)}, f32[40,128]{1,0:T(8,128)S(1)}, u32[]{:S(2)}, u32[]{:S(2)}) collective-permute-start(f32[40,128]{1,0:T(8,128)S(1)} %add.22), channel_id=1, source_target_pairs={{0,12},{2,14},{4,8},{6,10},{8,4},{10,6},{12,0},{14,2},{16,28},{18,... | collective-permute-start | bytes 61448 | tf_op jit(solution)/shard_map/ppermute | solution.py:502
  29.0 3.8 %collective-permute-start.8 = (f32[40,128]{1,0:T(8,128)S(1)}, f32[40,128]{1,0:T(8,128)S(1)}, u32[]{:S(2)}, u32[]{:S(2)}) collective-permute-start(f32[40,128]{1,0:T(8,128)S(1)} %add.22), channel_id=1, source_target_pairs={{0,4},{2,6},{4,0},{6,2},{8,12},{10,14},{12,8},{14,10},{16,20},{18,... | collective-permute-start | bytes 61448 | tf_op jit(solution)/shard_map/ppermute | solution.py:502
  32.8 4.7 %collective-permute-start.11 = (f32[40,128]{1,0:T(8,128)S(1)}, f32[40,128]{1,0:T(8,128)S(1)}, u32[]{:S(2)}, u32[]{:S(2)}) collective-permute-start(f32[40,128]{1,0:T(8,128)S(1)} %add_add_fusion.own_ref), channel_id=1, source_target_pairs={{0,16},{2,18},{4,20},{6,22},{8,24},{10,26},{12,28},{14,30},{16,0},... | collective-permute-start | bytes 61448 | tf_op jit(solution)/shard_map/ppermute | solution.py:507

commit v3 on v2

--- a/solution.py
+++ b/solution.py
@@ -118,13 +118,19 @@
 def merge_kernel(dims, *refs):
     nf, fl, G, T, nsc = dims
     F = nf * fl
-    dy_refs, refs = refs[:nf], refs[nf:]
     dx_refs, refs = refs[:nf], refs[nf:]
     goal_refs, refs = refs[:nf], refs[nf:]
     y_ref, yc_ref, yf_ref, var_ref = refs[:4]
-    merged_ref, pack_ref, pc_ref, pf_ref, h_ref = refs[4:9]
-    x_ref, idx_ref, p_ref, q_ref, xs_ref, mm_ref, goal_ref = refs[9:16]
-    fwd_ref, fwdl_ref, inv_ref, invl_ref = refs[16:20]
+    pack_ref, pc_ref, pf_ref, h_ref = refs[4:8]
+    x_ref, idx_ref, p_ref, q_ref, xs_ref, goal_ref = refs[8:14]
+    fwd_ref, fwdl_ref, inv_ref, invl_ref = refs[14:18]
+    dy_refs, sems = refs[18 : 18 + nf], refs[18 + nf]
+    moves = [
+        pltpu.make_async_copy(src, dst, sems.at[j])
+        for j, (src, dst) in enumerate(zip(dx_refs, dy_refs))
+    ]
+    for move in moves:
+        move.start()
     s = lax.axis_index("space")
     fr = lax.axis_index("frame")
     odd = lax.rem(s, 2)
@@ -275,6 +281,8 @@
         flat = out[0] + out[1] + out[2] + out[3]
         return sums, add_lists(carry[1] if carry is not None else None, flat)
 
+    for move in moves:
+        move.wait()
     carry = chunk_step(0, None)
     if chunks > 1:
         carry = lax.fori_loop(1, chunks, chunk_step, carry)
@@ -297,13 +305,9 @@
         for other in range(g + G, rows_out, G):
             val = val + xs_ref[pl.ds(other, 16, stride=rows_out), :]
         val = (sums[g] + val / 256.0) / F
-        mm_ref[g] = val
         pack_ref[g] = val
-    own = G // nf
-    for k in range(own):
-        merged_ref[:, k * LANES : (k + 1) * LANES] = mm_ref[fr * own + k]
-    low = jnp.concatenate([mm_ref[g, 0:4, :] for g in range(G)], axis=0)
-    high = jnp.concatenate([mm_ref[g, 12:16, :] for g in range(G)], axis=0)
+    low = jnp.concatenate([pack_ref[g, 0:4, :] for g in range(G)], axis=0)
+    high = jnp.concatenate([pack_ref[g, 12:16, :] for g in range(G)], axis=0)
     pc_ref[0:lead, :] = jnp.where(odd == 1, low, high).astype(BF16)
     pf_ref[0:lead, :] = jnp.where(odd == 1, high, low).astype(BF16)
 
@@ -446,11 +450,6 @@
     noise = noise * (-1.0 / (256.0 * F))
     for step in (64, 32, 16):
         noise = noise + pltpu.roll(noise, step, 1)
-    lane_tile = lax.broadcasted_iota(jnp.int32, (TILE, LANES), 1) // TILE
-    spot = lax.broadcasted_iota(jnp.int32, (TILE, LANES), 0) % 8
-    noise = jnp.where(lane_tile == spot, noise, 0.0)
-    upper = jnp.sum(noise[:8], axis=0, keepdims=True)
-    lower = jnp.sum(noise[8:], axis=0, keepdims=True)
 
     prod = dot(slope_bf[32:288], taps, ((1,), (1,)))
     gw = jnp.zeros((32, 256), F32)
@@ -463,19 +462,37 @@
     source = jnp.where(tap < 36, source, 0)
     lower_part = jnp.take_along_axis(gw[:, :LANES], source & 127, axis=1)
     upper_part = jnp.take_along_axis(gw[:, LANES:], source & 127, axis=1)
-    out_ref[0:32, :] = jnp.where(source < LANES, lower_part, upper_part)
-    bias = jnp.broadcast_to(jnp.sum(bias, axis=1, keepdims=True), (32, LANES))
-    bias = jnp.sum(jnp.where(diag, bias, 0.0), axis=0, keepdims=True)
-    row = lax.broadcasted_iota(jnp.int32, (8, LANES), 0)
-    tail = jnp.where(row == 0, bias, jnp.where(row == 1, upper, jnp.where(row == 2, lower, 0.0)))
-    out_ref[32:40, :] = tail
-
-
-def last_sum(own_ref, got_ref, weight_ref, bias_ref, noise_ref):
+    gw = jnp.where(source < LANES, lower_part, upper_part)
+    gw = jnp.where(tap == 36, jnp.sum(bias, axis=1, keepdims=True), gw)
+    gw = jnp.where(tap < 37, gw, 0.0)
+    first = gw[0:8] + (pltpu.roll(gw[8:16], 37, 1) + pltpu.roll(gw[16:24], 74, 1))
+    group = lane8 // TILE
+    second = jnp.where(group == 5, noise[:8], jnp.where(group == 6, noise[8:], gw[24:32]))
+    out_ref[...] = jnp.concatenate([first, second], axis=0)
+
+
+def last_sum(nf, pack_ref, own_ref, got_ref, merged_ref, weight_ref, bias_ref, noise_ref):
+    own = pack_ref.shape[0] // nf
+    fr = lax.axis_index("frame")
+    for k in range(own):
+        merged_ref[:, k * LANES : (k + 1) * LANES] = pack_ref[fr * own + k]
     total = own_ref[...] + got_ref[...]
-    weight_ref[...] = total[:32, :36]
-    bias_ref[...] = total[32:33, :32]
-    noise_ref[...] = total[33:35]
+    first, second = total[:8], total[8:]
+    gw = jnp.concatenate(
+        [first, pltpu.roll(first, LANES - 37, 1), pltpu.roll(first, LANES - 74, 1), second], axis=0
+    )
+    weight_ref[...] = gw[:, :36]
+    line = lax.broadcasted_iota(jnp.int32, (32, LANES), 0)
+    lane = lax.broadcasted_iota(jnp.int32, (32, LANES), 1)
+    bias = jnp.where(line == lane, jnp.broadcast_to(gw[:, 36:37], (32, LANES)), 0.0)
+    bias_ref[...] = jnp.sum(bias, axis=0, keepdims=True)[:, :32]
+    group = lane[:8] // TILE
+    for k in range(2):
+        part = jnp.where(group == 5 + k, second, 0.0)
+        for step in (16, 32, 64):
+            part = part + pltpu.roll(part, step, 1)
+        part = jnp.where(group == line[:8], part, 0.0)
+        noise_ref[k : k + 1, :] = jnp.sum(part, axis=0, keepdims=True)
 
 
 def involution(value, count, step, first):
@@ -508,15 +525,14 @@
     return value, got
 
 
-def call(body, args, smem, outs, scratch):
+def call(body, args, outs, scratch):
     vm = pl.BlockSpec(memory_space=pltpu.VMEM)
-    sm = pl.BlockSpec(memory_space=pltpu.SMEM)
     sizes = [int(np.prod(a.shape)) * a.dtype.itemsize for a in list(args) + list(outs)]
-    sizes += [int(np.prod(a.shape)) * 4 for a in scratch]
+    sizes += [int(np.prod(a.shape)) * 4 for a in scratch if a.memory_space == pltpu.VMEM]
     return pl.pallas_call(
         body,
         out_shape=tuple(outs),
-        in_specs=[sm] * smem + [vm] * (len(args) - smem),
+        in_specs=[vm] * len(args),
         out_specs=(vm,) * len(outs),
         scratch_shapes=scratch,
         compiler_params=pltpu.CompilerParams(vmem_limit_bytes=sum(sizes) + (12 << 20)),
@@ -555,14 +571,16 @@
     yf = involution(y, n_space, 1, 1)
     yc = involution(y, n_space, 1, 0)
     place, place_t = tap_tables()
+    big = dot(weight, jnp.asarray(place.reshape(36, -1), BF16))
+    big = big.reshape(channels, 10, 144).transpose(1, 0, 2).reshape(320, 144).astype(BF16)
+    bigt = dot(jnp.asarray(place_t.reshape(-1, 36), BF16), weight.T)
+    bigt = bigt.reshape(96, 320).astype(BF16)
     side = 4 * G + nf * nsc * channels
     shape = jax.ShapeDtypeStruct
-    merged, pack, pc, pf, moments = call(
+    pack, pc, pf, moments = call(
         functools.partial(merge_kernel, (nf, fl, G, T, nsc)),
-        [*shift_parts, *shift_parts, *goals, y, yc, yf, small],
-        nf,
+        [*shift_parts, *goals, y, yc, yf, small],
         [
-            shape((TILE, W // nf), F32),
             shape((G, TILE, LANES), F32),
             shape((side, LANES), BF16),
             shape((side, LANES), BF16),
@@ -574,26 +592,21 @@
             pltpu.VMEM((256, LANES), F32),
             pltpu.VMEM((256, LANES), F32),
             pltpu.VMEM((16 * rows_out, LANES), F32),
-            pltpu.VMEM((G, TILE, LANES), F32),
             pltpu.VMEM((nf * nsc, 256, LANES), F32),
             pltpu.VMEM((256, 256), BF16),
             pltpu.VMEM((128, 256), BF16),
             pltpu.VMEM((256, 256), BF16),
             pltpu.VMEM((256, 128), BF16),
+            *[pltpu.SMEM(shifts.shape, jnp.int32)] * nf,
+            pltpu.SemaphoreType.DMA((nf,)),
         ],
     )
-    pc, pf, weight = lax.optimization_barrier((pc, pf, weight))
     pf = involution(pf, n_space, 1, 1)
     pc = involution(pc, n_space, 1, 0)
-    big = dot(weight, jnp.asarray(place.reshape(36, -1), BF16))
-    big = big.reshape(channels, 10, 144).transpose(1, 0, 2).reshape(320, 144).astype(BF16)
-    bigt = dot(jnp.asarray(place_t.reshape(-1, 36), BF16), weight.T)
-    bigt = bigt.reshape(96, 320).astype(BF16)
     (partial,) = call(
         functools.partial(demosaic_kernel, (nf, fl, G, nsc, n_space, inv_pixels)),
         [pack, pc, pf, moments, *goals, big, bigt, small],
-        0,
-        [shape((40, LANES), F32)],
+        [shape((16, LANES), F32)],
         [
             pltpu.VMEM((10, channels, W // 2), F32),
             pltpu.VMEM((256, LANES), F32),
@@ -606,11 +619,15 @@
             pltpu.VMEM((256, 512), BF16),
         ],
     )
-    grad_weight, grad_bias, grad_noise = call(
-        last_sum,
-        sum_space(partial, n_space),
-        0,
-        [shape((channels, 36), F32), shape((1, channels), F32), shape((2, LANES), F32)],
+    merged, grad_weight, grad_bias, grad_noise = call(
+        functools.partial(last_sum, nf),
+        [pack, *sum_space(partial, n_space)],
+        [
+            shape((TILE, W // nf), F32),
+            shape((channels, 36), F32),
+            shape((1, channels), F32),
+            shape((2, LANES), F32),
+        ],
         [],
     )
     return merged, grad_weight, grad_bias.reshape(channels), grad_noise.reshape(256)

time: 38.4 us -> 37.7 us (0.982)
  matrix products: 0.35 us -> 1.3 us
  local copies, waits for them, and re-layouts: 2.35 us -> 1.56 us
  waiting for transfers between devices: 7.7 us -> 6.97 us
  Pallas kernels: 4.13 us -> 3.7 us
    dot_general x2, matrix products: 0.35 us -> 1.3 us  [dot(): return lax.dot_general(a, b, (dims, ((), ())), preferred_element_type=F32)]
    pad x1, local copies, waits for them, and re-layouts: 0.81 us -> 0.01 us  [shards(): y = jnp.pad(raw, ((0, F - fl), (0, 0), (0, 0)))]
    ppermute x3, waiting for transfers between devices: 0.56 us -> 0.01 us  [from_frame(): return lax.ppermute(value, 'frame', [(i, (i - j) % nf) for i in range(nf)])]
    pallas_call x3, Pallas kernels: 4.13 us -> 3.7 us  [call(): pl.pallas_call(body, out_shape=tuple(outs), in_specs=[vm] * len(args), ou...]
  transfers between devices with their start and end apart: 12 -> 12, of which waited for: 7 -> 6; matrix products, arithmetic and copies ran while one was open for 7% -> 8% of each run, Pallas kernels for 0% -> 0%
where the time goes in v3:
time: 37.7 us; the launch traced here: 37.5 us
  starting transfers between devices  22.3 us (59%)
  waiting for transfers between devices  6.97 us (18%)
  Pallas kernels  3.7 us (10%)
  local copies, waits for them, and re-layouts  1.56 us (4%)
  matrix products  1.3 us (3%)
  between operations  0.83 us (2%)
  other arithmetic  0.8 us (2%)
    ppermute x4, starting transfers between devices, sum_space(): got.append(lax.ppermute(value, 'space', [(i, i ^ m) for i in range(count)]))  8.41 us
    ppermute x4, starting transfers between devices, involution(): return lax.ppermute(value, 'space', pairs)  6.27 us
    ppermute x3, starting transfers between devices, from_frame(): return lax.ppermute(value, 'frame', [(i, (i - j) % nf) for i in range(nf)])  5.06 us
    ppermute x4, waiting for transfers between devices, sum_space(): got.append(lax.ppermute(value, 'space', [(i, i ^ m) for i in range(count)]))  4.48 us
    pallas_call x3, Pallas kernels, call(): pl.pallas_call(body, out_shape=tuple(outs), in_specs=[vm] * len(args), ou...  3.7 us
    ppermute x1, starting transfers between devices, sum_space(): got = lax.ppermute(value, 'space', [(i, i ^ mask) for i in range(count)])  2.59 us
    ppermute x1, waiting for transfers between devices, sum_space(): got = lax.ppermute(value, 'space', [(i, i ^ mask) for i in range(count)])  1.96 us
    dot_general x2, matrix products, dot(): return lax.dot_general(a, b, (dims, ((), ())), preferred_element_type=F32)  1.3 us
  transfers between devices with their start and end apart: 12, of which 6 were waited for; matrix products, arithmetic and copies ran while one was open for 8% of the time, Pallas kernels for 0%

profile of v3, /device:TPU:0, one launch (start us, length us, event | category | flops | bytes accessed | tf_op | source)
XLA Modules:
  0.0 37.5 jit_solution(1233068412586308955)
XLA Ops:
  0.6 0.0 copy-start
  0.7 3.0 %collective-permute-start.2 = (bf16[2,16,512]{2,1,0:T(8,128)(2,1)}, bf16[2,16,512]{2,1,0:T(8,128)(2,1)S(1)}, u32[]{:S(2)}, u32[]{:S(2)}) collective-permute-start(bf16[2,16,512]{2,1,0:T(8,128)(2,1)} %param.8), channel_id=1, source_target_pairs={{0,1},{1,0},{2,3},{3,2},{4,5},{5,4},{6,7},{7,6},{8,9},{9,8},{10,11... | collective-permute-start | bytes 98312 | tf_op jit(solution)/shard_map/ppermute | solution.py:555
  3.7 0.1 collective-permute-start.1
  3.8 1.9 %collective-permute-start = (s32[2,2,1,32]{3,2,1,0:T(1,128)}, s32[2,2,1,32]{3,2,1,0:T(1,128)S(1)}, u32[]{:S(2)}, u32[]{:S(2)}) collective-permute-start(s32[2,2,1,32]{3,2,1,0:T(1,128)} %param.9), channel_id=1, source_target_pairs={{0,1},{1,0},{2,3},{3,2},{4,5},{5,4},{6,7},{7,6},{8,9},{9,8},{10,11... | collective-permute-start | bytes 1544 | tf_op jit(solution)/shard_map/ppermute | solution.py:555
  5.7 0.7 %broadcast_add_fusion.1.refs_0_ = s32[2,2,1,32]{3,2,1,0:T(1,128)S(1)} fusion(s32[2,2,1,32]{3,2,1,0:T(1,128)} %param.9), kind=kLoop, calls=%fused_computation.6 | loop fusion | flops 128 | bytes 1024 | tf_op jit(solution)/shard_map/add | solution.py:567
  6.5 1.2 %convolution_convert_fusion.1 = bf16[960,32]{0,1:T(8,128)(2,1)S(1)} fusion(bf16[960,36]{1,0:T(8,128)(2,1)} %constant.15.clone, bf16[32,36]{1,0:T(8,128)(2,1)S(1)} %copy-done), kind=kOutput, calls=%fused_computation.2 | convolution fusion | flops 2242560 | bytes 132864 | tf_op jit(solution)/shard_map/dot_general | solution.py:21
  7.6 0.0 copy-start.5
  7.6 0.6 %copy-done.5 = f32[32]{0:T(128)S(1)} copy-done((f32[32]{0:T(128)S(1)}, f32[32]{0:T(128)}, u32[]{:S(2)}) %copy-start.5) | copy-done | bytes 152
  8.3 0.1 maximum_bitcast_fusion.refs_7_.refs_4_
  8.4 0.1 collective-permute-start.3
  8.5 0.7 %collective-permute-start.4 = (bf16[4,16,512]{2,1,0:T(8,128)(2,1)S(1)}, bf16[4,16,512]{2,1,0:T(8,128)(2,1)S(1)}, u32[]{:S(2)}, u32[]{:S(2)}) collective-permute-start(bf16[4,16,512]{2,1,0:T(8,128)(2,1)S(1)} %constant_dynamic-update-slice_fusion.refs_4_), channel_id=1, source_target_pairs={{2,4},{4,2},{6,8},{8,6},{10,12},{12,10},{14,16},{16,14},{18,20},{2... | collective-permute-start | bytes 196616 | tf_op jit(solution)/shard_map/ppermute | solution.py:504
  9.2 0.0 copy-start.2
  9.2 0.5 %collective-permute-done.3.refs_5_ = bf16[4,16,512]{2,1,0:T(8,128)(2,1)S(1)} collective-permute-done((bf16[4,16,512]{2,1,0:T(8,128)(2,1)S(1)}, bf16[4,16,512]{2,1,0:T(8,128)(2,1)S(1)}, u32[]{:S(2)}, u32[]{:S(2)}) %collective-permute-start.3) | collective-permute-done | bytes 65568 | tf_op jit(solution)/shard_map/ppermute | solution.py:504
  9.7 1.6 %shard_map.111 = (f32[4,16,128]{2,1,0:T(8,128)S(1)}, bf16[80,128]{1,0:T(8,128)(2,1)S(1)}, bf16[80,128]{1,0:T(8,128)(2,1)S(1)}, f32[256,128]{1,0:T(8,128)S(1)}) custom-call(s32[2,2,1,32]{3,2,1,0:T(1,128)S(1)} %broadcast_add_fusion.1.refs_0_, s32[2,2,1,32]{3,2,1,0:T(1,128)S(1)} %broadcast_add_fusion.refs_1_, bf16[32,8,128]{2,1,0:T(8,128)(2,1)S(1)} %copy-done.1, ...), custom_call_target="tpu_custom_call" | custom-call | tf_op jit(solution)/shard_map/pallas_call | solution.py:532
  11.4 4.9 %collective-permute-start.5 = (bf16[80,128]{1,0:T(8,128)(2,1)S(1)}, bf16[80,128]{1,0:T(8,128)(2,1)S(1)}, u32[]{:S(2)}, u32[]{:S(2)}) collective-permute-start(bf16[80,128]{1,0:T(8,128)(2,1)S(1)} %get-tuple-element.13), channel_id=1, source_target_pairs={{0,2},{2,0},{4,6},{6,4},{8,10},{10,8},{12,14},{14,12},{16,18},{18,... | collective-permute-start | bytes 61448 | tf_op jit(solution)/shard_map/ppermute | solution.py:504
  16.3 0.7 %collective-permute-start.6 = (bf16[80,128]{1,0:T(8,128)(2,1)S(1)}, bf16[80,128]{1,0:T(8,128)(2,1)S(1)}, u32[]{:S(2)}, u32[]{:S(2)}) collective-permute-start(bf16[80,128]{1,0:T(8,128)(2,1)S(1)} %get-tuple-element.14), channel_id=1, source_target_pairs={{2,4},{4,2},{6,8},{8,6},{10,12},{12,10},{14,16},{16,14},{18,20},{2... | collective-permute-start | bytes 61448 | tf_op jit(solution)/shard_map/ppermute | solution.py:504
  16.9 0.1 fusion
  17.1 0.4 %convert_element_type.17 = bf16[32,10,144]{2,1,0:T(8,128)(2,1)S(1)} reshape(bf16[32,1440]{1,0:T(8,128)(2,1)S(1)} %fusion) | data formatting | bytes 184320 | tf_op jit(solution)/shard_map/convert_element_type | solution.py:575
  17.5 0.1 copy.14
  17.6 0.2 copy.15
  17.8 0.2 convert_element_type.21.refs_3_
  18.0 1.3 %shard_map.112 = f32[16,128]{1,0:T(8,128)S(1)} custom-call(f32[4,16,128]{2,1,0:T(8,128)S(1)} %get-tuple-element.12.pack_ref, bf16[80,128]{1,0:T(8,128)(2,1)S(1)} %collective-permute-done.5.pc_ref, bf16[80,128]{1,0:T(8,128)(2,1)S(1)} %collective-permute-done.6.pf_ref, f32[256,128]{1,0:T(8,128)S(1)} %get-tuple-element.15.h_ref, ...), custom_call_target="tpu_custom_call" | custom-call | tf_op jit(solution)/shard_map/pallas_call | solution.py:532
  19.3 4.2 %collective-permute-start.7 = (f32[16,128]{1,0:T(8,128)S(1)}, f32[16,128]{1,0:T(8,128)S(1)}, u32[]{:S(2)}, u32[]{:S(2)}) collective-permute-start(f32[16,128]{1,0:T(8,128)S(1)} %shard_map.112), channel_id=1, source_target_pairs={{0,2},{2,0},{4,6},{6,4},{8,10},{10,8},{12,14},{14,12},{16,18},{18,... | collective-permute-start | bytes 24584 | tf_op jit(solution)/shard_map/ppermute | solution.py:519
  23.5 0.8 %collective-permute-done.7 = f32[16,128]{1,0:T(8,128)S(1)} collective-permute-done((f32[16,128]{1,0:T(8,128)S(1)}, f32[16,128]{1,0:T(8,128)S(1)}, u32[]{:S(2)}, u32[]{:S(2)}) %collective-permute-start.7) | collective-permute-done | bytes 8224 | tf_op jit(solution)/shard_map/ppermute | solution.py:519
  24.3 3.6 %collective-permute-start.10 = (f32[16,128]{1,0:T(8,128)S(1)}, f32[16,128]{1,0:T(8,128)S(1)}, u32[]{:S(2)}, u32[]{:S(2)}) collective-permute-start(f32[16,128]{1,0:T(8,128)S(1)} %add.22), channel_id=1, source_target_pairs={{0,12},{2,14},{4,8},{6,10},{8,4},{10,6},{12,0},{14,2},{16,28},{18,... | collective-permute-start | bytes 24584 | tf_op jit(solution)/shard_map/ppermute | solution.py:519
  27.9 0.6 %collective-permute-start.8 = (f32[16,128]{1,0:T(8,128)S(1)}, f32[16,128]{1,0:T(8,128)S(1)}, u32[]{:S(2)}, u32[]{:S(2)}) collective-permute-start(f32[16,128]{1,0:T(8,128)S(1)} %add.22), channel_id=1, source_target_pairs={{0,4},{2,6},{4,0},{6,2},{8,12},{10,14},{12,8},{14,10},{16,20},{18,... | collective-permute-start | bytes 24584 | tf_op jit(solution)/shard_map/ppermute | solution.py:519
  28.5 1.0 %collective-permute-done.10 = f32[16,128]{1,0:T(8,128)S(1)} collective-permute-done((f32[16,128]{1,0:T(8,128)S(1)}, f32[16,128]{1,0:T(8,128)S(1)}, u32[]{:S(2)}, u32[]{:S(2)}) %collective-permute-start.10) | collective-permute-done | bytes 8224 | tf_op jit(solution)/shard_map/ppermute | solution.py:519
  29.5 2.0 %collective-permute-done.8 = f32[16,128]{1,0:T(8,128)S(1)} collective-permute-done((f32[16,128]{1,0:T(8,128)S(1)}, f32[16,128]{1,0:T(8,128)S(1)}, u32[]{:S(2)}, u32[]{:S(2)}) %collective-permute-start.8) | collective-permute-done | bytes 8224 | tf_op jit(solution)/shard_map/ppermute | solution.py:519
  31.5 0.6 %collective-permute-done.9 = f32[16,128]{1,0:T(8,128)S(1)} collective-permute-done((f32[16,128]{1,0:T(8,128)S(1)}, f32[16,128]{1,0:T(8,128)S(1)}, u32[]{:S(2)}, u32[]{:S(2)}) %collective-permute-start.9) | collective-permute-done | bytes 8224 | tf_op jit(solution)/shard_map/ppermute | solution.py:519
  32.2 2.6 %collective-permute-start.11 = (f32[16,128]{1,0:T(8,128)S(1)}, f32[16,128]{1,0:T(8,128)S(1)}, u32[]{:S(2)}, u32[]{:S(2)}) collective-permute-start(f32[16,128]{1,0:T(8,128)S(1)} %add_add_fusion.own_ref), channel_id=1, source_target_pairs={{0,16},{2,18},{4,20},{6,22},{8,24},{10,26},{12,28},{14,30},{16,0},... | collective-permute-start | bytes 24584 | tf_op jit(solution)/shard_map/ppermute | solution.py:524
  34.8 2.0 %collective-permute-done.11.got_ref = f32[16,128]{1,0:T(8,128)S(1)} collective-permute-done((f32[16,128]{1,0:T(8,128)S(1)}, f32[16,128]{1,0:T(8,128)S(1)}, u32[]{:S(2)}, u32[]{:S(2)}) %collective-permute-start.11) | collective-permute-done | bytes 8224 | tf_op jit(solution)/shard_map/ppermute | solution.py:524
  36.7 0.8 %shard_map.113 = (f32[16,256]{1,0:T(8,128)}, f32[32,36]{1,0:T(8,128)}, f32[1,32]{1,0:T(1,128)}, f32[2,128]{1,0:T(2,128)}) custom-call(f32[4,16,128]{2,1,0:T(8,128)S(1)} %get-tuple-element.12.pack_ref, f32[16,128]{1,0:T(8,128)S(1)} %add_add_fusion.own_ref, f32[16,128]{1,0:T(8,128)S(1)} %collective-permute-done.11.got_ref), custom_call_target="tpu_custom_call" | custom-call | tf_op jit(solution)/shard_map/pallas_call | solution.py:532
  (22 shorter events, 0.1 us)
Async XLA Ops:
  0.6 5.8 %copy-start = (bf16[32,36]{1,0:T(8,128)(2,1)S(1)}, bf16[32,36]{1,0:T(8,128)(2,1)}, u32[]{:S(2)}) copy-start(bf16[32,36]{1,0:T(8,128)(2,1)} %param.10) | copy-start | bytes 6916
  0.6 5.8 %copy-start.4 = (f32[256]{0:T(256)S(1)}, f32[256]{0:T(256)}, u32[]{:S(2)}) copy-start(f32[256]{0:T(256)} %param.12) | copy-start | bytes 3076
  0.7 7.7 %collective-permute-start.2 = (bf16[2,16,512]{2,1,0:T(8,128)(2,1)}, bf16[2,16,512]{2,1,0:T(8,128)(2,1)S(1)}, u32[]{:S(2)}, u32[]{:S(2)}) collective-permute-start(bf16[2,16,512]{2,1,0:T(8,128)(2,1)} %param.8), channel_id=1, source_target_pairs={{0,1},{1,0},{2,3},{3,2},{4,5},{5,4},{6,7},{7,6},{8,9},{9,8},{10,11... | collective-permute-start | bytes 98312 | tf_op jit(solution)/shard_map/ppermute | solution.py:555
  3.7 5.5 %collective-permute-start.1 = (bf16[32,8,128]{2,1,0:T(8,128)(2,1)}, bf16[32,8,128]{2,1,0:T(8,128)(2,1)S(1)}, u32[]{:S(2)}, u32[]{:S(2)}) collective-permute-start(bf16[32,8,128]{2,1,0:T(8,128)(2,1)} %refs_0_.1), channel_id=1, source_target_pairs={{0,1},{1,0},{2,3},{3,2},{4,5},{5,4},{6,7},{7,6},{8,9},{9,8},{10,11... | collective-permute-start | bytes 196616 | tf_op jit(solution)/shard_map/ppermute | solution.py:555
  3.8 5.4 %collective-permute-start = (s32[2,2,1,32]{3,2,1,0:T(1,128)}, s32[2,2,1,32]{3,2,1,0:T(1,128)S(1)}, u32[]{:S(2)}, u32[]{:S(2)}) collective-permute-start(s32[2,2,1,32]{3,2,1,0:T(1,128)} %param.9), channel_id=1, source_target_pairs={{0,1},{1,0},{2,3},{3,2},{4,5},{5,4},{6,7},{7,6},{8,9},{9,8},{10,11... | collective-permute-start | bytes 1544 | tf_op jit(solution)/shard_map/ppermute | solution.py:555
  6.5 1.9 %copy-start.3 = (bf16[2,16,512]{2,1,0:T(8,128)(2,1)S(1)}, bf16[2,16,512]{2,1,0:T(8,128)(2,1)}, u32[]{:S(2)}) copy-start(bf16[2,16,512]{2,1,0:T(8,128)(2,1)} %param.8) | copy-start | bytes 98308
  7.6 0.7 %copy-start.5 = (f32[32]{0:T(128)S(1)}, f32[32]{0:T(128)}, u32[]{:S(2)}) copy-start(f32[32]{0:T(128)} %param.11) | copy-start | bytes 388
  8.4 1.4 %copy-start.1 = (bf16[32,8,128]{2,1,0:T(8,128)(2,1)S(1)}, bf16[32,8,128]{2,1,0:T(8,128)(2,1)}, u32[]{:S(2)}) copy-start(bf16[32,8,128]{2,1,0:T(8,128)(2,1)} %refs_0_.1) | copy-start | bytes 196612
  8.4 1.3 %collective-permute-start.3 = (bf16[4,16,512]{2,1,0:T(8,128)(2,1)S(1)}, bf16[4,16,512]{2,1,0:T(8,128)(2,1)S(1)}, u32[]{:S(2)}, u32[]{:S(2)}) collective-permute-start(bf16[4,16,512]{2,1,0:T(8,128)(2,1)S(1)} %constant_dynamic-update-slice_fusion.refs_4_), channel_id=1, source_target_pairs={{0,2},{2,0},{4,6},{6,4},{8,10},{10,8},{12,14},{14,12},{16,18},{18,... | collective-permute-start | bytes 196616 | tf_op jit(solution)/shard_map/ppermute | solution.py:504
  8.5 1.2 %collective-permute-start.4 = (bf16[4,16,512]{2,1,0:T(8,128)(2,1)S(1)}, bf16[4,16,512]{2,1,0:T(8,128)(2,1)S(1)}, u32[]{:S(2)}, u32[]{:S(2)}) collective-permute-start(bf16[4,16,512]{2,1,0:T(8,128)(2,1)S(1)} %constant_dynamic-update-slice_fusion.refs_4_), channel_id=1, source_target_pairs={{2,4},{4,2},{6,8},{8,6},{10,12},{12,10},{14,16},{16,14},{18,20},{2... | collective-permute-start | bytes 196616 | tf_op jit(solution)/shard_map/ppermute | solution.py:504
  9.2 7.8 %copy-start.2 = (bf16[36,1440]{1,0:T(8,128)(2,1)S(1)}, bf16[36,1440]{1,0:T(8,128)(2,1)}, u32[]{:S(2)}) copy-start(bf16[36,1440]{1,0:T(8,128)(2,1)} %constant.14.clone) | copy-start | bytes 311044
  11.4 6.6 %collective-permute-start.5 = (bf16[80,128]{1,0:T(8,128)(2,1)S(1)}, bf16[80,128]{1,0:T(8,128)(2,1)S(1)}, u32[]{:S(2)}, u32[]{:S(2)}) collective-permute-start(bf16[80,128]{1,0:T(8,128)(2,1)S(1)} %get-tuple-element.13), channel_id=1, source_target_pairs={{0,2},{2,0},{4,6},{6,4},{8,10},{10,8},{12,14},{14,12},{16,18},{18,... | collective-permute-start | bytes 61448 | tf_op jit(solution)/shard_map/ppermute | solution.py:504
  16.3 1.7 %collective-permute-start.6 = (bf16[80,128]{1,0:T(8,128)(2,1)S(1)}, bf16[80,128]{1,0:T(8,128)(2,1)S(1)}, u32[]{:S(2)}, u32[]{:S(2)}) collective-permute-start(bf16[80,128]{1,0:T(8,128)(2,1)S(1)} %get-tuple-element.14), channel_id=1, source_target_pairs={{2,4},{4,2},{6,8},{8,6},{10,12},{12,10},{14,16},{16,14},{18,20},{2... | collective-permute-start | bytes 61448 | tf_op jit(solution)/shard_map/ppermute | solution.py:504
  19.3 5.0 %collective-permute-start.7 = (f32[16,128]{1,0:T(8,128)S(1)}, f32[16,128]{1,0:T(8,128)S(1)}, u32[]{:S(2)}, u32[]{:S(2)}) collective-permute-start(f32[16,128]{1,0:T(8,128)S(1)} %shard_map.112), channel_id=1, source_target_pairs={{0,2},{2,0},{4,6},{6,4},{8,10},{10,8},{12,14},{14,12},{16,18},{18,... | collective-permute-start | bytes 24584 | tf_op jit(solution)/shard_map/ppermute | solution.py:519
  24.3 5.2 %collective-permute-start.10 = (f32[16,128]{1,0:T(8,128)S(1)}, f32[16,128]{1,0:T(8,128)S(1)}, u32[]{:S(2)}, u32[]{:S(2)}) collective-permute-start(f32[16,128]{1,0:T(8,128)S(1)} %add.22), channel_id=1, source_target_pairs={{0,12},{2,14},{4,8},{6,10},{8,4},{10,6},{12,0},{14,2},{16,28},{18,... | collective-permute-start | bytes 24584 | tf_op jit(solution)/shard_map/ppermute | solution.py:519
  27.9 3.7 %collective-permute-start.8 = (f32[16,128]{1,0:T(8,128)S(1)}, f32[16,128]{1,0:T(8,128)S(1)}, u32[]{:S(2)}, u32[]{:S(2)}) collective-permute-start(f32[16,128]{1,0:T(8,128)S(1)} %add.22), channel_id=1, source_target_pairs={{0,4},{2,6},{4,0},{6,2},{8,12},{10,14},{12,8},{14,10},{16,20},{18,... | collective-permute-start | bytes 24584 | tf_op jit(solution)/shard_map/ppermute | solution.py:519
  28.5 3.7 %collective-permute-start.9 = (f32[16,128]{1,0:T(8,128)S(1)}, f32[16,128]{1,0:T(8,128)S(1)}, u32[]{:S(2)}, u32[]{:S(2)}) collective-permute-start(f32[16,128]{1,0:T(8,128)S(1)} %add.22), channel_id=1, source_target_pairs={{0,8},{2,10},{4,12},{6,14},{8,0},{10,2},{12,4},{14,6},{16,24},{18,... | collective-permute-start | bytes 24584 | tf_op jit(solution)/shard_map/ppermute | solution.py:519
  32.2 4.5 %collective-permute-start.11 = (f32[16,128]{1,0:T(8,128)S(1)}, f32[16,128]{1,0:T(8,128)S(1)}, u32[]{:S(2)}, u32[]{:S(2)}) collective-permute-start(f32[16,128]{1,0:T(8,128)S(1)} %add_add_fusion.own_ref), channel_id=1, source_target_pairs={{0,16},{2,18},{4,20},{6,22},{8,24},{10,26},{12,28},{14,30},{16,0},... | collective-permute-start | bytes 24584 | tf_op jit(solution)/shard_map/ppermute | solution.py:524

commit v4 on v3

--- a/solution.py
+++ b/solution.py
@@ -56,22 +56,6 @@
 def waves(phase, parts):
     phase = phase & 15
     return wave(phase, parts), wave((phase + 12) & 15, parts)
-
-
-def tap_tables():
-    place = np.zeros((36, 10, 144))
-    back = np.zeros((96, 10, 36))
-    for a in range(3):
-        for b in range(3):
-            for p in range(2):
-                for q in range(2):
-                    tap = (3 * a + b) * 4 + 2 * p + q
-                    for sy in range(10):
-                        r = 2 * (sy + a) + p
-                        place[tap, sy, (q * 3 + b) * 24 + r] = 1.0
-                        if 4 <= r < 20:
-                            back[(q * 3 + b) * 16 + r - 4, sy, tap] = 1.0
-    return place, back
 
 
 def turn(re, im, k, n):
@@ -115,62 +99,16 @@
     return b if a is None else [x + y for x, y in zip(a, b)]
 
 
-def merge_kernel(dims, *refs):
-    nf, fl, G, T, nsc = dims
-    F = nf * fl
-    dx_refs, refs = refs[:nf], refs[nf:]
-    goal_refs, refs = refs[:nf], refs[nf:]
-    y_ref, yc_ref, yf_ref, var_ref = refs[:4]
-    pack_ref, pc_ref, pf_ref, h_ref = refs[4:8]
-    x_ref, idx_ref, p_ref, q_ref, xs_ref, goal_ref = refs[8:14]
-    fwd_ref, fwdl_ref, inv_ref, invl_ref = refs[14:18]
-    dy_refs, sems = refs[18 : 18 + nf], refs[18 + nf]
-    moves = [
-        pltpu.make_async_copy(src, dst, sems.at[j])
-        for j, (src, dst) in enumerate(zip(dx_refs, dy_refs))
-    ]
-    for move in moves:
-        move.start()
-    s = lax.axis_index("space")
-    fr = lax.axis_index("frame")
-    odd = lax.rem(s, 2)
-
-    slots = ((y_ref, 1), (yc_ref, 2 - 2 * odd), (yf_ref, 2 * odd))
-
-    def fill(f, carry):
-        for ref, slot in slots:
-            rows = ref[f].astype(F32)
-            for g in range(G):
-                block = rows[:, g * LANES : (g + 1) * LANES]
-                x_ref[f * G + g, pl.ds(pl.multiple_of(slot * TILE, TILE), TILE), :] = block
-        return carry
-
-    lax.fori_loop(0, F, fill, 0, unroll=min(F, 4))
-
-    spot = lax.broadcasted_iota(jnp.int32, (8, LANES), 1)
-    for j in range(nf):
-        for l in range(fl):
-            row = dx_refs[j][l, 1]
-            if T < LANES:
-                row = jnp.concatenate([row, jnp.zeros((1, LANES - T), jnp.int32)], axis=1)
-            row = jnp.broadcast_to(row, (8, LANES))
-            for g in range(G):
-                moved = jnp.take_along_axis(row, 8 * g + spot // TILE, axis=1)
-                idx_ref[(j * fl + l) * G + g] = (moved + (spot - TILE)) & (LANES - 1)
-
-    lead = G * 4
-    for j in range(nf):
-        for c in range(nsc):
-            cols = slice(c * LANES, (c + 1) * LANES)
-            goal_ref[j * nsc + c] = goal_refs[j][:, :, cols].astype(F32).reshape(256, LANES)
-    for k in range(nf * nsc):
-        rows = slice(lead + k * 32, lead + k * 32 + 32)
-        pc_ref[rows, :] = goal_ref[k, pl.ds(7 - 7 * odd, 32, stride=8), :].astype(BF16)
-        pf_ref[rows, :] = goal_ref[k, pl.ds(7 * odd, 32, stride=8), :].astype(BF16)
+def table_kernel(weight_ref, var_ref, offs_ref, shift_ref, *refs):
+    fwd_ref, fwdl_ref, inv_ref, invl_ref, part_ref, wideh_ref, widel_ref = refs[:7]
+    big_ref, bigt_ref, small_ref, shift_out_ref, rows_ref = refs[7:]
+    shift_out_ref[...] = shift_ref[...]
+    offs = jnp.concatenate([offs_ref[...], jnp.zeros((1, LANES - 32), F32)], axis=1)
+    small_ref[...] = jnp.concatenate(
+        [jnp.exp(var_ref[...]), offs, jnp.zeros((5, LANES), F32)], axis=0
+    )
 
     lane = lax.broadcasted_iota(jnp.int32, (TILE, LANES), 1)
-    kind = (lane // TILE) % 4
-
     line = lax.broadcasted_iota(jnp.int32, (TILE, LANES), 0)
     cos, sin = waves(line * (lane & 15), 3)
     for k in range(8):
@@ -186,6 +124,122 @@
         inv_ref[mid, :] = jnp.concatenate([-d[0], -d[1]], axis=1)
         invl_ref[at, :] = c[2]
         invl_ref[mid, :] = -d[2]
+    line = lax.broadcasted_iota(jnp.int32, (256, 256), 0)
+    column = lax.broadcasted_iota(jnp.int32, (256, 256), 1)
+    source = 2 * (column & 127) + (column >> 7)
+    part_ref[...] = jnp.where(line == source, 1.0, 0.0).astype(BF16)
+    lane8 = lax.broadcasted_iota(jnp.int32, (8, LANES), 1)
+    line8 = lax.broadcasted_iota(jnp.int32, (8, LANES), 0)
+    empty = jnp.zeros((8, LANES), F32)
+    for q in range(2):
+        cos, sin = waves((2 * line8 + q) * (lane8 & 15), 2)
+        for t in range(0, 16, 2):
+            for ref, c, d in ((wideh_ref, cos[0], sin[0]), (widel_ref, cos[1], sin[1])):
+                rows = []
+                for u in (t, t + 1):
+                    here = lane8 // TILE == u % 8
+                    row = []
+                    for v in (c, d):
+                        v = jnp.where(here, v, 0.0)
+                        row += [v, empty] if u < 8 else [empty, v]
+                    rows.append(jnp.concatenate(row, axis=1))
+                at = q * 128 + t * 8
+                ref[at : at + 16, :] = jnp.concatenate(rows, axis=0).astype(BF16)
+
+    weight = weight_ref[...].astype(F32)
+    weight = jnp.concatenate([weight, jnp.zeros((32, LANES - 36), F32)], axis=1)
+    halves = []
+    for h in range(2):
+        at = lax.broadcasted_iota(jnp.int32, (32, LANES), 1) + h * LANES
+        group = (at * 171) >> 12
+        row = at - 24 * group
+        q = jnp.where(group >= 3, 1, 0)
+        tap = (3 * (row >> 1) + group - 3 * q) * 4 + 2 * (row & 1) + q
+        valid = (row < 6) & (group < 6)
+        taken = jnp.take_along_axis(weight, jnp.where(valid, tap, 0), axis=1)
+        halves.append(jnp.where(valid, taken, 0.0))
+    base = jnp.concatenate(halves, axis=1)
+    for sy in range(10):
+        moved = pltpu.roll(base, 2 * sy, 1) if sy else base
+        big_ref[sy * 32 : (sy + 1) * 32, :] = moved.astype(BF16)
+
+    turned = jnp.transpose(jnp.concatenate([weight] * 4, axis=0))
+    rows_ref[...] = jnp.zeros_like(rows_ref)
+    for q in range(2):
+        for b in range(3):
+            for j in range(6):
+                tap = (3 * (j // 2) + b) * 4 + 2 * (j % 2) + q
+                rows_ref[q * 3 + b, 16 + j : 17 + j, :] = turned[tap : tap + 1, :]
+    quarter = lax.broadcasted_iota(jnp.int32, (TILE, LANES), 1) // 32
+    for k in range(6):
+        for tile in range(3):
+            value = jnp.zeros((TILE, LANES), F32)
+            for u in range(4):
+                sy = 4 * tile + u
+                if sy < 10:
+                    block = rows_ref[k, 20 - 2 * sy : 36 - 2 * sy, :]
+                    value = jnp.where(quarter == u, block, value)
+            width = 64 if tile == 2 else LANES
+            at = tile * LANES
+            bigt_ref[k * TILE : (k + 1) * TILE, at : at + width] = value[:, :width].astype(BF16)
+
+
+def merge_kernel(dims, *refs):
+    nf, fl, G, T, nsc = dims
+    F = nf * fl
+    dx_refs, refs = refs[:nf], refs[nf:]
+    goal_refs, refs = refs[:nf], refs[nf:]
+    y_ref, yc_ref, yf_ref, var_ref = refs[:4]
+    fwd_ref, fwdl_ref, inv_ref, invl_ref = refs[4:8]
+    pack_ref, pc_ref, pf_ref, h_ref = refs[8:12]
+    x_ref, idx_ref, p_ref, q_ref, xs_ref, goal_ref = refs[12:18]
+    dy_refs, sems = refs[18 : 18 + nf], refs[18 + nf]
+    moves = [
+        pltpu.make_async_copy(src, dst, sems.at[j])
+        for j, (src, dst) in enumerate(zip(dx_refs, dy_refs))
+    ]
+    for move in moves:
+        move.start()
+    s = lax.axis_index("space")
+    fr = lax.axis_index("frame")
+    odd = lax.rem(s, 2)
+
+    slots = ((y_ref, 1), (yc_ref, 2 - 2 * odd), (yf_ref, 2 * odd))
+
+    def fill(f, carry):
+        for ref, slot in slots:
+            rows = ref[f].astype(F32)
+            for g in range(G):
+                block = rows[:, g * LANES : (g + 1) * LANES]
+                x_ref[f * G + g, pl.ds(pl.multiple_of(slot * TILE, TILE), TILE), :] = block
+        return carry
+
+    lax.fori_loop(0, F, fill, 0, unroll=min(F, 4))
+
+    spot = lax.broadcasted_iota(jnp.int32, (8, LANES), 1)
+    for j in range(nf):
+        for l in range(fl):
+            row = dx_refs[j][l, 1]
+            if T < LANES:
+                row = jnp.concatenate([row, jnp.zeros((1, LANES - T), jnp.int32)], axis=1)
+            row = jnp.broadcast_to(row, (8, LANES))
+            for g in range(G):
+                moved = jnp.take_along_axis(row, 8 * g + spot // TILE, axis=1)
+                idx_ref[(j * fl + l) * G + g] = (moved + spot) & (LANES - 1)
+
+    lead = G * 4
+    for j in range(nf):
+        for c in range(nsc):
+            cols = slice(c * LANES, (c + 1) * LANES)
+            goal_ref[j * nsc + c] = goal_refs[j][:, :, cols].astype(F32).reshape(256, LANES)
+    for k in range(nf * nsc):
+        rows = slice(lead + k * 32, lead + k * 32 + 32)
+        pc_ref[rows, :] = goal_ref[k, pl.ds(7 - 7 * odd, 32, stride=8), :].astype(BF16)
+        pf_ref[rows, :] = goal_ref[k, pl.ds(7 * odd, 32, stride=8), :].astype(BF16)
+
+    lane = lax.broadcasted_iota(jnp.int32, (TILE, LANES), 1)
+    kind = (lane // TILE) % 4
+
     per = 16 // G
     chunks = F * G // 16
     rows_out = max(G, 8)
@@ -225,7 +279,7 @@
             def load(t, group):
                 if group < 0 or group >= G:
                     return zero
-                start = row_shift(f, 8 * g + t)
+                start = TILE + row_shift(f, 8 * g + t)
                 return x_ref[f * G + group, pl.ds(start, TILE), :]
 
             idx = idx_ref[f * G + g]
@@ -318,9 +372,8 @@
     W = G * LANES
     half = W // 2
     goal_refs = refs[:nf]
-    big_ref, bigt_ref, offs_ref = refs[nf : nf + 3]
-    out_ref, goal_ref, raw_ref, mm_ref, p_ref, q_ref, ns_ref = refs[nf + 3 : nf + 10]
-    part_ref, wideh_ref, widel_ref = refs[nf + 10 :]
+    big_ref, bigt_ref, offs_ref, part_ref, wideh_ref, widel_ref = refs[nf : nf + 6]
+    out_ref, goal_ref, raw_ref, mm_ref, p_ref, q_ref, ns_ref = refs[nf + 6 :]
     s = lax.axis_index("space")
     fr = lax.axis_index("frame")
     odd = lax.rem(s, 2)
@@ -341,28 +394,6 @@
                 val = ref[first : first + 32, :].astype(F32)
                 goal_ref[row, :, pl.ds(pl.multiple_of(at + c * LANES, LANES), LANES)] = val
 
-    line = lax.broadcasted_iota(jnp.int32, (256, 256), 0)
-    column = lax.broadcasted_iota(jnp.int32, (256, 256), 1)
-    source = 2 * (column & 127) + (column >> 7)
-    part_ref[...] = jnp.where(line == source, 1.0, 0.0).astype(BF16)
-    lane8 = lax.broadcasted_iota(jnp.int32, (8, LANES), 1)
-    line8 = lax.broadcasted_iota(jnp.int32, (8, LANES), 0)
-    empty = jnp.zeros((8, LANES), F32)
-    for q in range(2):
-        cos, sin = waves((2 * line8 + q) * (lane8 & 15), 2)
-        for t in range(0, 16, 2):
-            for ref, c, d in ((wideh_ref, cos[0], sin[0]), (widel_ref, cos[1], sin[1])):
-                rows = []
-                for u in (t, t + 1):
-                    here = lane8 // TILE == u % 8
-                    row = []
-                    for v in (c, d):
-                        v = jnp.where(here, v, 0.0)
-                        row += [v, empty] if u < 8 else [empty, v]
-                    rows.append(jnp.concatenate(row, axis=1))
-                at = q * 128 + t * 8
-                ref[at : at + 16, :] = jnp.concatenate(rows, axis=0).astype(BF16)
-
     near = pc_ref[0:lead, :].astype(F32)
     far = pf_ref[0:lead, :].astype(F32)
     low = jnp.where(odd == 1, near, far)
@@ -388,7 +419,7 @@
     pieces.append(jnp.zeros((112, half), F32))
     taps = jnp.concatenate(pieces, axis=0).astype(BF16)
 
-    preact = dot(big_ref[...], taps[:144])
+    preact = dot(big_ref[...], taps)
     diag = lax.broadcasted_iota(jnp.int32, (32, LANES), 0) == lax.broadcasted_iota(
         jnp.int32, (32, LANES), 1
     )
@@ -466,7 +497,7 @@
     gw = jnp.where(tap == 36, jnp.sum(bias, axis=1, keepdims=True), gw)
     gw = jnp.where(tap < 37, gw, 0.0)
     first = gw[0:8] + (pltpu.roll(gw[8:16], 37, 1) + pltpu.roll(gw[16:24], 74, 1))
-    group = lane8 // TILE
+    group = lax.broadcasted_iota(jnp.int32, (8, LANES), 1) // TILE
     second = jnp.where(group == 5, noise[:8], jnp.where(group == 6, noise[8:], gw[24:32]))
     out_ref[...] = jnp.concatenate([first, second], axis=0)
 
@@ -564,22 +595,33 @@
     y = lax.optimization_barrier(y)
     for j in range(1, nf):
         y = lax.dynamic_update_slice(y, raws[j], (j * fl, 0, 0))
-    shift_parts = [v + TILE for v in shift_parts]
-    small = jnp.concatenate(
-        [jnp.exp(log_var), offset, jnp.zeros((6 * LANES - channels,), F32)]
-    ).reshape(8, LANES)
     yf = involution(y, n_space, 1, 1)
     yc = involution(y, n_space, 1, 0)
-    place, place_t = tap_tables()
-    big = dot(weight, jnp.asarray(place.reshape(36, -1), BF16))
-    big = big.reshape(channels, 10, 144).transpose(1, 0, 2).reshape(320, 144).astype(BF16)
-    bigt = dot(jnp.asarray(place_t.reshape(-1, 36), BF16), weight.T)
-    bigt = bigt.reshape(96, 320).astype(BF16)
+    shape = jax.ShapeDtypeStruct
+    *tables, big, bigt, small, own_shifts = call(
+        table_kernel,
+        [weight, log_var.reshape(2, LANES), offset.reshape(1, channels), shifts],
+        [
+            shape((256, 256), BF16),
+            shape((128, 256), BF16),
+            shape((256, 256), BF16),
+            shape((256, 128), BF16),
+            shape((256, 256), BF16),
+            shape((256, 512), BF16),
+            shape((256, 512), BF16),
+            shape((320, 256), BF16),
+            shape((96, 320), BF16),
+            shape((8, LANES), F32),
+            shape(shifts.shape, jnp.int32),
+        ],
+        [pltpu.VMEM((6, 40, LANES), F32)],
+    )
+    shift_parts[0] = own_shifts
+
     side = 4 * G + nf * nsc * channels
-    shape = jax.ShapeDtypeStruct
     pack, pc, pf, moments = call(
         functools.partial(merge_kernel, (nf, fl, G, T, nsc)),
-        [*shift_parts, *goals, y, yc, yf, small],
+        [*shift_parts, *goals, y, yc, yf, small, *tables[:4]],
         [
             shape((G, TILE, LANES), F32),
             shape((side, LANES), BF16),
@@ -593,10 +635,6 @@
             pltpu.VMEM((256, LANES), F32),
             pltpu.VMEM((16 * rows_out, LANES), F32),
             pltpu.VMEM((nf * nsc, 256, LANES), F32),
-            pltpu.VMEM((256, 256), BF16),
-            pltpu.VMEM((128, 256), BF16),
-            pltpu.VMEM((256, 256), BF16),
-            pltpu.VMEM((256, 128), BF16),
             *[pltpu.SMEM(shifts.shape, jnp.int32)] * nf,
             pltpu.SemaphoreType.DMA((nf,)),
         ],
@@ -605,7 +643,7 @@
     pc = involution(pc, n_space, 1, 0)
     (partial,) = call(
         functools.partial(demosaic_kernel, (nf, fl, G, nsc, n_space, inv_pixels)),
-        [pack, pc, pf, moments, *goals, big, bigt, small],
+        [pack, pc, pf, moments, *goals, big, bigt, small, *tables[4:]],
         [shape((16, LANES), F32)],
         [
             pltpu.VMEM((10, channels, W // 2), F32),
@@ -614,9 +652,6 @@
             pltpu.VMEM((rows_out * TILE, LANES), F32),
             pltpu.VMEM((rows_out * TILE, LANES), F32),
             pltpu.VMEM((rows_out * TILE, LANES), F32),
-            pltpu.VMEM((256, 256), BF16),
-            pltpu.VMEM((256, 512), BF16),
-            pltpu.VMEM((256, 512), BF16),
         ],
     )
     merged, grad_weight, grad_bias, grad_noise = call(

time: 37.7 us -> 36.3 us (0.963)
  waiting for transfers between devices: 6.97 us -> 9.41 us
  starting transfers between devices: 22.3 us -> 20.5 us
  matrix products: 1.3 us -> 0 us
  other arithmetic: 0.8 us -> 0.01 us
    ppermute x3, waiting for transfers between devices: 0.01 us -> 2.58 us  [from_frame(): return lax.ppermute(value, 'frame', [(i, (i - j) % nf) for i in range(nf)])]
    dot_general x2 -> x0, matrix products: 1.3 us -> none  [dot(): return lax.dot_general(a, b, (dims, ((), ())), preferred_element_type=F32)]
    ppermute x4, starting transfers between devices: 6.27 us -> 5.13 us  [involution(): return lax.ppermute(value, 'space', pairs)]
    convert_element_type x4 -> x0, local copies, waits for them, and re-layouts: 0.87 us -> none  [the longest x2 0.47 us: shards(): big.reshape(channels, 10, 144).transpose(1, 0, 2).reshape(320, 144)]
    pad x1, local copies, waits for them, and re-layouts: 0.01 us -> 0.79 us  [shards(): y = jnp.pad(raw, ((0, F - fl), (0, 0), (0, 0)))]
    ppermute x3, starting transfers between devices: 5.06 us -> 4.33 us  [from_frame(): return lax.ppermute(value, 'frame', [(i, (i - j) % nf) for i in range(nf)])]
    add x2 -> x0, other arithmetic: 0.72 us -> none  [shards(): shift_parts = [v + TILE for v in shift_parts]]
    pallas_call x3 -> x4, Pallas kernels: 3.7 us -> 3.97 us  [call(): pl.pallas_call(body, out_shape=tuple(outs), in_specs=[vm] * len(args), ou...]
  transfers between devices with their start and end apart: 12 -> 12, of which waited for: 6 -> 8; matrix products, arithmetic and copies ran while one was open for 8% -> 2% of each run, Pallas kernels for 0% -> 1%
where the time goes in v4:
time: 36.3 us; the launch traced here: 36.1 us
  starting transfers between devices  20.5 us (56%)
  waiting for transfers between devices  9.41 us (26%)
  Pallas kernels  3.97 us (11%)
  local copies, waits for them, and re-layouts  1.48 us (4%)
  between operations  0.7 us (2%)
    ppermute x4, starting transfers between devices, sum_space(): got.append(lax.ppermute(value, 'space', [(i, i ^ m) for i in range(count)]))  8.46 us
    ppermute x4, starting transfers between devices, involution(): return lax.ppermute(value, 'space', pairs)  5.13 us
    ppermute x4, waiting for transfers between devices, sum_space(): got.append(lax.ppermute(value, 'space', [(i, i ^ m) for i in range(count)]))  4.36 us
    ppermute x3, starting transfers between devices, from_frame(): return lax.ppermute(value, 'frame', [(i, (i - j) % nf) for i in range(nf)])  4.33 us
    pallas_call x4, Pallas kernels, call(): pl.pallas_call(body, out_shape=tuple(outs), in_specs=[vm] * len(args), ou...  3.97 us
    ppermute x1, starting transfers between devices, sum_space(): got = lax.ppermute(value, 'space', [(i, i ^ mask) for i in range(count)])  2.58 us
    ppermute x3, waiting for transfers between devices, from_frame(): return lax.ppermute(value, 'frame', [(i, (i - j) % nf) for i in range(nf)])  2.58 us
    ppermute x1, waiting for transfers between devices, sum_space(): got = lax.ppermute(value, 'space', [(i, i ^ mask) for i in range(count)])  1.96 us
  transfers between devices with their start and end apart: 12, of which 8 were waited for; matrix products, arithmetic and copies ran while one was open for 2% of the time, Pallas kernels for 1%

profile of v4, /device:TPU:0, one launch (start us, length us, event | category | flops | bytes accessed | tf_op | source)
XLA Modules:
  0.0 36.1 jit_solution(142647896897358012)
XLA Ops:
  0.6 3.0 %collective-permute-start.2 = (bf16[2,16,512]{2,1,0:T(8,128)(2,1)}, bf16[2,16,512]{2,1,0:T(8,128)(2,1)S(1)}, u32[]{:S(2)}, u32[]{:S(2)}) collective-permute-start(bf16[2,16,512]{2,1,0:T(8,128)(2,1)} %param.6), channel_id=1, source_target_pairs={{0,1},{1,0},{2,3},{3,2},{4,5},{5,4},{6,7},{7,6},{8,9},{9,8},{10,11... | collective-permute-start | bytes 98312 | tf_op jit(solution)/shard_map/ppermute | solution.py:586
  3.7 0.1 collective-permute-start.1
  3.7 0.8 %pad.4 = bf16[4,16,512]{2,1,0:T(8,128)(2,1)S(1)} pad(bf16[2,16,512]{2,1,0:T(8,128)(2,1)} %param.6, bf16[]{:T(256)} %constant.1.clone.1), padding=0_2x0_0x0_0 | pad | bytes 98306 | tf_op jit(solution)/shard_map/jit(_pad)/pad | solution.py:594
  4.5 1.2 %collective-permute-done.2 = bf16[2,16,512]{2,1,0:T(8,128)(2,1)S(1)} collective-permute-done((bf16[2,16,512]{2,1,0:T(8,128)(2,1)}, bf16[2,16,512]{2,1,0:T(8,128)(2,1)S(1)}, u32[]{:S(2)}, u32[]{:S(2)}) %collective-permute-start.2) | collective-permute-done | bytes 32800 | tf_op jit(solution)/shard_map/ppermute | solution.py:586
  5.8 0.7 %collective-permute-start.4 = (bf16[4,16,512]{2,1,0:T(8,128)(2,1)S(1)}, bf16[4,16,512]{2,1,0:T(8,128)(2,1)S(1)}, u32[]{:S(2)}, u32[]{:S(2)}) collective-permute-start(bf16[4,16,512]{2,1,0:T(8,128)(2,1)S(1)} %constant_dynamic-update-slice_fusion.refs_4_), channel_id=1, source_target_pairs={{2,4},{4,2},{6,8},{8,6},{10,12},{12,10},{14,16},{16,14},{18,20},{2... | collective-permute-start | bytes 196616 | tf_op jit(solution)/shard_map/ppermute | solution.py:535
  6.4 3.7 %collective-permute-start.3 = (bf16[4,16,512]{2,1,0:T(8,128)(2,1)S(1)}, bf16[4,16,512]{2,1,0:T(8,128)(2,1)S(1)}, u32[]{:S(2)}, u32[]{:S(2)}) collective-permute-start(bf16[4,16,512]{2,1,0:T(8,128)(2,1)S(1)} %constant_dynamic-update-slice_fusion.refs_4_), channel_id=1, source_target_pairs={{0,2},{2,0},{4,6},{6,4},{8,10},{10,8},{12,14},{14,12},{16,18},{18,... | collective-permute-start | bytes 196616 | tf_op jit(solution)/shard_map/ppermute | solution.py:535
  10.2 0.0 copy-done.2
  10.2 1.2 %collective-permute-start = (s32[2,2,1,32]{3,2,1,0:T(1,128)S(1)}, s32[2,2,1,32]{3,2,1,0:T(1,128)S(1)}, u32[]{:S(2)}, u32[]{:S(2)}) collective-permute-start(s32[2,2,1,32]{3,2,1,0:T(1,128)S(1)} %copy-done.2), channel_id=1, source_target_pairs={{0,1},{1,0},{2,3},{3,2},{4,5},{5,4},{6,7},{7,6},{8,9},{9,8},{10,11... | collective-permute-start | bytes 1544 | tf_op jit(solution)/shard_map/ppermute | solution.py:586
  11.4 0.0 copy-done.1
  11.4 0.7 %copy-done.3 = f32[256]{0:T(256)S(1)} copy-done((f32[256]{0:T(256)S(1)}, f32[256]{0:T(256)}, u32[]{:S(2)}) %copy-start.3) | copy-done | bytes 1048
  12.1 0.3 shard_map.93
  12.4 1.3 %collective-permute-done.refs_1_ = s32[2,2,1,32]{3,2,1,0:T(1,128)S(1)} collective-permute-done((s32[2,2,1,32]{3,2,1,0:T(1,128)S(1)}, s32[2,2,1,32]{3,2,1,0:T(1,128)S(1)}, u32[]{:S(2)}, u32[]{:S(2)}) %collective-permute-start) | collective-permute-done | bytes 544 | tf_op jit(solution)/shard_map/ppermute | solution.py:586
  13.8 0.0 collective-permute-done.1.refs_3_.refs_1_
  13.8 0.0 collective-permute-done.4.refs_6_
  13.8 0.0 collective-permute-done.3.refs_5_
  13.8 1.6 %shard_map.94 = (f32[4,16,128]{2,1,0:T(8,128)S(1)}, bf16[80,128]{1,0:T(8,128)(2,1)S(1)}, bf16[80,128]{1,0:T(8,128)(2,1)S(1)}, f32[256,128]{1,0:T(8,128)S(1)}) custom-call(s32[2,2,1,32]{3,2,1,0:T(1,128)S(1)} %get-tuple-element.23.refs_0_, s32[2,2,1,32]{3,2,1,0:T(1,128)S(1)} %collective-permute-done.refs_1_, bf16[32,8,128]{2,1,0:T(8,128)(2,1)S(1)} %copy-done, ...), custom_call_target="tpu_custom_call" | custom-call | tf_op jit(solution)/shard_map/pallas_call | solution.py:563
  15.4 0.1 collective-permute-start.5
  15.5 0.7 %collective-permute-start.6 = (bf16[80,128]{1,0:T(8,128)(2,1)S(1)}, bf16[80,128]{1,0:T(8,128)(2,1)S(1)}, u32[]{:S(2)}, u32[]{:S(2)}) collective-permute-start(bf16[80,128]{1,0:T(8,128)(2,1)S(1)} %get-tuple-element.31), channel_id=1, source_target_pairs={{2,4},{4,2},{6,8},{8,6},{10,12},{12,10},{14,16},{16,14},{18,20},{2... | collective-permute-start | bytes 61448 | tf_op jit(solution)/shard_map/ppermute | solution.py:535
  16.1 0.5 %collective-permute-done.5.pc_ref = bf16[80,128]{1,0:T(8,128)(2,1)S(1)} collective-permute-done((bf16[80,128]{1,0:T(8,128)(2,1)S(1)}, bf16[80,128]{1,0:T(8,128)(2,1)S(1)}, u32[]{:S(2)}, u32[]{:S(2)}) %collective-permute-start.5) | collective-permute-done | bytes 20512 | tf_op jit(solution)/shard_map/ppermute | solution.py:535
  16.6 0.0 collective-permute-done.6.pf_ref
  16.6 1.3 %shard_map.95 = f32[16,128]{1,0:T(8,128)S(1)} custom-call(f32[4,16,128]{2,1,0:T(8,128)S(1)} %get-tuple-element.29.pack_ref, bf16[80,128]{1,0:T(8,128)(2,1)S(1)} %collective-permute-done.5.pc_ref, bf16[80,128]{1,0:T(8,128)(2,1)S(1)} %collective-permute-done.6.pf_ref, f32[256,128]{1,0:T(8,128)S(1)} %get-tuple-element.32.h_ref, ...), custom_call_target="tpu_custom_call" | custom-call | tf_op jit(solution)/shard_map/pallas_call | solution.py:563
  17.9 4.5 %collective-permute-start.7 = (f32[16,128]{1,0:T(8,128)S(1)}, f32[16,128]{1,0:T(8,128)S(1)}, u32[]{:S(2)}, u32[]{:S(2)}) collective-permute-start(f32[16,128]{1,0:T(8,128)S(1)} %shard_map.95), channel_id=1, source_target_pairs={{0,2},{2,0},{4,6},{6,4},{8,10},{10,8},{12,14},{14,12},{16,18},{18,... | collective-permute-start | bytes 24584 | tf_op jit(solution)/shard_map/ppermute | solution.py:550
  22.4 0.8 %collective-permute-done.7 = f32[16,128]{1,0:T(8,128)S(1)} collective-permute-done((f32[16,128]{1,0:T(8,128)S(1)}, f32[16,128]{1,0:T(8,128)S(1)}, u32[]{:S(2)}, u32[]{:S(2)}) %collective-permute-start.7) | collective-permute-done | bytes 8224 | tf_op jit(solution)/shard_map/ppermute | solution.py:550
  23.2 3.4 %collective-permute-start.10 = (f32[16,128]{1,0:T(8,128)S(1)}, f32[16,128]{1,0:T(8,128)S(1)}, u32[]{:S(2)}, u32[]{:S(2)}) collective-permute-start(f32[16,128]{1,0:T(8,128)S(1)} %add.14), channel_id=1, source_target_pairs={{0,12},{2,14},{4,8},{6,10},{8,4},{10,6},{12,0},{14,2},{16,28},{18,... | collective-permute-start | bytes 24584 | tf_op jit(solution)/shard_map/ppermute | solution.py:550
  26.6 0.4 %collective-permute-start.9 = (f32[16,128]{1,0:T(8,128)S(1)}, f32[16,128]{1,0:T(8,128)S(1)}, u32[]{:S(2)}, u32[]{:S(2)}) collective-permute-start(f32[16,128]{1,0:T(8,128)S(1)} %add.14), channel_id=1, source_target_pairs={{0,8},{2,10},{4,12},{6,14},{8,0},{10,2},{12,4},{14,6},{16,24},{18,... | collective-permute-start | bytes 24584 | tf_op jit(solution)/shard_map/ppermute | solution.py:550
  27.1 0.1 collective-permute-start.8
  27.2 1.1 %collective-permute-done.10 = f32[16,128]{1,0:T(8,128)S(1)} collective-permute-done((f32[16,128]{1,0:T(8,128)S(1)}, f32[16,128]{1,0:T(8,128)S(1)}, u32[]{:S(2)}, u32[]{:S(2)}) %collective-permute-start.10) | collective-permute-done | bytes 8224 | tf_op jit(solution)/shard_map/ppermute | solution.py:550
  28.3 2.0 %collective-permute-done.9 = f32[16,128]{1,0:T(8,128)S(1)} collective-permute-done((f32[16,128]{1,0:T(8,128)S(1)}, f32[16,128]{1,0:T(8,128)S(1)}, u32[]{:S(2)}, u32[]{:S(2)}) %collective-permute-start.9) | collective-permute-done | bytes 8224 | tf_op jit(solution)/shard_map/ppermute | solution.py:550
  30.3 0.4 %collective-permute-done.8 = f32[16,128]{1,0:T(8,128)S(1)} collective-permute-done((f32[16,128]{1,0:T(8,128)S(1)}, f32[16,128]{1,0:T(8,128)S(1)}, u32[]{:S(2)}, u32[]{:S(2)}) %collective-permute-start.8) | collective-permute-done | bytes 8224 | tf_op jit(solution)/shard_map/ppermute | solution.py:550
  30.7 2.6 %collective-permute-start.11 = (f32[16,128]{1,0:T(8,128)S(1)}, f32[16,128]{1,0:T(8,128)S(1)}, u32[]{:S(2)}, u32[]{:S(2)}) collective-permute-start(f32[16,128]{1,0:T(8,128)S(1)} %add_add_fusion.own_ref), channel_id=1, source_target_pairs={{0,16},{2,18},{4,20},{6,22},{8,24},{10,26},{12,28},{14,30},{16,0},... | collective-permute-start | bytes 24584 | tf_op jit(solution)/shard_map/ppermute | solution.py:555
  33.3 2.0 %collective-permute-done.11.got_ref = f32[16,128]{1,0:T(8,128)S(1)} collective-permute-done((f32[16,128]{1,0:T(8,128)S(1)}, f32[16,128]{1,0:T(8,128)S(1)}, u32[]{:S(2)}, u32[]{:S(2)}) %collective-permute-start.11) | collective-permute-done | bytes 8224 | tf_op jit(solution)/shard_map/ppermute | solution.py:555
  35.3 0.8 %shard_map.96 = (f32[16,256]{1,0:T(8,128)}, f32[32,36]{1,0:T(8,128)}, f32[1,32]{1,0:T(1,128)}, f32[2,128]{1,0:T(2,128)}) custom-call(f32[4,16,128]{2,1,0:T(8,128)S(1)} %get-tuple-element.29.pack_ref, f32[16,128]{1,0:T(8,128)S(1)} %add_add_fusion.own_ref, f32[16,128]{1,0:T(8,128)S(1)} %collective-permute-done.11.got_ref), custom_call_target="tpu_custom_call" | custom-call | tf_op jit(solution)/shard_map/pallas_call | solution.py:563
  (10 shorter events, 0.0 us)
Async XLA Ops:
  0.6 5.1 %collective-permute-start.2 = (bf16[2,16,512]{2,1,0:T(8,128)(2,1)}, bf16[2,16,512]{2,1,0:T(8,128)(2,1)S(1)}, u32[]{:S(2)}, u32[]{:S(2)}) collective-permute-start(bf16[2,16,512]{2,1,0:T(8,128)(2,1)} %param.6), channel_id=1, source_target_pairs={{0,1},{1,0},{2,3},{3,2},{4,5},{5,4},{6,7},{7,6},{8,9},{9,8},{10,11... | collective-permute-start | bytes 98312 | tf_op jit(solution)/shard_map/ppermute | solution.py:586
  3.7 10.1 %collective-permute-start.1 = (bf16[32,8,128]{2,1,0:T(8,128)(2,1)}, bf16[32,8,128]{2,1,0:T(8,128)(2,1)S(1)}, u32[]{:S(2)}, u32[]{:S(2)}) collective-permute-start(bf16[32,8,128]{2,1,0:T(8,128)(2,1)} %refs_0_.1), channel_id=1, source_target_pairs={{0,1},{1,0},{2,3},{3,2},{4,5},{5,4},{6,7},{7,6},{8,9},{9,8},{10,11... | collective-permute-start | bytes 196616 | tf_op jit(solution)/shard_map/ppermute | solution.py:586
  3.7 6.4 %copy-start.2 = (s32[2,2,1,32]{3,2,1,0:T(1,128)S(1)}, s32[2,2,1,32]{3,2,1,0:T(1,128)}, u32[]{:S(2)}) copy-start(s32[2,2,1,32]{3,2,1,0:T(1,128)} %shift_ref.1) | copy-start | bytes 1540
  3.7 7.7 %copy-start.1 = (bf16[32,36]{1,0:T(8,128)(2,1)S(1)}, bf16[32,36]{1,0:T(8,128)(2,1)}, u32[]{:S(2)}) copy-start(bf16[32,36]{1,0:T(8,128)(2,1)} %weight_ref.1) | copy-start | bytes 6916
  4.5 9.2 %copy-start = (bf16[32,8,128]{2,1,0:T(8,128)(2,1)S(1)}, bf16[32,8,128]{2,1,0:T(8,128)(2,1)}, u32[]{:S(2)}) copy-start(bf16[32,8,128]{2,1,0:T(8,128)(2,1)} %refs_0_.1) | copy-start | bytes 196612
  5.8 8.0 %collective-permute-start.4 = (bf16[4,16,512]{2,1,0:T(8,128)(2,1)S(1)}, bf16[4,16,512]{2,1,0:T(8,128)(2,1)S(1)}, u32[]{:S(2)}, u32[]{:S(2)}) collective-permute-start(bf16[4,16,512]{2,1,0:T(8,128)(2,1)S(1)} %constant_dynamic-update-slice_fusion.refs_4_), channel_id=1, source_target_pairs={{2,4},{4,2},{6,8},{8,6},{10,12},{12,10},{14,16},{16,14},{18,20},{2... | collective-permute-start | bytes 196616 | tf_op jit(solution)/shard_map/ppermute | solution.py:535
  6.4 7.3 %collective-permute-start.3 = (bf16[4,16,512]{2,1,0:T(8,128)(2,1)S(1)}, bf16[4,16,512]{2,1,0:T(8,128)(2,1)S(1)}, u32[]{:S(2)}, u32[]{:S(2)}) collective-permute-start(bf16[4,16,512]{2,1,0:T(8,128)(2,1)S(1)} %constant_dynamic-update-slice_fusion.refs_4_), channel_id=1, source_target_pairs={{0,2},{2,0},{4,6},{6,4},{8,10},{10,8},{12,14},{14,12},{16,18},{18,... | collective-permute-start | bytes 196616 | tf_op jit(solution)/shard_map/ppermute | solution.py:535
  10.2 3.6 %collective-permute-start = (s32[2,2,1,32]{3,2,1,0:T(1,128)S(1)}, s32[2,2,1,32]{3,2,1,0:T(1,128)S(1)}, u32[]{:S(2)}, u32[]{:S(2)}) collective-permute-start(s32[2,2,1,32]{3,2,1,0:T(1,128)S(1)} %copy-done.2), channel_id=1, source_target_pairs={{0,1},{1,0},{2,3},{3,2},{4,5},{5,4},{6,7},{7,6},{8,9},{9,8},{10,11... | collective-permute-start | bytes 1544 | tf_op jit(solution)/shard_map/ppermute | solution.py:586
  11.4 0.7 %copy-start.3 = (f32[256]{0:T(256)S(1)}, f32[256]{0:T(256)}, u32[]{:S(2)}) copy-start(f32[256]{0:T(256)} %param.10) | copy-start | bytes 3076
  11.4 0.7 %copy-start.4 = (f32[32]{0:T(128)S(1)}, f32[32]{0:T(128)}, u32[]{:S(2)}) copy-start(f32[32]{0:T(128)} %param.9) | copy-start | bytes 388
  15.4 1.3 %collective-permute-start.5 = (bf16[80,128]{1,0:T(8,128)(2,1)S(1)}, bf16[80,128]{1,0:T(8,128)(2,1)S(1)}, u32[]{:S(2)}, u32[]{:S(2)}) collective-permute-start(bf16[80,128]{1,0:T(8,128)(2,1)S(1)} %get-tuple-element.30), channel_id=1, source_target_pairs={{0,2},{2,0},{4,6},{6,4},{8,10},{10,8},{12,14},{14,12},{16,18},{18,... | collective-permute-start | bytes 61448 | tf_op jit(solution)/shard_map/ppermute | solution.py:535
  15.5 1.2 %collective-permute-start.6 = (bf16[80,128]{1,0:T(8,128)(2,1)S(1)}, bf16[80,128]{1,0:T(8,128)(2,1)S(1)}, u32[]{:S(2)}, u32[]{:S(2)}) collective-permute-start(bf16[80,128]{1,0:T(8,128)(2,1)S(1)} %get-tuple-element.31), channel_id=1, source_target_pairs={{2,4},{4,2},{6,8},{8,6},{10,12},{12,10},{14,16},{16,14},{18,20},{2... | collective-permute-start | bytes 61448 | tf_op jit(solution)/shard_map/ppermute | solution.py:535
  17.9 5.3 %collective-permute-start.7 = (f32[16,128]{1,0:T(8,128)S(1)}, f32[16,128]{1,0:T(8,128)S(1)}, u32[]{:S(2)}, u32[]{:S(2)}) collective-permute-start(f32[16,128]{1,0:T(8,128)S(1)} %shard_map.95), channel_id=1, source_target_pairs={{0,2},{2,0},{4,6},{6,4},{8,10},{10,8},{12,14},{14,12},{16,18},{18,... | collective-permute-start | bytes 24584 | tf_op jit(solution)/shard_map/ppermute | solution.py:550
  23.2 5.1 %collective-permute-start.10 = (f32[16,128]{1,0:T(8,128)S(1)}, f32[16,128]{1,0:T(8,128)S(1)}, u32[]{:S(2)}, u32[]{:S(2)}) collective-permute-start(f32[16,128]{1,0:T(8,128)S(1)} %add.14), channel_id=1, source_target_pairs={{0,12},{2,14},{4,8},{6,10},{8,4},{10,6},{12,0},{14,2},{16,28},{18,... | collective-permute-start | bytes 24584 | tf_op jit(solution)/shard_map/ppermute | solution.py:550
  26.6 3.7 %collective-permute-start.9 = (f32[16,128]{1,0:T(8,128)S(1)}, f32[16,128]{1,0:T(8,128)S(1)}, u32[]{:S(2)}, u32[]{:S(2)}) collective-permute-start(f32[16,128]{1,0:T(8,128)S(1)} %add.14), channel_id=1, source_target_pairs={{0,8},{2,10},{4,12},{6,14},{8,0},{10,2},{12,4},{14,6},{16,24},{18,... | collective-permute-start | bytes 24584 | tf_op jit(solution)/shard_map/ppermute | solution.py:550
  27.1 3.7 %collective-permute-start.8 = (f32[16,128]{1,0:T(8,128)S(1)}, f32[16,128]{1,0:T(8,128)S(1)}, u32[]{:S(2)}, u32[]{:S(2)}) collective-permute-start(f32[16,128]{1,0:T(8,128)S(1)} %add.14), channel_id=1, source_target_pairs={{0,4},{2,6},{4,0},{6,2},{8,12},{10,14},{12,8},{14,10},{16,20},{18,... | collective-permute-start | bytes 24584 | tf_op jit(solution)/shard_map/ppermute | solution.py:550
  30.7 4.5 %collective-permute-start.11 = (f32[16,128]{1,0:T(8,128)S(1)}, f32[16,128]{1,0:T(8,128)S(1)}, u32[]{:S(2)}, u32[]{:S(2)}) collective-permute-start(f32[16,128]{1,0:T(8,128)S(1)} %add_add_fusion.own_ref), channel_id=1, source_target_pairs={{0,16},{2,18},{4,20},{6,22},{8,24},{10,26},{12,28},{14,30},{16,0},... | collective-permute-start | bytes 24584 | tf_op jit(solution)/shard_map/ppermute | solution.py:555

commit v5 on v4

--- a/solution.py
+++ b/solution.py
@@ -99,14 +99,42 @@
     return b if a is None else [x + y for x, y in zip(a, b)]
 
 
-def table_kernel(weight_ref, var_ref, offs_ref, shift_ref, *refs):
+def table_kernel(dims, weight_ref, var_ref, offs_ref, *refs):
+    nf, fl, nsc, T = dims
+    shift_refs, goal_refs, refs = refs[:nf], refs[nf : 2 * nf], refs[2 * nf :]
     fwd_ref, fwdl_ref, inv_ref, invl_ref, part_ref, wideh_ref, widel_ref = refs[:7]
-    big_ref, bigt_ref, small_ref, shift_out_ref, rows_ref = refs[7:]
-    shift_out_ref[...] = shift_ref[...]
+    big_ref, bigt_ref, small_ref, own_ref, side_ref, edge_ref, goal_ref, rows_ref, raw_ref = refs[7:]
+    odd = lax.rem(lax.axis_index("space"), 2)
+    fr = lax.axis_index("frame")
     offs = jnp.concatenate([offs_ref[...], jnp.zeros((1, LANES - 32), F32)], axis=1)
     small_ref[...] = jnp.concatenate(
         [jnp.exp(var_ref[...]), offs, jnp.zeros((5, LANES), F32)], axis=0
     )
+    for j in range(nf):
+        for l in range(fl):
+            for c in range(2):
+                row = shift_refs[j][l, c]
+                if T < LANES:
+                    row = jnp.concatenate([row, jnp.zeros((1, LANES - T), jnp.int32)], axis=1)
+                at = (j * fl + l) * 2 + c
+                own_ref[at : at + 1, :] = row
+    count = nf * fl * 2
+    words = own_ref[...].astype(F32)
+    if count % 16:
+        words = jnp.concatenate([words, jnp.zeros((16 - count % 16, LANES), F32)], axis=0)
+    lead = nf * nsc * 32
+    side_ref[lead:, :] = words.astype(BF16)
+    for j in range(nf):
+        at = pl.multiple_of(lax.rem(fr + j, nf) * (nsc * LANES), LANES)
+        for c in range(nsc):
+            cols = slice(c * LANES, (c + 1) * LANES)
+            raw_ref[...] = goal_refs[j][:, :, cols].astype(F32).reshape(256, LANES)
+            to = pl.ds(pl.multiple_of(at + c * LANES, LANES), LANES)
+            for r in range(8):
+                goal_ref[r, :, to] = raw_ref[pl.ds(r, 32, stride=8), :]
+            rows = slice((j * nsc + c) * 32, (j * nsc + c) * 32 + 32)
+            edge_ref[rows, :] = raw_ref[pl.ds(7 - 7 * odd, 32, stride=8), :].astype(BF16)
+            side_ref[rows, :] = raw_ref[pl.ds(7 * odd, 32, stride=8), :].astype(BF16)
 
     lane = lax.broadcasted_iota(jnp.int32, (TILE, LANES), 1)
     line = lax.broadcasted_iota(jnp.int32, (TILE, LANES), 0)
@@ -185,30 +213,36 @@
 
 
 def merge_kernel(dims, *refs):
-    nf, fl, G, T, nsc = dims
+    nf, fl, G, _, nsc = dims
     F = nf * fl
-    dx_refs, refs = refs[:nf], refs[nf:]
-    goal_refs, refs = refs[:nf], refs[nf:]
-    y_ref, yc_ref, yf_ref, var_ref = refs[:4]
-    fwd_ref, fwdl_ref, inv_ref, invl_ref = refs[4:8]
-    pack_ref, pc_ref, pf_ref, h_ref = refs[8:12]
-    x_ref, idx_ref, p_ref, q_ref, xs_ref, goal_ref = refs[12:18]
-    dy_refs, sems = refs[18 : 18 + nf], refs[18 + nf]
-    moves = [
-        pltpu.make_async_copy(src, dst, sems.at[j])
-        for j, (src, dst) in enumerate(zip(dx_refs, dy_refs))
-    ]
-    for move in moves:
-        move.start()
+    own_ref, side_ref, edge_ref, y_ref, yc_ref, yf_ref, var_ref = refs[:7]
+    fwd_ref, fwdl_ref, inv_ref, invl_ref = refs[7:11]
+    pack_ref, pc_ref, far_ref, h_ref = refs[11:15]
+    x_ref, idx_ref, p_ref, q_ref, xs_ref, words_ref, own_sm, far_sm, sems = refs[15:]
     s = lax.axis_index("space")
     fr = lax.axis_index("frame")
     odd = lax.rem(s, 2)
-
-    slots = ((y_ref, 1), (yc_ref, 2 - 2 * odd), (yf_ref, 2 * odd))
+    lead = nf * nsc * 32
+
+    words = side_ref[lead:, :].astype(F32).astype(jnp.int32)
+    words_ref[...] = words[: 2 * F]
+    moves = (
+        pltpu.make_async_copy(own_ref, own_sm, sems.at[0]),
+        pltpu.make_async_copy(words_ref, far_sm, sems.at[1]),
+    )
+    for move in moves:
+        move.start()
+
+    slots = (
+        (y_ref, 0, 2 - odd),
+        (yc_ref, 0, 3 - 3 * odd),
+        (yf_ref, 0, 1 + odd),
+        (yf_ref, F, 3 * odd),
+    )
 
     def fill(f, carry):
-        for ref, slot in slots:
-            rows = ref[f].astype(F32)
+        for ref, start, slot in slots:
+            rows = ref[start + f].astype(F32)
             for g in range(G):
                 block = rows[:, g * LANES : (g + 1) * LANES]
                 x_ref[f * G + g, pl.ds(pl.multiple_of(slot * TILE, TILE), TILE), :] = block
@@ -217,29 +251,16 @@
     lax.fori_loop(0, F, fill, 0, unroll=min(F, 4))
 
     spot = lax.broadcasted_iota(jnp.int32, (8, LANES), 1)
-    for j in range(nf):
-        for l in range(fl):
-            row = dx_refs[j][l, 1]
-            if T < LANES:
-                row = jnp.concatenate([row, jnp.zeros((1, LANES - T), jnp.int32)], axis=1)
-            row = jnp.broadcast_to(row, (8, LANES))
+    for which, ref in enumerate((own_ref, words_ref)):
+        for f in range(F):
+            row = jnp.broadcast_to(ref[2 * f + 1 : 2 * f + 2, :], (8, LANES))
             for g in range(G):
                 moved = jnp.take_along_axis(row, 8 * g + spot // TILE, axis=1)
-                idx_ref[(j * fl + l) * G + g] = (moved + spot) & (LANES - 1)
-
-    lead = G * 4
-    for j in range(nf):
-        for c in range(nsc):
-            cols = slice(c * LANES, (c + 1) * LANES)
-            goal_ref[j * nsc + c] = goal_refs[j][:, :, cols].astype(F32).reshape(256, LANES)
-    for k in range(nf * nsc):
-        rows = slice(lead + k * 32, lead + k * 32 + 32)
-        pc_ref[rows, :] = goal_ref[k, pl.ds(7 - 7 * odd, 32, stride=8), :].astype(BF16)
-        pf_ref[rows, :] = goal_ref[k, pl.ds(7 * odd, 32, stride=8), :].astype(BF16)
+                idx_ref[which, f * G + g] = (moved + spot) & (LANES - 1)
+    pc_ref[4 * G :, :] = edge_ref[...]
 
     lane = lax.broadcasted_iota(jnp.int32, (TILE, LANES), 1)
     kind = (lane // TILE) % 4
-
     per = 16 // G
     chunks = F * G // 16
     rows_out = max(G, 8)
@@ -250,16 +271,6 @@
         if nf == 2:
             return f
         return lax.rem(f // fl + nf - fr, nf) * fl + f % fl
-
-    def row_shift(f, t):
-        if isinstance(f, int):
-            return dy_refs[f // fl][f % fl, 0, 0, t]
-        j = lax.div(f, fl)
-        l = lax.rem(f, fl)
-        value = dy_refs[0][l, 0, 0, t]
-        for k in range(1, nf):
-            value = jnp.where(j == k, dy_refs[k][l, 0, 0, t], value)
-        return value
 
     first = lax.rem(nf - fr, nf) * fl
     log_var = var_ref[...]
@@ -269,7 +280,7 @@
         row = jnp.take_along_axis(row, (k % 8) * TILE + spot % TILE, axis=1)
         variances.append(jnp.concatenate([row, row], axis=0))
 
-    def chunk_step(c, carry):
+    def tile_row(which, row0, dy_ref, c, carry):
         sums = carry[0] if carry is not None else None
         blocks = []
         for q in range(16):
@@ -279,10 +290,10 @@
             def load(t, group):
                 if group < 0 or group >= G:
                     return zero
-                start = TILE + row_shift(f, 8 * g + t)
+                start = row0 + dy_ref[2 * f, 8 * g + t]
                 return x_ref[f * G + group, pl.ds(start, TILE), :]
 
-            idx = idx_ref[f * G + g]
+            idx = idx_ref[which, f * G + g]
             idx = jnp.concatenate([idx, idx], axis=0)
             mixes = (
                 jnp.where(
@@ -306,20 +317,18 @@
                     jnp.where(kind == 2, moved[2], moved[3]),
                 )
             )
-        part = [tree(blocks[g::G]) for g in range(G)]
-        sums = add_lists(sums, part)
-        base = [x_ref[first * G + g, TILE : 2 * TILE, :] for g in range(G)]
+        base = [x_ref[first * G + g, pl.ds(pl.multiple_of(row0, TILE), TILE), :] for g in range(G)]
         both = jnp.concatenate(blocks + base, axis=0).astype(BF16)
         pq = dot(jnp.concatenate([both, both], axis=1), fwd_ref[...]) + dot(both, fwdl_ref[...])
         for q in range(16):
             rows = slice(q * TILE, (q + 1) * TILE)
             ref_rows = slice(256 + (q % G) * TILE, 256 + (q % G + 1) * TILE)
             diff = pq[ref_rows] - pq[rows]
-            p_ref[rows, :] = diff[:, :LANES]
-            q_ref[rows, :] = -diff[:, LANES:]
+            p_ref[which, rows, :] = diff[:, :LANES]
+            q_ref[which, rows, :] = -diff[:, LANES:]
         re, im = fft(
-            [p_ref[pl.ds(n, 16, stride=16), :] for n in range(16)],
-            [q_ref[pl.ds(n, 16, stride=16), :] for n in range(16)],
+            [p_ref[which, pl.ds(n, 16, stride=16), :] for n in range(16)],
+            [q_ref[which, pl.ds(n, 16, stride=16), :] for n in range(16)],
         )
         out = [[], [], [], []]
         for k in range(16):
@@ -327,53 +336,69 @@
             weight = energy / (energy + variances[k])
             wr = weight * re[k]
             wi = weight * im[k]
-            rest = 1.0 - weight
-            for store, val in zip(out, (wr, wi, wr * rest, wi * rest)):
+            vals = (wr, wi)
+            if which == 0:
+                rest = 1.0 - weight
+                vals = (wr, wi, wr * rest, wi * rest)
+            for store, val in zip(out, vals):
                 if fold == 2:
                     val = val[:8] + val[8:]
                 store.append(val)
         flat = out[0] + out[1] + out[2] + out[3]
-        return sums, add_lists(carry[1] if carry is not None else None, flat)
-
-    for move in moves:
-        move.wait()
-    carry = chunk_step(0, None)
-    if chunks > 1:
-        carry = lax.fori_loop(1, chunks, chunk_step, carry)
-    sums, flat = carry
+        return sums_of(sums, blocks), add_lists(carry[1] if carry is not None else None, flat)
+
+    def sums_of(sums, blocks):
+        return add_lists(sums, [tree(blocks[g::G]) for g in range(G)])
+
+    def whole_row(which, row0, dy_ref):
+        step = functools.partial(tile_row, which, row0, dy_ref)
+        carry = step(0, None)
+        if chunks > 1:
+            carry = lax.fori_loop(1, chunks, step, carry)
+        return carry
+
+    moves[0].wait()
+    sums, flat = whole_row(0, (2 - odd) * TILE, own_sm)
     for k in range(32):
         h_ref[k * rows_out : (k + 1) * rows_out, :] = flat[32 + k]
+    moves[1].wait()
+    far_sums, far_flat = whole_row(1, (1 + odd) * TILE, far_sm)
 
     vi, ur = fft(flat[16:32], flat[:16])
-    uv = jnp.concatenate(
-        [jnp.concatenate(ur, axis=0), jnp.concatenate(vi, axis=0)], axis=1
-    )
-    m = 16 * rows_out
+    far_vi, far_ur = fft(far_flat[16:32], far_flat[:16])
+    at_odd = odd == 1
+    ur += [jnp.where(at_odd, far_ur[k], far_ur[12 + k]) for k in range(4)]
+    vi += [jnp.where(at_odd, far_vi[k], far_vi[12 + k]) for k in range(4)]
+    uv = jnp.concatenate([jnp.concatenate(ur, axis=0), jnp.concatenate(vi, axis=0)], axis=1)
+    m = 20 * rows_out
     terms = split(uv, 3)
     wide = dot(jnp.concatenate(terms, axis=0), inv_ref[...])
     pix = wide[:m, :LANES] + (wide[m : 2 * m, :LANES] + wide[:m, LANES:])
     pix = pix + (wide[2 * m :, :LANES] + wide[m : 2 * m, LANES:] + dot(terms[0], invl_ref[...]))
     xs_ref[...] = pix
+    far_rows = []
     for g in range(G):
         val = xs_ref[pl.ds(g, 16, stride=rows_out), :]
+        far = xs_ref[pl.ds(16 * rows_out + g, 4, stride=rows_out), :]
         for other in range(g + G, rows_out, G):
             val = val + xs_ref[pl.ds(other, 16, stride=rows_out), :]
-        val = (sums[g] + val / 256.0) / F
-        pack_ref[g] = val
+            far = far + xs_ref[pl.ds(16 * rows_out + other, 4, stride=rows_out), :]
+        pack_ref[g] = (sums[g] + val / 256.0) / F
+        far_sum = jnp.where(at_odd, far_sums[g][0:4], far_sums[g][12:16])
+        far_rows.append((far_sum + far / 256.0) / F)
+    far_ref[...] = jnp.concatenate(far_rows, axis=0)
     low = jnp.concatenate([pack_ref[g, 0:4, :] for g in range(G)], axis=0)
     high = jnp.concatenate([pack_ref[g, 12:16, :] for g in range(G)], axis=0)
-    pc_ref[0:lead, :] = jnp.where(odd == 1, low, high).astype(BF16)
-    pf_ref[0:lead, :] = jnp.where(odd == 1, high, low).astype(BF16)
-
-
-def demosaic_kernel(dims, pack_ref, pc_ref, pf_ref, h_ref, *refs):
+    pc_ref[0 : 4 * G, :] = jnp.where(at_odd, low, high).astype(BF16)
+
+
+def demosaic_kernel(dims, pack_ref, pc_ref, far_ref, side_ref, goals_ref, h_ref, *refs):
     nf, fl, G, nsc, n_space, inv_pixels = dims
     F = nf * fl
     W = G * LANES
     half = W // 2
-    goal_refs = refs[:nf]
-    big_ref, bigt_ref, offs_ref, part_ref, wideh_ref, widel_ref = refs[nf : nf + 6]
-    out_ref, goal_ref, raw_ref, mm_ref, p_ref, q_ref, ns_ref = refs[nf + 6 :]
+    big_ref, bigt_ref, offs_ref, part_ref, wideh_ref, widel_ref = refs[:6]
+    out_ref, goal_ref, mm_ref, p_ref, q_ref, ns_ref = refs[6:]
     s = lax.axis_index("space")
     fr = lax.axis_index("frame")
     odd = lax.rem(s, 2)
@@ -383,19 +408,13 @@
     for j in range(nf):
         at = pl.multiple_of(lax.rem(fr + j, nf) * (nsc * LANES), LANES)
         for c in range(nsc):
-            cols = slice(c * LANES, (c + 1) * LANES)
-            raw_ref[...] = goal_refs[j][:, :, cols].astype(F32).reshape(256, LANES)
+            first = (j * nsc + c) * 32
             to = pl.ds(pl.multiple_of(at + c * LANES, LANES), LANES)
-            for r in range(8):
-                goal_ref[r + 1, :, to] = raw_ref[pl.ds(r, 32, stride=8), :]
-        for ref, row in ((pc_ref, 9 - 9 * odd), (pf_ref, 9 * odd)):
-            for c in range(nsc):
-                first = lead + (j * nsc + c) * 32
-                val = ref[first : first + 32, :].astype(F32)
-                goal_ref[row, :, pl.ds(pl.multiple_of(at + c * LANES, LANES), LANES)] = val
+            goal_ref[1 - odd, :, to] = pc_ref[lead + first : lead + first + 32, :].astype(F32)
+            goal_ref[odd, :, to] = side_ref[first : first + 32, :].astype(F32)
 
     near = pc_ref[0:lead, :].astype(F32)
-    far = pf_ref[0:lead, :].astype(F32)
+    far = far_ref[...]
     low = jnp.where(odd == 1, near, far)
     high = jnp.where(odd == 1, far, near)
     for g in range(G):
@@ -430,7 +449,8 @@
     for sy in range(10):
         v = preact[sy * 32 : sy * 32 + 32] + offs
         sig = jax.nn.sigmoid(v)
-        slope = (v * sig - goal_ref[sy]) * inv_pixels * (sig * (1.0 + v * (1.0 - sig)))
+        goal = goal_ref[0] if sy == 0 else goal_ref[1] if sy == 9 else goals_ref[sy - 1]
+        slope = (v * sig - goal) * inv_pixels * (sig * (1.0 + v * (1.0 - sig)))
         if sy == 0:
             slope = jnp.where(s == 0, 0.0, slope)
         elif sy == 9:
@@ -595,12 +615,15 @@
     y = lax.optimization_barrier(y)
     for j in range(1, nf):
         y = lax.dynamic_update_slice(y, raws[j], (j * fl, 0, 0))
-    yf = involution(y, n_space, 1, 1)
     yc = involution(y, n_space, 1, 0)
+    pair = jnp.concatenate([y, yc], axis=0)
+    yf = involution(pair, n_space, 1, 1)
+
     shape = jax.ShapeDtypeStruct
-    *tables, big, bigt, small, own_shifts = call(
-        table_kernel,
-        [weight, log_var.reshape(2, LANES), offset.reshape(1, channels), shifts],
+    side_rows = nf * nsc * channels + -(-2 * F // 16) * 16
+    *tables, big, bigt, small, own_rows, side, edge, site_goals = call(
+        functools.partial(table_kernel, (nf, fl, nsc, T)),
+        [weight, log_var.reshape(2, LANES), offset.reshape(1, channels), *shift_parts, *goals],
         [
             shape((256, 256), BF16),
             shape((128, 256), BF16),
@@ -612,42 +635,43 @@
             shape((320, 256), BF16),
             shape((96, 320), BF16),
             shape((8, LANES), F32),
-            shape(shifts.shape, jnp.int32),
+            shape((2 * F, LANES), jnp.int32),
+            shape((side_rows, LANES), BF16),
+            shape((nf * nsc * channels, LANES), BF16),
+            shape((8, channels, W // 2), F32),
         ],
-        [pltpu.VMEM((6, 40, LANES), F32)],
-    )
-    shift_parts[0] = own_shifts
-
-    side = 4 * G + nf * nsc * channels
-    pack, pc, pf, moments = call(
+        [pltpu.VMEM((6, 40, LANES), F32), pltpu.VMEM((256, LANES), F32)],
+    )
+    side = involution(side, n_space, 1, 1)
+
+    pack, pc, far, moments = call(
         functools.partial(merge_kernel, (nf, fl, G, T, nsc)),
-        [*shift_parts, *goals, y, yc, yf, small, *tables[:4]],
+        [own_rows, side, edge, y, yc, yf, small, *tables[:4]],
         [
             shape((G, TILE, LANES), F32),
-            shape((side, LANES), BF16),
-            shape((side, LANES), BF16),
+            shape((4 * G + nf * nsc * channels, LANES), BF16),
+            shape((4 * G, LANES), F32),
             shape((32 * rows_out, LANES), F32),
         ],
         [
-            pltpu.VMEM((F * G, 3 * TILE, LANES), F32),
-            pltpu.VMEM((F * G, 8, LANES), jnp.int32),
-            pltpu.VMEM((256, LANES), F32),
-            pltpu.VMEM((256, LANES), F32),
-            pltpu.VMEM((16 * rows_out, LANES), F32),
-            pltpu.VMEM((nf * nsc, 256, LANES), F32),
-            *[pltpu.SMEM(shifts.shape, jnp.int32)] * nf,
-            pltpu.SemaphoreType.DMA((nf,)),
+            pltpu.VMEM((F * G, 4 * TILE, LANES), F32),
+            pltpu.VMEM((2, F * G, 8, LANES), jnp.int32),
+            pltpu.VMEM((2, 256, LANES), F32),
+            pltpu.VMEM((2, 256, LANES), F32),
+            pltpu.VMEM((20 * rows_out, LANES), F32),
+            pltpu.VMEM((2 * F, LANES), jnp.int32),
+            pltpu.SMEM((2 * F, LANES), jnp.int32),
+            pltpu.SMEM((2 * F, LANES), jnp.int32),
+            pltpu.SemaphoreType.DMA((2,)),
         ],
     )
-    pf = involution(pf, n_space, 1, 1)
     pc = involution(pc, n_space, 1, 0)
     (partial,) = call(
         functools.partial(demosaic_kernel, (nf, fl, G, nsc, n_space, inv_pixels)),
-        [pack, pc, pf, moments, *goals, big, bigt, small, *tables[4:]],
+        [pack, pc, far, side, site_goals, moments, big, bigt, small, *tables[4:]],
         [shape((16, LANES), F32)],
         [
-            pltpu.VMEM((10, channels, W // 2), F32),
-            pltpu.VMEM((256, LANES), F32),
+            pltpu.VMEM((2, channels, W // 2), F32),
             pltpu.VMEM((G, 24, LANES), F32),
             pltpu.VMEM((rows_out * TILE, LANES), F32),
             pltpu.VMEM((rows_out * TILE, LANES), F32),

time: 36.3 us -> 40.1 us (1.10)
  waiting for transfers between devices: 9.41 us -> 12.3 us
  Pallas kernels: 3.97 us -> 4.56 us
    ppermute x4, starting transfers between devices: 8.46 us -> 5.65 us  [sum_space(): got.append(lax.ppermute(value, 'space', [(i, i ^ m) for i in range(count)]))]
    ppermute x3, waiting for transfers between devices: 2.58 us -> 4.81 us  [from_frame(): return lax.ppermute(value, 'frame', [(i, (i - j) % nf) for i in range(nf)])]
    ppermute x4, starting transfers between devices: 5.13 us -> 7.33 us  [involution(): return lax.ppermute(value, 'space', pairs)]
    ppermute x4, waiting for transfers between devices: 0.51 us -> 2.09 us  [involution(): return lax.ppermute(value, 'space', pairs)]
    ppermute x4, waiting for transfers between devices: 4.36 us -> 3.41 us  [sum_space(): got.append(lax.ppermute(value, 'space', [(i, i ^ m) for i in range(count)]))]
    ppermute x3, starting transfers between devices: 4.33 us -> 5.2 us  [from_frame(): return lax.ppermute(value, 'frame', [(i, (i - j) % nf) for i in range(nf)])]
    pallas_call x4, Pallas kernels: 3.97 us -> 4.56 us  [call(): pl.pallas_call(body, out_shape=tuple(outs), in_specs=[vm] * len(args), ou...]
  transfers between devices with their start and end apart: 12 -> 12, of which waited for: 8 -> 9; matrix products, arithmetic and copies ran while one was open for 2% -> 2% of each run, Pallas kernels for 1% -> 1%
where the time goes in v5:
time: 40.1 us; the launch traced here: 39.8 us
  starting transfers between devices  20.8 us (52%)
  waiting for transfers between devices  12.3 us (31%)
  Pallas kernels  4.56 us (11%)
  local copies, waits for them, and re-layouts  1.49 us (4%)
  between operations  0.72 us (2%)
    ppermute x4, starting transfers between devices, involution(): return lax.ppermute(value, 'space', pairs)  7.33 us
    ppermute x4, starting transfers between devices, sum_space(): got.append(lax.ppermute(value, 'space', [(i, i ^ m) for i in range(count)]))  5.65 us
    ppermute x3, starting transfers between devices, from_frame(): return lax.ppermute(value, 'frame', [(i, (i - j) % nf) for i in range(nf)])  5.2 us
    ppermute x3, waiting for transfers between devices, from_frame(): return lax.ppermute(value, 'frame', [(i, (i - j) % nf) for i in range(nf)])  4.81 us
    pallas_call x4, Pallas kernels, call(): pl.pallas_call(body, out_shape=tuple(outs), in_specs=[vm] * len(args), ou...  4.56 us
    ppermute x4, waiting for transfers between devices, sum_space(): got.append(lax.ppermute(value, 'space', [(i, i ^ m) for i in range(count)]))  3.41 us
    ppermute x1, starting transfers between devices, sum_space(): got = lax.ppermute(value, 'space', [(i, i ^ mask) for i in range(count)])  2.58 us
    ppermute x4, waiting for transfers between devices, involution(): return lax.ppermute(value, 'space', pairs)  2.09 us
  transfers between devices with their start and end apart: 12, of which 9 were waited for; matrix products, arithmetic and copies ran while one was open for 2% of the time, Pallas kernels for 1%

profile of v5, /device:TPU:0, one launch (start us, length us, event | category | flops | bytes accessed | tf_op | source)
XLA Modules:
  0.0 39.8 jit_solution(14209613378881966200)
XLA Ops:
  0.6 3.0 %collective-permute-start.3 = (bf16[2,16,512]{2,1,0:T(8,128)(2,1)}, bf16[2,16,512]{2,1,0:T(8,128)(2,1)S(1)}, u32[]{:S(2)}, u32[]{:S(2)}) collective-permute-start(bf16[2,16,512]{2,1,0:T(8,128)(2,1)} %param.6), channel_id=1, source_target_pairs={{0,1},{1,0},{2,3},{3,2},{4,5},{5,4},{6,7},{7,6},{8,9},{9,8},{10,11... | collective-permute-start | bytes 98312 | tf_op jit(solution)/shard_map/ppermute | solution.py:606
  3.7 0.8 %pad.4 = bf16[4,16,512]{2,1,0:T(8,128)(2,1)S(1)} pad(bf16[2,16,512]{2,1,0:T(8,128)(2,1)} %param.6, bf16[]{:T(256)} %constant.1.clone.1), padding=0_2x0_0x0_0 | pad | bytes 98306 | tf_op jit(solution)/shard_map/jit(_pad)/pad | solution.py:614
  4.5 1.3 %collective-permute-done.3 = bf16[2,16,512]{2,1,0:T(8,128)(2,1)S(1)} collective-permute-done((bf16[2,16,512]{2,1,0:T(8,128)(2,1)}, bf16[2,16,512]{2,1,0:T(8,128)(2,1)S(1)}, u32[]{:S(2)}, u32[]{:S(2)}) %collective-permute-start.3) | collective-permute-done | bytes 32800 | tf_op jit(solution)/shard_map/ppermute | solution.py:606
  5.8 0.1 collective-permute-start.4
  5.9 1.2 %collective-permute-done.4.refs_4_ = bf16[4,16,512]{2,1,0:T(8,128)(2,1)S(1)} collective-permute-done((bf16[4,16,512]{2,1,0:T(8,128)(2,1)S(1)}, bf16[4,16,512]{2,1,0:T(8,128)(2,1)S(1)}, u32[]{:S(2)}, u32[]{:S(2)}) %collective-permute-start.4) | collective-permute-done | bytes 65568 | tf_op jit(solution)/shard_map/ppermute | solution.py:555
  7.1 0.7 %collective-permute-start.5 = (bf16[8,16,512]{2,1,0:T(8,128)(2,1)S(1)}, bf16[8,16,512]{2,1,0:T(8,128)(2,1)S(1)}, u32[]{:S(2)}, u32[]{:S(2)}) collective-permute-start(bf16[8,16,512]{2,1,0:T(8,128)(2,1)S(1)} %pad_maximum_fusion), channel_id=1, source_target_pairs={{2,4},{4,2},{6,8},{8,6},{10,12},{12,10},{14,16},{16,14},{18,20},{2... | collective-permute-start | bytes 393224 | tf_op jit(solution)/shard_map/ppermute | solution.py:555
  7.8 0.0 copy-done
  7.8 2.1 %collective-permute-start.1 = (bf16[32,8,128]{2,1,0:T(8,128)(2,1)S(1)}, bf16[32,8,128]{2,1,0:T(8,128)(2,1)S(1)}, u32[]{:S(2)}, u32[]{:S(2)}) collective-permute-start(bf16[32,8,128]{2,1,0:T(8,128)(2,1)S(1)} %copy-done), channel_id=1, source_target_pairs={{0,1},{1,0},{2,3},{3,2},{4,5},{5,4},{6,7},{7,6},{8,9},{9,8},{10,11... | collective-permute-start | bytes 196616 | tf_op jit(solution)/shard_map/ppermute | solution.py:606
  9.9 0.0 copy-done.2
  9.9 0.1 collective-permute-start
  10.0 3.5 %collective-permute-done.refs_1_ = s32[2,2,1,32]{3,2,1,0:T(1,128)S(1)} collective-permute-done((s32[2,2,1,32]{3,2,1,0:T(1,128)S(1)}, s32[2,2,1,32]{3,2,1,0:T(1,128)S(1)}, u32[]{:S(2)}, u32[]{:S(2)}) %collective-permute-start) | collective-permute-done | bytes 544 | tf_op jit(solution)/shard_map/ppermute | solution.py:606
  13.5 0.0 collective-permute-done.1.refs_3_
  13.5 0.7 %copy-done.3 = f32[256]{0:T(256)S(1)} copy-done((f32[256]{0:T(256)S(1)}, f32[256]{0:T(256)}, u32[]{:S(2)}) %copy-start.3) | copy-done | bytes 1048
  14.2 0.4 shard_map.93
  14.6 0.7 %collective-permute-start.2 = (bf16[80,128]{1,0:T(8,128)(2,1)S(1)}, bf16[80,128]{1,0:T(8,128)(2,1)S(1)}, u32[]{:S(2)}, u32[]{:S(2)}) collective-permute-start(bf16[80,128]{1,0:T(8,128)(2,1)S(1)} %get-tuple-element.27), channel_id=1, source_target_pairs={{2,4},{4,2},{6,8},{8,6},{10,12},{12,10},{14,16},{16,14},{18,20},{2... | collective-permute-start | bytes 61448 | tf_op jit(solution)/shard_map/ppermute | solution.py:555
  15.2 0.0 collective-permute-done.2.refs_1_.side_ref
  15.2 0.0 collective-permute-done.5.refs_5_
  15.3 2.1 %shard_map.94 = (f32[4,16,128]{2,1,0:T(8,128)S(1)}, bf16[80,128]{1,0:T(8,128)(2,1)S(1)}, f32[16,128]{1,0:T(8,128)S(1)}, f32[256,128]{1,0:T(8,128)S(1)}) custom-call(s32[8,128]{1,0:T(8,128)S(1)} %get-tuple-element.26.refs_0_, bf16[80,128]{1,0:T(8,128)(2,1)S(1)} %collective-permute-done.2.refs_1_.side_ref, bf16[64,128]{1,0:T(8,128)(2,1)S(1)} %get-tuple-element.28.refs_2_, ...), custom_call_target="tpu_custom_call" | custom-call | tf_op jit(solution)/shard_map/pallas_call | solution.py:583
  17.4 5.9 %collective-permute-start.6 = (bf16[80,128]{1,0:T(8,128)(2,1)S(1)}, bf16[80,128]{1,0:T(8,128)(2,1)S(1)}, u32[]{:S(2)}, u32[]{:S(2)}) collective-permute-start(bf16[80,128]{1,0:T(8,128)(2,1)S(1)} %get-tuple-element.35), channel_id=1, source_target_pairs={{0,2},{2,0},{4,6},{6,4},{8,10},{10,8},{12,14},{14,12},{16,18},{18,... | collective-permute-start | bytes 61448 | tf_op jit(solution)/shard_map/ppermute | solution.py:555
  23.3 0.8 %collective-permute-done.6.pc_ref = bf16[80,128]{1,0:T(8,128)(2,1)S(1)} collective-permute-done((bf16[80,128]{1,0:T(8,128)(2,1)S(1)}, bf16[80,128]{1,0:T(8,128)(2,1)S(1)}, u32[]{:S(2)}, u32[]{:S(2)}) %collective-permute-start.6) | collective-permute-done | bytes 20512 | tf_op jit(solution)/shard_map/ppermute | solution.py:555
  24.2 1.3 %shard_map.95 = f32[16,128]{1,0:T(8,128)S(1)} custom-call(f32[4,16,128]{2,1,0:T(8,128)S(1)} %get-tuple-element.34.pack_ref, bf16[80,128]{1,0:T(8,128)(2,1)S(1)} %collective-permute-done.6.pc_ref, f32[16,128]{1,0:T(8,128)S(1)} %get-tuple-element.36.far_ref, bf16[80,128]{1,0:T(8,128)(2,1)S(1)} %collective-permute-done.2.refs_1_.side_ref, ...), custom_call_target="tpu_custom_call" | custom-call | tf_op jit(solution)/shard_map/pallas_call | solution.py:583
  25.4 0.4 %collective-permute-start.7 = (f32[16,128]{1,0:T(8,128)S(1)}, f32[16,128]{1,0:T(8,128)S(1)}, u32[]{:S(2)}, u32[]{:S(2)}) collective-permute-start(f32[16,128]{1,0:T(8,128)S(1)} %shard_map.95), channel_id=1, source_target_pairs={{0,2},{2,0},{4,6},{6,4},{8,10},{10,8},{12,14},{14,12},{16,18},{18,... | collective-permute-start | bytes 24584 | tf_op jit(solution)/shard_map/ppermute | solution.py:570
  25.8 0.8 %collective-permute-done.7 = f32[16,128]{1,0:T(8,128)S(1)} collective-permute-done((f32[16,128]{1,0:T(8,128)S(1)}, f32[16,128]{1,0:T(8,128)S(1)}, u32[]{:S(2)}, u32[]{:S(2)}) %collective-permute-start.7) | collective-permute-done | bytes 8224 | tf_op jit(solution)/shard_map/ppermute | solution.py:570
  26.7 3.7 %collective-permute-start.10 = (f32[16,128]{1,0:T(8,128)S(1)}, f32[16,128]{1,0:T(8,128)S(1)}, u32[]{:S(2)}, u32[]{:S(2)}) collective-permute-start(f32[16,128]{1,0:T(8,128)S(1)} %add.14), channel_id=1, source_target_pairs={{0,12},{2,14},{4,8},{6,10},{8,4},{10,6},{12,0},{14,2},{16,28},{18,... | collective-permute-start | bytes 24584 | tf_op jit(solution)/shard_map/ppermute | solution.py:570
  30.4 0.4 %collective-permute-start.9 = (f32[16,128]{1,0:T(8,128)S(1)}, f32[16,128]{1,0:T(8,128)S(1)}, u32[]{:S(2)}, u32[]{:S(2)}) collective-permute-start(f32[16,128]{1,0:T(8,128)S(1)} %add.14), channel_id=1, source_target_pairs={{0,8},{2,10},{4,12},{6,14},{8,0},{10,2},{12,4},{14,6},{16,24},{18,... | collective-permute-start | bytes 24584 | tf_op jit(solution)/shard_map/ppermute | solution.py:570
  30.8 1.1 %collective-permute-start.8 = (f32[16,128]{1,0:T(8,128)S(1)}, f32[16,128]{1,0:T(8,128)S(1)}, u32[]{:S(2)}, u32[]{:S(2)}) collective-permute-start(f32[16,128]{1,0:T(8,128)S(1)} %add.14), channel_id=1, source_target_pairs={{0,4},{2,6},{4,0},{6,2},{8,12},{10,14},{12,8},{14,10},{16,20},{18,... | collective-permute-start | bytes 24584 | tf_op jit(solution)/shard_map/ppermute | solution.py:570
  31.9 0.1 collective-permute-done.10
  32.0 2.0 %collective-permute-done.9 = f32[16,128]{1,0:T(8,128)S(1)} collective-permute-done((f32[16,128]{1,0:T(8,128)S(1)}, f32[16,128]{1,0:T(8,128)S(1)}, u32[]{:S(2)}, u32[]{:S(2)}) %collective-permute-start.9) | collective-permute-done | bytes 8224 | tf_op jit(solution)/shard_map/ppermute | solution.py:570
  34.0 0.4 %collective-permute-done.8 = f32[16,128]{1,0:T(8,128)S(1)} collective-permute-done((f32[16,128]{1,0:T(8,128)S(1)}, f32[16,128]{1,0:T(8,128)S(1)}, u32[]{:S(2)}, u32[]{:S(2)}) %collective-permute-start.8) | collective-permute-done | bytes 8224 | tf_op jit(solution)/shard_map/ppermute | solution.py:570
  34.5 2.6 %collective-permute-start.11 = (f32[16,128]{1,0:T(8,128)S(1)}, f32[16,128]{1,0:T(8,128)S(1)}, u32[]{:S(2)}, u32[]{:S(2)}) collective-permute-start(f32[16,128]{1,0:T(8,128)S(1)} %add_add_fusion.own_ref), channel_id=1, source_target_pairs={{0,16},{2,18},{4,20},{6,22},{8,24},{10,26},{12,28},{14,30},{16,0},... | collective-permute-start | bytes 24584 | tf_op jit(solution)/shard_map/ppermute | solution.py:575
  37.1 2.0 %collective-permute-done.11.got_ref = f32[16,128]{1,0:T(8,128)S(1)} collective-permute-done((f32[16,128]{1,0:T(8,128)S(1)}, f32[16,128]{1,0:T(8,128)S(1)}, u32[]{:S(2)}, u32[]{:S(2)}) %collective-permute-start.11) | collective-permute-done | bytes 8224 | tf_op jit(solution)/shard_map/ppermute | solution.py:575
  39.1 0.8 %shard_map.96 = (f32[16,256]{1,0:T(8,128)}, f32[32,36]{1,0:T(8,128)}, f32[1,32]{1,0:T(1,128)}, f32[2,128]{1,0:T(2,128)}) custom-call(f32[4,16,128]{2,1,0:T(8,128)S(1)} %get-tuple-element.34.pack_ref, f32[16,128]{1,0:T(8,128)S(1)} %add_add_fusion.own_ref, f32[16,128]{1,0:T(8,128)S(1)} %collective-permute-done.11.got_ref), custom_call_target="tpu_custom_call" | custom-call | tf_op jit(solution)/shard_map/pallas_call | solution.py:583
  (11 shorter events, 0.0 us)
Async XLA Ops:
  0.6 5.1 %collective-permute-start.3 = (bf16[2,16,512]{2,1,0:T(8,128)(2,1)}, bf16[2,16,512]{2,1,0:T(8,128)(2,1)S(1)}, u32[]{:S(2)}, u32[]{:S(2)}) collective-permute-start(bf16[2,16,512]{2,1,0:T(8,128)(2,1)} %param.6), channel_id=1, source_target_pairs={{0,1},{1,0},{2,3},{3,2},{4,5},{5,4},{6,7},{7,6},{8,9},{9,8},{10,11... | collective-permute-start | bytes 98312 | tf_op jit(solution)/shard_map/ppermute | solution.py:606
  5.8 2.0 %copy-start = (bf16[32,8,128]{2,1,0:T(8,128)(2,1)S(1)}, bf16[32,8,128]{2,1,0:T(8,128)(2,1)}, u32[]{:S(2)}) copy-start(bf16[32,8,128]{2,1,0:T(8,128)(2,1)} %refs_2_.1) | copy-start | bytes 196612
  5.8 4.1 %copy-start.2 = (s32[2,2,1,32]{3,2,1,0:T(1,128)S(1)}, s32[2,2,1,32]{3,2,1,0:T(1,128)}, u32[]{:S(2)}) copy-start(s32[2,2,1,32]{3,2,1,0:T(1,128)} %refs_0_.1) | copy-start | bytes 1540
  5.8 1.3 %collective-permute-start.4 = (bf16[4,16,512]{2,1,0:T(8,128)(2,1)S(1)}, bf16[4,16,512]{2,1,0:T(8,128)(2,1)S(1)}, u32[]{:S(2)}, u32[]{:S(2)}) collective-permute-start(bf16[4,16,512]{2,1,0:T(8,128)(2,1)S(1)} %constant_dynamic-update-slice_fusion.refs_3_), channel_id=1, source_target_pairs={{0,2},{2,0},{4,6},{6,4},{8,10},{10,8},{12,14},{14,12},{16,18},{18,... | collective-permute-start | bytes 196616 | tf_op jit(solution)/shard_map/ppermute | solution.py:555
  7.1 6.4 %copy-start.1 = (bf16[32,36]{1,0:T(8,128)(2,1)S(1)}, bf16[32,36]{1,0:T(8,128)(2,1)}, u32[]{:S(2)}) copy-start(bf16[32,36]{1,0:T(8,128)(2,1)} %weight_ref.1) | copy-start | bytes 6916
  7.1 8.1 %collective-permute-start.5 = (bf16[8,16,512]{2,1,0:T(8,128)(2,1)S(1)}, bf16[8,16,512]{2,1,0:T(8,128)(2,1)S(1)}, u32[]{:S(2)}, u32[]{:S(2)}) collective-permute-start(bf16[8,16,512]{2,1,0:T(8,128)(2,1)S(1)} %pad_maximum_fusion), channel_id=1, source_target_pairs={{2,4},{4,2},{6,8},{8,6},{10,12},{12,10},{14,16},{16,14},{18,20},{2... | collective-permute-start | bytes 393224 | tf_op jit(solution)/shard_map/ppermute | solution.py:555
  7.8 5.7 %collective-permute-start.1 = (bf16[32,8,128]{2,1,0:T(8,128)(2,1)S(1)}, bf16[32,8,128]{2,1,0:T(8,128)(2,1)S(1)}, u32[]{:S(2)}, u32[]{:S(2)}) collective-permute-start(bf16[32,8,128]{2,1,0:T(8,128)(2,1)S(1)} %copy-done), channel_id=1, source_target_pairs={{0,1},{1,0},{2,3},{3,2},{4,5},{5,4},{6,7},{7,6},{8,9},{9,8},{10,11... | collective-permute-start | bytes 196616 | tf_op jit(solution)/shard_map/ppermute | solution.py:606
  9.9 3.6 %collective-permute-start = (s32[2,2,1,32]{3,2,1,0:T(1,128)S(1)}, s32[2,2,1,32]{3,2,1,0:T(1,128)S(1)}, u32[]{:S(2)}, u32[]{:S(2)}) collective-permute-start(s32[2,2,1,32]{3,2,1,0:T(1,128)S(1)} %copy-done.2), channel_id=1, source_target_pairs={{0,1},{1,0},{2,3},{3,2},{4,5},{5,4},{6,7},{7,6},{8,9},{9,8},{10,11... | collective-permute-start | bytes 1544 | tf_op jit(solution)/shard_map/ppermute | solution.py:606
  13.5 0.7 %copy-start.3 = (f32[256]{0:T(256)S(1)}, f32[256]{0:T(256)}, u32[]{:S(2)}) copy-start(f32[256]{0:T(256)} %param.10) | copy-start | bytes 3076
  13.5 0.7 %copy-start.4 = (f32[32]{0:T(128)S(1)}, f32[32]{0:T(128)}, u32[]{:S(2)}) copy-start(f32[32]{0:T(128)} %param.9) | copy-start | bytes 388
  14.6 0.7 %collective-permute-start.2 = (bf16[80,128]{1,0:T(8,128)(2,1)S(1)}, bf16[80,128]{1,0:T(8,128)(2,1)S(1)}, u32[]{:S(2)}, u32[]{:S(2)}) collective-permute-start(bf16[80,128]{1,0:T(8,128)(2,1)S(1)} %get-tuple-element.27), channel_id=1, source_target_pairs={{2,4},{4,2},{6,8},{8,6},{10,12},{12,10},{14,16},{16,14},{18,20},{2... | collective-permute-start | bytes 61448 | tf_op jit(solution)/shard_map/ppermute | solution.py:555
  17.4 6.8 %collective-permute-start.6 = (bf16[80,128]{1,0:T(8,128)(2,1)S(1)}, bf16[80,128]{1,0:T(8,128)(2,1)S(1)}, u32[]{:S(2)}, u32[]{:S(2)}) collective-permute-start(bf16[80,128]{1,0:T(8,128)(2,1)S(1)} %get-tuple-element.35), channel_id=1, source_target_pairs={{0,2},{2,0},{4,6},{6,4},{8,10},{10,8},{12,14},{14,12},{16,18},{18,... | collective-permute-start | bytes 61448 | tf_op jit(solution)/shard_map/ppermute | solution.py:555
  25.4 1.2 %collective-permute-start.7 = (f32[16,128]{1,0:T(8,128)S(1)}, f32[16,128]{1,0:T(8,128)S(1)}, u32[]{:S(2)}, u32[]{:S(2)}) collective-permute-start(f32[16,128]{1,0:T(8,128)S(1)} %shard_map.95), channel_id=1, source_target_pairs={{0,2},{2,0},{4,6},{6,4},{8,10},{10,8},{12,14},{14,12},{16,18},{18,... | collective-permute-start | bytes 24584 | tf_op jit(solution)/shard_map/ppermute | solution.py:570
  26.7 5.4 %collective-permute-start.10 = (f32[16,128]{1,0:T(8,128)S(1)}, f32[16,128]{1,0:T(8,128)S(1)}, u32[]{:S(2)}, u32[]{:S(2)}) collective-permute-start(f32[16,128]{1,0:T(8,128)S(1)} %add.14), channel_id=1, source_target_pairs={{0,12},{2,14},{4,8},{6,10},{8,4},{10,6},{12,0},{14,2},{16,28},{18,... | collective-permute-start | bytes 24584 | tf_op jit(solution)/shard_map/ppermute | solution.py:570
  30.4 3.7 %collective-permute-start.9 = (f32[16,128]{1,0:T(8,128)S(1)}, f32[16,128]{1,0:T(8,128)S(1)}, u32[]{:S(2)}, u32[]{:S(2)}) collective-permute-start(f32[16,128]{1,0:T(8,128)S(1)} %add.14), channel_id=1, source_target_pairs={{0,8},{2,10},{4,12},{6,14},{8,0},{10,2},{12,4},{14,6},{16,24},{18,... | collective-permute-start | bytes 24584 | tf_op jit(solution)/shard_map/ppermute | solution.py:570
  30.8 3.7 %collective-permute-start.8 = (f32[16,128]{1,0:T(8,128)S(1)}, f32[16,128]{1,0:T(8,128)S(1)}, u32[]{:S(2)}, u32[]{:S(2)}) collective-permute-start(f32[16,128]{1,0:T(8,128)S(1)} %add.14), channel_id=1, source_target_pairs={{0,4},{2,6},{4,0},{6,2},{8,12},{10,14},{12,8},{14,10},{16,20},{18,... | collective-permute-start | bytes 24584 | tf_op jit(solution)/shard_map/ppermute | solution.py:570
  34.5 4.5 %collective-permute-start.11 = (f32[16,128]{1,0:T(8,128)S(1)}, f32[16,128]{1,0:T(8,128)S(1)}, u32[]{:S(2)}, u32[]{:S(2)}) collective-permute-start(f32[16,128]{1,0:T(8,128)S(1)} %add_add_fusion.own_ref), channel_id=1, source_target_pairs={{0,16},{2,18},{4,20},{6,22},{8,24},{10,26},{12,28},{14,30},{16,0},... | collective-permute-start | bytes 24584 | tf_op jit(solution)/shard_map/ppermute | solution.py:575

commit v6 on v5

--- a/solution.py
+++ b/solution.py
@@ -99,17 +99,13 @@
     return b if a is None else [x + y for x, y in zip(a, b)]
 
 
-def table_kernel(dims, weight_ref, var_ref, offs_ref, *refs):
+def table_kernel(dims, weight_ref, *refs):
     nf, fl, nsc, T = dims
     shift_refs, goal_refs, refs = refs[:nf], refs[nf : 2 * nf], refs[2 * nf :]
     fwd_ref, fwdl_ref, inv_ref, invl_ref, part_ref, wideh_ref, widel_ref = refs[:7]
-    big_ref, bigt_ref, small_ref, own_ref, side_ref, edge_ref, goal_ref, rows_ref, raw_ref = refs[7:]
+    big_ref, bigt_ref, own_ref, side_ref, edge_ref, goal_ref, rows_ref, raw_ref = refs[7:]
     odd = lax.rem(lax.axis_index("space"), 2)
     fr = lax.axis_index("frame")
-    offs = jnp.concatenate([offs_ref[...], jnp.zeros((1, LANES - 32), F32)], axis=1)
-    small_ref[...] = jnp.concatenate(
-        [jnp.exp(var_ref[...]), offs, jnp.zeros((5, LANES), F32)], axis=0
-    )
     for j in range(nf):
         for l in range(fl):
             for c in range(2):
@@ -122,8 +118,8 @@
     words = own_ref[...].astype(F32)
     if count % 16:
         words = jnp.concatenate([words, jnp.zeros((16 - count % 16, LANES), F32)], axis=0)
-    lead = nf * nsc * 32
-    side_ref[lead:, :] = words.astype(BF16)
+    G = side_ref.shape[2] // LANES
+    blocks = [words[16 * k : 16 * k + 16] for k in range(words.shape[0] // 16)]
     for j in range(nf):
         at = pl.multiple_of(lax.rem(fr + j, nf) * (nsc * LANES), LANES)
         for c in range(nsc):
@@ -134,7 +130,14 @@
                 goal_ref[r, :, to] = raw_ref[pl.ds(r, 32, stride=8), :]
             rows = slice((j * nsc + c) * 32, (j * nsc + c) * 32 + 32)
             edge_ref[rows, :] = raw_ref[pl.ds(7 - 7 * odd, 32, stride=8), :].astype(BF16)
-            side_ref[rows, :] = raw_ref[pl.ds(7 * odd, 32, stride=8), :].astype(BF16)
+            edge = raw_ref[pl.ds(7 * odd, 32, stride=8), :]
+            blocks += [edge[:16], edge[16:]]
+    for k, block in enumerate(blocks):
+        at = (k % G) * LANES
+        side_ref[k // G, :, at : at + LANES] = block.astype(BF16)
+    for k in range(len(blocks), side_ref.shape[0] * G):
+        at = (k % G) * LANES
+        side_ref[k // G, :, at : at + LANES] = jnp.zeros((TILE, LANES), BF16)
 
     lane = lax.broadcasted_iota(jnp.int32, (TILE, LANES), 1)
     line = lax.broadcasted_iota(jnp.int32, (TILE, LANES), 0)
@@ -212,20 +215,25 @@
             bigt_ref[k * TILE : (k + 1) * TILE, at : at + width] = value[:, :width].astype(BF16)
 
 
+def side_block(ref, plane, k):
+    per = ref.shape[2] // LANES
+    at = (k % per) * LANES
+    return ref[plane + k // per, :, at : at + LANES].astype(F32)
+
+
 def merge_kernel(dims, *refs):
-    nf, fl, G, _, nsc = dims
+    nf, fl, G, _, _ = dims
     F = nf * fl
-    own_ref, side_ref, edge_ref, y_ref, yc_ref, yf_ref, var_ref = refs[:7]
-    fwd_ref, fwdl_ref, inv_ref, invl_ref = refs[7:11]
-    pack_ref, pc_ref, far_ref, h_ref = refs[11:15]
-    x_ref, idx_ref, p_ref, q_ref, xs_ref, words_ref, own_sm, far_sm, sems = refs[15:]
+    own_ref, edge_ref, y_ref, yc_ref, yf_ref, var_ref = refs[:6]
+    fwd_ref, fwdl_ref, inv_ref, invl_ref = refs[6:10]
+    pack_ref, pc_ref, far_ref, h_ref = refs[10:14]
+    x_ref, idx_ref, p_ref, q_ref, xs_ref, words_ref, own_sm, far_sm, sems = refs[14:]
     s = lax.axis_index("space")
     fr = lax.axis_index("frame")
     odd = lax.rem(s, 2)
-    lead = nf * nsc * 32
-
-    words = side_ref[lead:, :].astype(F32).astype(jnp.int32)
-    words_ref[...] = words[: 2 * F]
+
+    words = [side_block(yf_ref, 2 * F, k) for k in range(-(-2 * F // 16))]
+    words_ref[...] = jnp.concatenate(words, axis=0)[: 2 * F].astype(jnp.int32)
     moves = (
         pltpu.make_async_copy(own_ref, own_sm, sems.at[0]),
         pltpu.make_async_copy(words_ref, far_sm, sems.at[1]),
@@ -392,7 +400,7 @@
     pc_ref[0 : 4 * G, :] = jnp.where(at_odd, low, high).astype(BF16)
 
 
-def demosaic_kernel(dims, pack_ref, pc_ref, far_ref, side_ref, goals_ref, h_ref, *refs):
+def demosaic_kernel(dims, pack_ref, pc_ref, far_ref, yf_ref, goals_ref, h_ref, *refs):
     nf, fl, G, nsc, n_space, inv_pixels = dims
     F = nf * fl
     W = G * LANES
@@ -411,7 +419,10 @@
             first = (j * nsc + c) * 32
             to = pl.ds(pl.multiple_of(at + c * LANES, LANES), LANES)
             goal_ref[1 - odd, :, to] = pc_ref[lead + first : lead + first + 32, :].astype(F32)
-            goal_ref[odd, :, to] = side_ref[first : first + 32, :].astype(F32)
+            block = -(-2 * F // 16) + 2 * (j * nsc + c)
+            goal_ref[odd, :, to] = jnp.concatenate(
+                [side_block(yf_ref, 2 * F, block), side_block(yf_ref, 2 * F, block + 1)], axis=0
+            )
 
     near = pc_ref[0:lead, :].astype(F32)
     far = far_ref[...]
@@ -616,14 +627,11 @@
     for j in range(1, nf):
         y = lax.dynamic_update_slice(y, raws[j], (j * fl, 0, 0))
     yc = involution(y, n_space, 1, 0)
-    pair = jnp.concatenate([y, yc], axis=0)
-    yf = involution(pair, n_space, 1, 1)
-
     shape = jax.ShapeDtypeStruct
-    side_rows = nf * nsc * channels + -(-2 * F // 16) * 16
-    *tables, big, bigt, small, own_rows, side, edge, site_goals = call(
+    planes = -(-(2 * nf * nsc + -(-2 * F // 16)) // G)
+    *tables, big, bigt, own_rows, side, edge, site_goals = call(
         functools.partial(table_kernel, (nf, fl, nsc, T)),
-        [weight, log_var.reshape(2, LANES), offset.reshape(1, channels), *shift_parts, *goals],
+        [weight, *shift_parts, *goals],
         [
             shape((256, 256), BF16),
             shape((128, 256), BF16),
@@ -634,19 +642,22 @@
             shape((256, 512), BF16),
             shape((320, 256), BF16),
             shape((96, 320), BF16),
-            shape((8, LANES), F32),
             shape((2 * F, LANES), jnp.int32),
-            shape((side_rows, LANES), BF16),
+            shape((planes, TILE, W), BF16),
             shape((nf * nsc * channels, LANES), BF16),
             shape((8, channels, W // 2), F32),
         ],
         [pltpu.VMEM((6, 40, LANES), F32), pltpu.VMEM((256, LANES), F32)],
     )
-    side = involution(side, n_space, 1, 1)
+    pair = jnp.concatenate([y, yc, side], axis=0)
+    yf = involution(pair, n_space, 1, 1)
+    small = jnp.concatenate(
+        [jnp.exp(log_var), offset, jnp.zeros((6 * LANES - channels,), F32)]
+    ).reshape(8, LANES)
 
     pack, pc, far, moments = call(
         functools.partial(merge_kernel, (nf, fl, G, T, nsc)),
-        [own_rows, side, edge, y, yc, yf, small, *tables[:4]],
+        [own_rows, edge, y, yc, yf, small, *tables[:4]],
         [
             shape((G, TILE, LANES), F32),
             shape((4 * G + nf * nsc * channels, LANES), BF16),
@@ -668,7 +679,7 @@
     pc = involution(pc, n_space, 1, 0)
     (partial,) = call(
         functools.partial(demosaic_kernel, (nf, fl, G, nsc, n_space, inv_pixels)),
-        [pack, pc, far, side, site_goals, moments, big, bigt, small, *tables[4:]],
+        [pack, pc, far, yf, site_goals, moments, big, bigt, small, *tables[4:]],
         [shape((16, LANES), F32)],
         [
             pltpu.VMEM((2, channels, W // 2), F32),

time: 40.1 us -> 37.2 us (0.928)
  waiting for transfers between devices: 12.3 us -> 9.99 us
  starting transfers between devices: 20.8 us -> 20.1 us
    ppermute x3, waiting for transfers between devices: 4.81 us -> 2.82 us  [from_frame(): return lax.ppermute(value, 'frame', [(i, (i - j) % nf) for i in range(nf)])]
    ppermute x4 -> x3, waiting for transfers between devices: 2.09 us -> 0.85 us  [involution(): return lax.ppermute(value, 'space', pairs)]
    ppermute x4, starting transfers between devices: 5.65 us -> 4.7 us  [sum_space(): got.append(lax.ppermute(value, 'space', [(i, i ^ m) for i in range(count)]))]
    ppermute x4, waiting for transfers between devices: 3.41 us -> 4.36 us  [sum_space(): got.append(lax.ppermute(value, 'space', [(i, i ^ m) for i in range(count)]))]
    ppermute x4 -> x3, starting transfers between devices: 7.33 us -> 7.66 us  [involution(): return lax.ppermute(value, 'space', pairs)]
  transfers between devices with their start and end apart: 12 -> 11, of which waited for: 9 -> 8; matrix products, arithmetic and copies ran while one was open for 2% -> 2% of each run, Pallas kernels for 1% -> 1%
where the time goes in v6:
time: 37.2 us; the launch traced here: 37 us
  starting transfers between devices  20.1 us (54%)
  waiting for transfers between devices  9.99 us (27%)
  Pallas kernels  4.61 us (12%)
  local copies, waits for them, and re-layouts  1.43 us (4%)
  between operations  0.74 us (2%)
    ppermute x3, starting transfers between devices, involution(): return lax.ppermute(value, 'space', pairs)  7.66 us
    ppermute x3, starting transfers between devices, from_frame(): return lax.ppermute(value, 'frame', [(i, (i - j) % nf) for i in range(nf)])  5.2 us
    ppermute x4, starting transfers between devices, sum_space(): got.append(lax.ppermute(value, 'space', [(i, i ^ m) for i in range(count)]))  4.7 us
    pallas_call x4, Pallas kernels, call(): pl.pallas_call(body, out_shape=tuple(outs), in_specs=[vm] * len(args), ou...  4.61 us
    ppermute x4, waiting for transfers between devices, sum_space(): got.append(lax.ppermute(value, 'space', [(i, i ^ m) for i in range(count)]))  4.36 us
    ppermute x3, waiting for transfers between devices, from_frame(): return lax.ppermute(value, 'frame', [(i, (i - j) % nf) for i in range(nf)])  2.82 us
    ppermute x1, starting transfers between devices, sum_space(): got = lax.ppermute(value, 'space', [(i, i ^ mask) for i in range(count)])  2.59 us
    ppermute x1, waiting for transfers between devices, sum_space(): got = lax.ppermute(value, 'space', [(i, i ^ mask) for i in range(count)])  1.96 us
  transfers between devices with their start and end apart: 11, of which 8 were waited for; matrix products, arithmetic and copies ran while one was open for 2% of the time, Pallas kernels for 1%

profile of v6, /device:TPU:0, one launch (start us, length us, event | category | flops | bytes accessed | tf_op | source)
XLA Modules:
  0.0 37.0 jit_solution(1388125109324808745)
XLA Ops:
  0.6 3.0 %collective-permute-start.2 = (bf16[2,16,512]{2,1,0:T(8,128)(2,1)}, bf16[2,16,512]{2,1,0:T(8,128)(2,1)S(1)}, u32[]{:S(2)}, u32[]{:S(2)}) collective-permute-start(bf16[2,16,512]{2,1,0:T(8,128)(2,1)} %param.6), channel_id=1, source_target_pairs={{0,1},{1,0},{2,3},{3,2},{4,5},{5,4},{6,7},{7,6},{8,9},{9,8},{10,11... | collective-permute-start | bytes 98312 | tf_op jit(solution)/shard_map/ppermute | solution.py:617
  3.7 0.1 collective-permute-start.1
  3.8 0.8 %pad.4 = bf16[4,16,512]{2,1,0:T(8,128)(2,1)S(1)} pad(bf16[2,16,512]{2,1,0:T(8,128)(2,1)} %param.6, bf16[]{:T(256)} %constant.1.clone.1), padding=0_2x0_0x0_0 | pad | bytes 98306 | tf_op jit(solution)/shard_map/jit(_pad)/pad | solution.py:625
  4.5 1.3 %collective-permute-done.2 = bf16[2,16,512]{2,1,0:T(8,128)(2,1)S(1)} collective-permute-done((bf16[2,16,512]{2,1,0:T(8,128)(2,1)}, bf16[2,16,512]{2,1,0:T(8,128)(2,1)S(1)}, u32[]{:S(2)}, u32[]{:S(2)}) %collective-permute-start.2) | collective-permute-done | bytes 32800 | tf_op jit(solution)/shard_map/ppermute | solution.py:617
  5.8 0.0 collective-permute-start.3
  5.8 2.1 %collective-permute-start = (s32[2,2,1,32]{3,2,1,0:T(1,128)S(1)}, s32[2,2,1,32]{3,2,1,0:T(1,128)S(1)}, u32[]{:S(2)}, u32[]{:S(2)}) collective-permute-start(s32[2,2,1,32]{3,2,1,0:T(1,128)S(1)} %copy-done.2), channel_id=1, source_target_pairs={{0,1},{1,0},{2,3},{3,2},{4,5},{5,4},{6,7},{7,6},{8,9},{9,8},{10,11... | collective-permute-start | bytes 1544 | tf_op jit(solution)/shard_map/ppermute | solution.py:617
  7.9 1.6 %collective-permute-done.refs_1_ = s32[2,2,1,32]{3,2,1,0:T(1,128)S(1)} collective-permute-done((s32[2,2,1,32]{3,2,1,0:T(1,128)S(1)}, s32[2,2,1,32]{3,2,1,0:T(1,128)S(1)}, u32[]{:S(2)}, u32[]{:S(2)}) %collective-permute-start) | collective-permute-done | bytes 544 | tf_op jit(solution)/shard_map/ppermute | solution.py:617
  9.4 0.0 collective-permute-done.1.refs_3_
  9.5 0.5 %shard_map.93 = (bf16[256,256]{1,0:T(8,128)(2,1)S(1)}, bf16[128,256]{1,0:T(8,128)(2,1)S(1)}, bf16[256,256]{1,0:T(8,128)(2,1)S(1)}, bf16[256,128]{1,0:T(8,128)(2,...) custom-call(bf16[32,36]{1,0:T(8,128)(2,1)S(1)} %copy-done.1, ...), custom_call_target="tpu_custom_call" | custom-call | tf_op jit(solution)/shard_map/pallas_call | solution.py:594
  9.9 0.0 collective-permute-done.3.refs_3_
  9.9 0.0 copy-start.3
  10.0 0.7 %collective-permute-start.4 = (bf16[10,16,512]{2,1,0:T(8,128)(2,1)S(1)}, bf16[10,16,512]{2,1,0:T(8,128)(2,1)S(1)}, u32[]{:S(2)}, u32[]{:S(2)}) collective-permute-start(bf16[10,16,512]{2,1,0:T(8,128)(2,1)S(1)} %pad_maximum_fusion), channel_id=1, source_target_pairs={{2,4},{4,2},{6,8},{8,6},{10,12},{12,10},{14,16},{16,14},{18,20},{2... | collective-permute-start | bytes 491528 | tf_op jit(solution)/shard_map/ppermute | solution.py:566
  10.6 0.0 copy-done.3
  10.7 0.0 copy-start.4
  10.7 0.6 %copy-done.4 = f32[32]{0:T(128)S(1)} copy-done((f32[32]{0:T(128)S(1)}, f32[32]{0:T(128)}, u32[]{:S(2)}) %copy-start.4) | copy-done | bytes 152
  11.3 0.1 maximum_bitcast_fusion.refs_5_.refs_2_
  11.4 0.0 collective-permute-done.4.refs_4_.yf_ref
  11.4 2.1 %shard_map.94 = (f32[4,16,128]{2,1,0:T(8,128)S(1)}, bf16[80,128]{1,0:T(8,128)(2,1)S(1)}, f32[16,128]{1,0:T(8,128)S(1)}, f32[256,128]{1,0:T(8,128)S(1)}) custom-call(s32[8,128]{1,0:T(8,128)S(1)} %get-tuple-element.25.refs_0_, bf16[64,128]{1,0:T(8,128)(2,1)S(1)} %get-tuple-element.26.refs_1_, ...), custom_call_target="tpu_custom_call" | custom-call | tf_op jit(solution)/shard_map/pallas_call | solution.py:594
  13.5 7.0 %collective-permute-start.5 = (bf16[80,128]{1,0:T(8,128)(2,1)S(1)}, bf16[80,128]{1,0:T(8,128)(2,1)S(1)}, u32[]{:S(2)}, u32[]{:S(2)}) collective-permute-start(bf16[80,128]{1,0:T(8,128)(2,1)S(1)} %get-tuple-element.33), channel_id=1, source_target_pairs={{0,2},{2,0},{4,6},{6,4},{8,10},{10,8},{12,14},{14,12},{16,18},{18,... | collective-permute-start | bytes 61448 | tf_op jit(solution)/shard_map/ppermute | solution.py:566
  20.5 0.8 %collective-permute-done.5.pc_ref = bf16[80,128]{1,0:T(8,128)(2,1)S(1)} collective-permute-done((bf16[80,128]{1,0:T(8,128)(2,1)S(1)}, bf16[80,128]{1,0:T(8,128)(2,1)S(1)}, u32[]{:S(2)}, u32[]{:S(2)}) %collective-permute-start.5) | collective-permute-done | bytes 20512 | tf_op jit(solution)/shard_map/ppermute | solution.py:566
  21.4 1.2 %shard_map.95 = f32[16,128]{1,0:T(8,128)S(1)} custom-call(f32[4,16,128]{2,1,0:T(8,128)S(1)} %get-tuple-element.32.pack_ref, bf16[80,128]{1,0:T(8,128)(2,1)S(1)} %collective-permute-done.5.pc_ref, f32[16,128]{1,0:T(8,128)S(1)} %get-tuple-element.34.far_ref, bf16[10,16,512]{2,1,0:T(8,128)(2,1)S(1)} %collective-permute-done.4.refs_4_.yf_ref, ...), custom_call_target="tpu_custom_call" | custom-call | tf_op jit(solution)/shard_map/pallas_call | solution.py:594
  22.6 0.4 %collective-permute-start.6 = (f32[16,128]{1,0:T(8,128)S(1)}, f32[16,128]{1,0:T(8,128)S(1)}, u32[]{:S(2)}, u32[]{:S(2)}) collective-permute-start(f32[16,128]{1,0:T(8,128)S(1)} %shard_map.95), channel_id=1, source_target_pairs={{0,2},{2,0},{4,6},{6,4},{8,10},{10,8},{12,14},{14,12},{16,18},{18,... | collective-permute-start | bytes 24584 | tf_op jit(solution)/shard_map/ppermute | solution.py:581
  23.0 0.8 %collective-permute-done.6 = f32[16,128]{1,0:T(8,128)S(1)} collective-permute-done((f32[16,128]{1,0:T(8,128)S(1)}, f32[16,128]{1,0:T(8,128)S(1)}, u32[]{:S(2)}, u32[]{:S(2)}) %collective-permute-start.6) | collective-permute-done | bytes 8224 | tf_op jit(solution)/shard_map/ppermute | solution.py:581
  23.9 3.7 %collective-permute-start.9 = (f32[16,128]{1,0:T(8,128)S(1)}, f32[16,128]{1,0:T(8,128)S(1)}, u32[]{:S(2)}, u32[]{:S(2)}) collective-permute-start(f32[16,128]{1,0:T(8,128)S(1)} %add.14), channel_id=1, source_target_pairs={{0,12},{2,14},{4,8},{6,10},{8,4},{10,6},{12,0},{14,2},{16,28},{18,... | collective-permute-start | bytes 24584 | tf_op jit(solution)/shard_map/ppermute | solution.py:581
  27.6 0.4 %collective-permute-start.8 = (f32[16,128]{1,0:T(8,128)S(1)}, f32[16,128]{1,0:T(8,128)S(1)}, u32[]{:S(2)}, u32[]{:S(2)}) collective-permute-start(f32[16,128]{1,0:T(8,128)S(1)} %add.14), channel_id=1, source_target_pairs={{0,8},{2,10},{4,12},{6,14},{8,0},{10,2},{12,4},{14,6},{16,24},{18,... | collective-permute-start | bytes 24584 | tf_op jit(solution)/shard_map/ppermute | solution.py:581
  28.0 0.1 collective-permute-start.7
  28.2 1.1 %collective-permute-done.9 = f32[16,128]{1,0:T(8,128)S(1)} collective-permute-done((f32[16,128]{1,0:T(8,128)S(1)}, f32[16,128]{1,0:T(8,128)S(1)}, u32[]{:S(2)}, u32[]{:S(2)}) %collective-permute-start.9) | collective-permute-done | bytes 8224 | tf_op jit(solution)/shard_map/ppermute | solution.py:581
  29.2 2.0 %collective-permute-done.8 = f32[16,128]{1,0:T(8,128)S(1)} collective-permute-done((f32[16,128]{1,0:T(8,128)S(1)}, f32[16,128]{1,0:T(8,128)S(1)}, u32[]{:S(2)}, u32[]{:S(2)}) %collective-permute-start.8) | collective-permute-done | bytes 8224 | tf_op jit(solution)/shard_map/ppermute | solution.py:581
  31.2 0.4 %collective-permute-done.7 = f32[16,128]{1,0:T(8,128)S(1)} collective-permute-done((f32[16,128]{1,0:T(8,128)S(1)}, f32[16,128]{1,0:T(8,128)S(1)}, u32[]{:S(2)}, u32[]{:S(2)}) %collective-permute-start.7) | collective-permute-done | bytes 8224 | tf_op jit(solution)/shard_map/ppermute | solution.py:581
  31.7 2.6 %collective-permute-start.10 = (f32[16,128]{1,0:T(8,128)S(1)}, f32[16,128]{1,0:T(8,128)S(1)}, u32[]{:S(2)}, u32[]{:S(2)}) collective-permute-start(f32[16,128]{1,0:T(8,128)S(1)} %add_add_fusion.own_ref), channel_id=1, source_target_pairs={{0,16},{2,18},{4,20},{6,22},{8,24},{10,26},{12,28},{14,30},{16,0},... | collective-permute-start | bytes 24584 | tf_op jit(solution)/shard_map/ppermute | solution.py:586
  34.3 2.0 %collective-permute-done.10.got_ref = f32[16,128]{1,0:T(8,128)S(1)} collective-permute-done((f32[16,128]{1,0:T(8,128)S(1)}, f32[16,128]{1,0:T(8,128)S(1)}, u32[]{:S(2)}, u32[]{:S(2)}) %collective-permute-start.10) | collective-permute-done | bytes 8224 | tf_op jit(solution)/shard_map/ppermute | solution.py:586
  36.2 0.8 %shard_map.96 = (f32[16,256]{1,0:T(8,128)}, f32[32,36]{1,0:T(8,128)}, f32[1,32]{1,0:T(1,128)}, f32[2,128]{1,0:T(2,128)}) custom-call(f32[4,16,128]{2,1,0:T(8,128)S(1)} %get-tuple-element.32.pack_ref, f32[16,128]{1,0:T(8,128)S(1)} %add_add_fusion.own_ref, f32[16,128]{1,0:T(8,128)S(1)} %collective-permute-done.10.got_ref), custom_call_target="tpu_custom_call" | custom-call | tf_op jit(solution)/shard_map/pallas_call | solution.py:594
  (12 shorter events, 0.1 us)
Async XLA Ops:
  0.6 8.8 %copy-start = (bf16[32,8,128]{2,1,0:T(8,128)(2,1)S(1)}, bf16[32,8,128]{2,1,0:T(8,128)(2,1)}, u32[]{:S(2)}) copy-start(bf16[32,8,128]{2,1,0:T(8,128)(2,1)} %refs_2_.1) | copy-start | bytes 196612
  0.6 5.1 %collective-permute-start.2 = (bf16[2,16,512]{2,1,0:T(8,128)(2,1)}, bf16[2,16,512]{2,1,0:T(8,128)(2,1)S(1)}, u32[]{:S(2)}, u32[]{:S(2)}) collective-permute-start(bf16[2,16,512]{2,1,0:T(8,128)(2,1)} %param.6), channel_id=1, source_target_pairs={{0,1},{1,0},{2,3},{3,2},{4,5},{5,4},{6,7},{7,6},{8,9},{9,8},{10,11... | collective-permute-start | bytes 98312 | tf_op jit(solution)/shard_map/ppermute | solution.py:617
  3.7 5.8 %collective-permute-start.1 = (bf16[32,8,128]{2,1,0:T(8,128)(2,1)}, bf16[32,8,128]{2,1,0:T(8,128)(2,1)S(1)}, u32[]{:S(2)}, u32[]{:S(2)}) collective-permute-start(bf16[32,8,128]{2,1,0:T(8,128)(2,1)} %refs_2_.1), channel_id=1, source_target_pairs={{0,1},{1,0},{2,3},{3,2},{4,5},{5,4},{6,7},{7,6},{8,9},{9,8},{10,11... | collective-permute-start | bytes 196616 | tf_op jit(solution)/shard_map/ppermute | solution.py:617
  4.5 1.3 %copy-start.2 = (s32[2,2,1,32]{3,2,1,0:T(1,128)S(1)}, s32[2,2,1,32]{3,2,1,0:T(1,128)}, u32[]{:S(2)}) copy-start(s32[2,2,1,32]{3,2,1,0:T(1,128)} %refs_0_.1) | copy-start | bytes 1540
  4.5 4.9 %copy-start.1 = (bf16[32,36]{1,0:T(8,128)(2,1)S(1)}, bf16[32,36]{1,0:T(8,128)(2,1)}, u32[]{:S(2)}) copy-start(bf16[32,36]{1,0:T(8,128)(2,1)} %weight_ref.1) | copy-start | bytes 6916
  5.8 4.1 %collective-permute-start.3 = (bf16[4,16,512]{2,1,0:T(8,128)(2,1)S(1)}, bf16[4,16,512]{2,1,0:T(8,128)(2,1)S(1)}, u32[]{:S(2)}, u32[]{:S(2)}) collective-permute-start(bf16[4,16,512]{2,1,0:T(8,128)(2,1)S(1)} %constant_dynamic-update-slice_fusion.refs_2_), channel_id=1, source_target_pairs={{0,2},{2,0},{4,6},{6,4},{8,10},{10,8},{12,14},{14,12},{16,18},{18,... | collective-permute-start | bytes 196616 | tf_op jit(solution)/shard_map/ppermute | solution.py:566
  5.8 3.7 %collective-permute-start = (s32[2,2,1,32]{3,2,1,0:T(1,128)S(1)}, s32[2,2,1,32]{3,2,1,0:T(1,128)S(1)}, u32[]{:S(2)}, u32[]{:S(2)}) collective-permute-start(s32[2,2,1,32]{3,2,1,0:T(1,128)S(1)} %copy-done.2), channel_id=1, source_target_pairs={{0,1},{1,0},{2,3},{3,2},{4,5},{5,4},{6,7},{7,6},{8,9},{9,8},{10,11... | collective-permute-start | bytes 1544 | tf_op jit(solution)/shard_map/ppermute | solution.py:617
  9.9 0.7 %copy-start.3 = (f32[256]{0:T(256)S(1)}, f32[256]{0:T(256)}, u32[]{:S(2)}) copy-start(f32[256]{0:T(256)} %param.10) | copy-start | bytes 3076
  10.0 1.4 %collective-permute-start.4 = (bf16[10,16,512]{2,1,0:T(8,128)(2,1)S(1)}, bf16[10,16,512]{2,1,0:T(8,128)(2,1)S(1)}, u32[]{:S(2)}, u32[]{:S(2)}) collective-permute-start(bf16[10,16,512]{2,1,0:T(8,128)(2,1)S(1)} %pad_maximum_fusion), channel_id=1, source_target_pairs={{2,4},{4,2},{6,8},{8,6},{10,12},{12,10},{14,16},{16,14},{18,20},{2... | collective-permute-start | bytes 491528 | tf_op jit(solution)/shard_map/ppermute | solution.py:566
  10.7 0.7 %copy-start.4 = (f32[32]{0:T(128)S(1)}, f32[32]{0:T(128)}, u32[]{:S(2)}) copy-start(f32[32]{0:T(128)} %param.9) | copy-start | bytes 388
  13.5 7.8 %collective-permute-start.5 = (bf16[80,128]{1,0:T(8,128)(2,1)S(1)}, bf16[80,128]{1,0:T(8,128)(2,1)S(1)}, u32[]{:S(2)}, u32[]{:S(2)}) collective-permute-start(bf16[80,128]{1,0:T(8,128)(2,1)S(1)} %get-tuple-element.33), channel_id=1, source_target_pairs={{0,2},{2,0},{4,6},{6,4},{8,10},{10,8},{12,14},{14,12},{16,18},{18,... | collective-permute-start | bytes 61448 | tf_op jit(solution)/shard_map/ppermute | solution.py:566
  22.6 1.2 %collective-permute-start.6 = (f32[16,128]{1,0:T(8,128)S(1)}, f32[16,128]{1,0:T(8,128)S(1)}, u32[]{:S(2)}, u32[]{:S(2)}) collective-permute-start(f32[16,128]{1,0:T(8,128)S(1)} %shard_map.95), channel_id=1, source_target_pairs={{0,2},{2,0},{4,6},{6,4},{8,10},{10,8},{12,14},{14,12},{16,18},{18,... | collective-permute-start | bytes 24584 | tf_op jit(solution)/shard_map/ppermute | solution.py:581
  23.9 5.3 %collective-permute-start.9 = (f32[16,128]{1,0:T(8,128)S(1)}, f32[16,128]{1,0:T(8,128)S(1)}, u32[]{:S(2)}, u32[]{:S(2)}) collective-permute-start(f32[16,128]{1,0:T(8,128)S(1)} %add.14), channel_id=1, source_target_pairs={{0,12},{2,14},{4,8},{6,10},{8,4},{10,6},{12,0},{14,2},{16,28},{18,... | collective-permute-start | bytes 24584 | tf_op jit(solution)/shard_map/ppermute | solution.py:581
  27.6 3.7 %collective-permute-start.8 = (f32[16,128]{1,0:T(8,128)S(1)}, f32[16,128]{1,0:T(8,128)S(1)}, u32[]{:S(2)}, u32[]{:S(2)}) collective-permute-start(f32[16,128]{1,0:T(8,128)S(1)} %add.14), channel_id=1, source_target_pairs={{0,8},{2,10},{4,12},{6,14},{8,0},{10,2},{12,4},{14,6},{16,24},{18,... | collective-permute-start | bytes 24584 | tf_op jit(solution)/shard_map/ppermute | solution.py:581
  28.0 3.7 %collective-permute-start.7 = (f32[16,128]{1,0:T(8,128)S(1)}, f32[16,128]{1,0:T(8,128)S(1)}, u32[]{:S(2)}, u32[]{:S(2)}) collective-permute-start(f32[16,128]{1,0:T(8,128)S(1)} %add.14), channel_id=1, source_target_pairs={{0,4},{2,6},{4,0},{6,2},{8,12},{10,14},{12,8},{14,10},{16,20},{18,... | collective-permute-start | bytes 24584 | tf_op jit(solution)/shard_map/ppermute | solution.py:581
  31.7 4.5 %collective-permute-start.10 = (f32[16,128]{1,0:T(8,128)S(1)}, f32[16,128]{1,0:T(8,128)S(1)}, u32[]{:S(2)}, u32[]{:S(2)}) collective-permute-start(f32[16,128]{1,0:T(8,128)S(1)} %add_add_fusion.own_ref), channel_id=1, source_target_pairs={{0,16},{2,18},{4,20},{6,22},{8,24},{10,26},{12,28},{14,30},{16,0},... | collective-permute-start | bytes 24584 | tf_op jit(solution)/shard_map/ppermute | solution.py:586

commit v7 on v6

--- a/solution.py
+++ b/solution.py
@@ -99,27 +99,37 @@
     return b if a is None else [x + y for x, y in zip(a, b)]
 
 
-def table_kernel(dims, weight_ref, *refs):
-    nf, fl, nsc, T = dims
-    shift_refs, goal_refs, refs = refs[:nf], refs[nf : 2 * nf], refs[2 * nf :]
-    fwd_ref, fwdl_ref, inv_ref, invl_ref, part_ref, wideh_ref, widel_ref = refs[:7]
-    big_ref, bigt_ref, own_ref, side_ref, edge_ref, goal_ref, rows_ref, raw_ref = refs[7:]
+def side_kernel(dims, shift_ref, goal_ref, side_ref, raw_ref, words_ref):
+    fl, nsc, T = dims
     odd = lax.rem(lax.axis_index("space"), 2)
+    G = side_ref.shape[2] // LANES
+    for l in range(fl):
+        for c in range(2):
+            row = shift_ref[l, c]
+            if T < LANES:
+                row = jnp.concatenate([row, jnp.zeros((1, LANES - T), jnp.int32)], axis=1)
+            words_ref[l * 2 + c : l * 2 + c + 1, :] = row
+    far, core = [], []
+    for c in range(nsc):
+        raw_ref[...] = goal_ref[:, :, c * LANES : (c + 1) * LANES].astype(F32).reshape(256, LANES)
+        edge = raw_ref[pl.ds(7 * odd, 32, stride=8), :]
+        far += [edge[:16], edge[16:]]
+        edge = raw_ref[pl.ds(7 - 7 * odd, 32, stride=8), :]
+        core += [edge[:16], edge[16:]]
+    words = words_ref[...].astype(F32)
+    blocks = far + [words[16 * k : 16 * k + 16] for k in range(words.shape[0] // 16)]
+    blocks += [jnp.zeros((TILE, LANES), F32)] * (-len(blocks) % G)
+    blocks += core
+    blocks += [jnp.zeros((TILE, LANES), F32)] * (-len(blocks) % G)
+    for k, block in enumerate(blocks):
+        at = (k % G) * LANES
+        side_ref[k // G, :, at : at + LANES] = block.astype(BF16)
+
+
+def target_kernel(dims, *refs):
+    nf, nsc = dims
+    goal_refs, goal_ref, raw_ref = refs[:nf], refs[nf], refs[nf + 1]
     fr = lax.axis_index("frame")
-    for j in range(nf):
-        for l in range(fl):
-            for c in range(2):
-                row = shift_refs[j][l, c]
-                if T < LANES:
-                    row = jnp.concatenate([row, jnp.zeros((1, LANES - T), jnp.int32)], axis=1)
-                at = (j * fl + l) * 2 + c
-                own_ref[at : at + 1, :] = row
-    count = nf * fl * 2
-    words = own_ref[...].astype(F32)
-    if count % 16:
-        words = jnp.concatenate([words, jnp.zeros((16 - count % 16, LANES), F32)], axis=0)
-    G = side_ref.shape[2] // LANES
-    blocks = [words[16 * k : 16 * k + 16] for k in range(words.shape[0] // 16)]
     for j in range(nf):
         at = pl.multiple_of(lax.rem(fr + j, nf) * (nsc * LANES), LANES)
         for c in range(nsc):
@@ -128,17 +138,11 @@
             to = pl.ds(pl.multiple_of(at + c * LANES, LANES), LANES)
             for r in range(8):
                 goal_ref[r, :, to] = raw_ref[pl.ds(r, 32, stride=8), :]
-            rows = slice((j * nsc + c) * 32, (j * nsc + c) * 32 + 32)
-            edge_ref[rows, :] = raw_ref[pl.ds(7 - 7 * odd, 32, stride=8), :].astype(BF16)
-            edge = raw_ref[pl.ds(7 * odd, 32, stride=8), :]
-            blocks += [edge[:16], edge[16:]]
-    for k, block in enumerate(blocks):
-        at = (k % G) * LANES
-        side_ref[k // G, :, at : at + LANES] = block.astype(BF16)
-    for k in range(len(blocks), side_ref.shape[0] * G):
-        at = (k % G) * LANES
-        side_ref[k // G, :, at : at + LANES] = jnp.zeros((TILE, LANES), BF16)
-
+
+
+def table_kernel(weight_ref, *refs):
+    fwd_ref, fwdl_ref, inv_ref, invl_ref, part_ref, wideh_ref, widel_ref = refs[:7]
+    big_ref, bigt_ref, rows_ref = refs[7:]
     lane = lax.broadcasted_iota(jnp.int32, (TILE, LANES), 1)
     line = lax.broadcasted_iota(jnp.int32, (TILE, LANES), 0)
     cos, sin = waves(line * (lane & 15), 3)
@@ -222,18 +226,22 @@
 
 
 def merge_kernel(dims, *refs):
-    nf, fl, G, _, _ = dims
+    nf, fl, G, _, nsc = dims
     F = nf * fl
-    own_ref, edge_ref, y_ref, yc_ref, yf_ref, var_ref = refs[:6]
-    fwd_ref, fwdl_ref, inv_ref, invl_ref = refs[6:10]
-    pack_ref, pc_ref, far_ref, h_ref = refs[10:14]
-    x_ref, idx_ref, p_ref, q_ref, xs_ref, words_ref, own_sm, far_sm, sems = refs[14:]
+    near_refs, far_refs, refs = refs[:nf], refs[nf : 2 * nf], refs[2 * nf :]
+    var_ref, fwd_ref, fwdl_ref, inv_ref, invl_ref = refs[:5]
+    pack_ref, pc_ref, far_ref, h_ref = refs[5:9]
+    x_ref, idx_ref, p_ref, q_ref, xs_ref, own_ref, words_ref, own_sm, far_sm, sems = refs[9:]
     s = lax.axis_index("space")
     fr = lax.axis_index("frame")
     odd = lax.rem(s, 2)
 
-    words = [side_block(yf_ref, 2 * F, k) for k in range(-(-2 * F // 16))]
-    words_ref[...] = jnp.concatenate(words, axis=0)[: 2 * F].astype(jnp.int32)
+    wb = -(-2 * fl // 16)
+    for group, ref in ((near_refs, own_ref), (far_refs, words_ref)):
+        for j in range(nf):
+            words = [side_block(group[j], 2 * fl, 2 * nsc + k) for k in range(wb)]
+            words = jnp.concatenate(words, axis=0)[: 2 * fl].astype(jnp.int32)
+            ref[2 * fl * j : 2 * fl * (j + 1), :] = words
     moves = (
         pltpu.make_async_copy(own_ref, own_sm, sems.at[0]),
         pltpu.make_async_copy(words_ref, far_sm, sems.at[1]),
@@ -242,21 +250,19 @@
         move.start()
 
     slots = (
-        (y_ref, 0, 2 - odd),
-        (yc_ref, 0, 3 - 3 * odd),
-        (yf_ref, 0, 1 + odd),
-        (yf_ref, F, 3 * odd),
-    )
-
-    def fill(f, carry):
-        for ref, start, slot in slots:
-            rows = ref[start + f].astype(F32)
-            for g in range(G):
-                block = rows[:, g * LANES : (g + 1) * LANES]
-                x_ref[f * G + g, pl.ds(pl.multiple_of(slot * TILE, TILE), TILE), :] = block
-        return carry
-
-    lax.fori_loop(0, F, fill, 0, unroll=min(F, 4))
+        (near_refs, 0, 2 - odd),
+        (near_refs, fl, 3 - 3 * odd),
+        (far_refs, 0, 1 + odd),
+        (far_refs, fl, 3 * odd),
+    )
+    for group, start, slot in slots:
+        for j in range(nf):
+            for l in range(fl):
+                rows = group[j][start + l].astype(F32)
+                for g in range(G):
+                    block = rows[:, g * LANES : (g + 1) * LANES]
+                    at = pl.ds(pl.multiple_of(slot * TILE, TILE), TILE)
+                    x_ref[(j * fl + l) * G + g, at, :] = block
 
     spot = lax.broadcasted_iota(jnp.int32, (8, LANES), 1)
     for which, ref in enumerate((own_ref, words_ref)):
@@ -265,7 +271,12 @@
             for g in range(G):
                 moved = jnp.take_along_axis(row, 8 * g + spot // TILE, axis=1)
                 idx_ref[which, f * G + g] = (moved + spot) & (LANES - 1)
-    pc_ref[4 * G :, :] = edge_ref[...]
+    first_core = -(-(2 * nsc + wb) // G) * G
+    for j in range(nf):
+        for k in range(2 * nsc):
+            at = 4 * G + (j * 2 * nsc + k) * TILE
+            block = side_block(near_refs[j], 2 * fl, first_core + k)
+            pc_ref[at : at + TILE, :] = block.astype(BF16)
 
     lane = lax.broadcasted_iota(jnp.int32, (TILE, LANES), 1)
     kind = (lane // TILE) % 4
@@ -400,11 +411,12 @@
     pc_ref[0 : 4 * G, :] = jnp.where(at_odd, low, high).astype(BF16)
 
 
-def demosaic_kernel(dims, pack_ref, pc_ref, far_ref, yf_ref, goals_ref, h_ref, *refs):
+def demosaic_kernel(dims, pack_ref, pc_ref, far_ref, goals_ref, h_ref, *refs):
     nf, fl, G, nsc, n_space, inv_pixels = dims
     F = nf * fl
     W = G * LANES
     half = W // 2
+    far_refs, refs = refs[:nf], refs[nf:]
     big_ref, bigt_ref, offs_ref, part_ref, wideh_ref, widel_ref = refs[:6]
     out_ref, goal_ref, mm_ref, p_ref, q_ref, ns_ref = refs[6:]
     s = lax.axis_index("space")
@@ -419,10 +431,8 @@
             first = (j * nsc + c) * 32
             to = pl.ds(pl.multiple_of(at + c * LANES, LANES), LANES)
             goal_ref[1 - odd, :, to] = pc_ref[lead + first : lead + first + 32, :].astype(F32)
-            block = -(-2 * F // 16) + 2 * (j * nsc + c)
-            goal_ref[odd, :, to] = jnp.concatenate(
-                [side_block(yf_ref, 2 * F, block), side_block(yf_ref, 2 * F, block + 1)], axis=0
-            )
+            blocks = [side_block(far_refs[j], 2 * fl, 2 * c + k) for k in range(2)]
+            goal_ref[odd, :, to] = jnp.concatenate(blocks, axis=0)
 
     near = pc_ref[0:lead, :].astype(F32)
     far = far_ref[...]
@@ -619,19 +629,25 @@
     def pieces(value):
         return [value] + [from_frame(value, j) for j in range(1, nf)]
 
-    raws = pieces(raw)
-    goals = pieces(goal)
-    shift_parts = pieces(shifts)
-    y = jnp.pad(raw, ((0, F - fl), (0, 0), (0, 0)))
-    y = lax.optimization_barrier(y)
-    for j in range(1, nf):
-        y = lax.dynamic_update_slice(y, raws[j], (j * fl, 0, 0))
-    yc = involution(y, n_space, 1, 0)
     shape = jax.ShapeDtypeStruct
-    planes = -(-(2 * nf * nsc + -(-2 * F // 16)) // G)
-    *tables, big, bigt, own_rows, side, edge, site_goals = call(
-        functools.partial(table_kernel, (nf, fl, nsc, T)),
-        [weight, *shift_parts, *goals],
+    words = -(-2 * fl // 16)
+    far_planes = -(-(2 * nsc + words) // G)
+    planes = far_planes + -(-2 * nsc // G)
+    raw_core = involution(raw, n_space, 1, 0)
+    (side,) = call(
+        functools.partial(side_kernel, (fl, nsc, T)),
+        [shifts, goal],
+        [shape((planes, TILE, W), BF16)],
+        [pltpu.VMEM((256, LANES), F32), pltpu.VMEM((16 * words, LANES), jnp.int32)],
+    )
+    near = lax.optimization_barrier(jnp.pad(raw, ((0, fl + planes), (0, 0), (0, 0))))
+    near = lax.dynamic_update_slice(near, side, (2 * fl, 0, 0))
+    near = lax.dynamic_update_slice(near, raw_core, (fl, 0, 0))
+    far_own = involution(near[: 2 * fl + far_planes], n_space, 1, 1)
+    nears = pieces(near)
+    *tables, big, bigt = call(
+        table_kernel,
+        [weight],
         [
             shape((256, 256), BF16),
             shape((128, 256), BF16),
@@ -642,22 +658,24 @@
             shape((256, 512), BF16),
             shape((320, 256), BF16),
             shape((96, 320), BF16),
-            shape((2 * F, LANES), jnp.int32),
-            shape((planes, TILE, W), BF16),
-            shape((nf * nsc * channels, LANES), BF16),
-            shape((8, channels, W // 2), F32),
         ],
-        [pltpu.VMEM((6, 40, LANES), F32), pltpu.VMEM((256, LANES), F32)],
-    )
-    pair = jnp.concatenate([y, yc, side], axis=0)
-    yf = involution(pair, n_space, 1, 1)
+        [pltpu.VMEM((6, 40, LANES), F32)],
+    )
     small = jnp.concatenate(
         [jnp.exp(log_var), offset, jnp.zeros((6 * LANES - channels,), F32)]
     ).reshape(8, LANES)
+    fars = pieces(far_own)
+    goals = pieces(goal)
+    (site_goals,) = call(
+        functools.partial(target_kernel, (nf, nsc)),
+        goals,
+        [shape((8, channels, W // 2), F32)],
+        [pltpu.VMEM((256, LANES), F32)],
+    )
 
     pack, pc, far, moments = call(
         functools.partial(merge_kernel, (nf, fl, G, T, nsc)),
-        [own_rows, edge, y, yc, yf, small, *tables[:4]],
+        [*nears, *fars, small, *tables[:4]],
         [
             shape((G, TILE, LANES), F32),
             shape((4 * G + nf * nsc * channels, LANES), BF16),
@@ -671,6 +689,7 @@
             pltpu.VMEM((2, 256, LANES), F32),
             pltpu.VMEM((20 * rows_out, LANES), F32),
             pltpu.VMEM((2 * F, LANES), jnp.int32),
+            pltpu.VMEM((2 * F, LANES), jnp.int32),
             pltpu.SMEM((2 * F, LANES), jnp.int32),
             pltpu.SMEM((2 * F, LANES), jnp.int32),
             pltpu.SemaphoreType.DMA((2,)),
@@ -679,7 +698,7 @@
     pc = involution(pc, n_space, 1, 0)
     (partial,) = call(
         functools.partial(demosaic_kernel, (nf, fl, G, nsc, n_space, inv_pixels)),
-        [pack, pc, far, yf, site_goals, moments, big, bigt, small, *tables[4:]],
+        [pack, pc, far, site_goals, moments, *fars, big, bigt, small, *tables[4:]],
         [shape((16, LANES), F32)],
         [
             pltpu.VMEM((2, channels, W // 2), F32),

time: 37.2 us -> 34 us (0.914)
  starting transfers between devices: 20.1 us -> 14.1 us
  waiting for transfers between devices: 9.99 us -> 13.4 us
  local copies, waits for them, and re-layouts: 1.43 us -> 0.81 us
    ppermute x3, starting transfers between devices: 7.66 us -> 2.35 us  [involution(): return lax.ppermute(value, 'space', pairs)]
    ppermute x3, waiting for transfers between devices: 2.82 us -> 4.57 us  [from_frame(): return lax.ppermute(value, 'frame', [(i, (i - j) % nf) for i in range(nf)])]
    ppermute x1, waiting for transfers between devices: 1.96 us -> 2.83 us  [sum_space(): got = lax.ppermute(value, 'space', [(i, i ^ mask) for i in range(count)])]
    ppermute x1, starting transfers between devices: 2.59 us -> 1.72 us  [sum_space(): got = lax.ppermute(value, 'space', [(i, i ^ mask) for i in range(count)])]
    ppermute x4, waiting for transfers between devices: 4.36 us -> 5.03 us  [sum_space(): got.append(lax.ppermute(value, 'space', [(i, i ^ m) for i in range(count)]))]
    unnamed x10, local copies, waits for them, and re-layouts: 0.66 us -> 0.02 us
    ppermute x4, starting transfers between devices: 4.7 us -> 5.08 us  [sum_space(): got.append(lax.ppermute(value, 'space', [(i, i ^ m) for i in range(count)]))]
    pallas_call x4 -> x6, Pallas kernels: 4.61 us -> 4.63 us  [call(): pl.pallas_call(body, out_shape=tuple(outs), in_specs=[vm] * len(args), ou...]
  transfers between devices with their start and end apart: 11 -> 11, of which waited for: 8 -> 8; matrix products, arithmetic and copies ran while one was open for 2% -> 3% of each run, Pallas kernels for 1% -> 8%
where the time goes in v7:
time: 34 us; the launch traced here: 33.8 us
  starting transfers between devices  14.1 us (41%)
  waiting for transfers between devices  13.4 us (39%)
  Pallas kernels  4.63 us (14%)
  local copies, waits for them, and re-layouts  0.81 us (2%)
  between operations  0.73 us (2%)
    ppermute x4, starting transfers between devices, sum_space(): got.append(lax.ppermute(value, 'space', [(i, i ^ m) for i in range(count)]))  5.08 us
    ppermute x4, waiting for transfers between devices, sum_space(): got.append(lax.ppermute(value, 'space', [(i, i ^ m) for i in range(count)]))  5.03 us
    ppermute x3, starting transfers between devices, from_frame(): return lax.ppermute(value, 'frame', [(i, (i - j) % nf) for i in range(nf)])  4.93 us
    pallas_call x6, Pallas kernels, call(): pl.pallas_call(body, out_shape=tuple(outs), in_specs=[vm] * len(args), ou...  4.63 us
    ppermute x3, waiting for transfers between devices, from_frame(): return lax.ppermute(value, 'frame', [(i, (i - j) % nf) for i in range(nf)])  4.57 us
    ppermute x1, waiting for transfers between devices, sum_space(): got = lax.ppermute(value, 'space', [(i, i ^ mask) for i in range(count)])  2.83 us
    ppermute x3, starting transfers between devices, involution(): return lax.ppermute(value, 'space', pairs)  2.35 us
    ppermute x1, starting transfers between devices, sum_space(): got = lax.ppermute(value, 'space', [(i, i ^ mask) for i in range(count)])  1.72 us
  transfers between devices with their start and end apart: 11, of which 8 were waited for; matrix products, arithmetic and copies ran while one was open for 3% of the time, Pallas kernels for 8%

profile of v7, /device:TPU:0, one launch (start us, length us, event | category | flops | bytes accessed | tf_op | source)
XLA Modules:
  0.0 33.8 jit_solution(15480205006482326415)
XLA Ops:
  0.6 0.0 copy-start
  0.6 0.0 copy-start.2
  0.7 0.6 %collective-permute-start = (bf16[2,16,512]{2,1,0:T(8,128)(2,1)}, bf16[2,16,512]{2,1,0:T(8,128)(2,1)S(1)}, u32[]{:S(2)}, u32[]{:S(2)}) collective-permute-start(bf16[2,16,512]{2,1,0:T(8,128)(2,1)} %param.6), channel_id=1, source_target_pairs={{0,2},{2,0},{4,6},{6,4},{8,10},{10,8},{12,14},{14,12},{16,18},{18,... | collective-permute-start | bytes 98312 | tf_op jit(solution)/shard_map/ppermute | solution.py:576
  1.2 0.8 %pad.4 = bf16[6,16,512]{2,1,0:T(8,128)(2,1)S(1)} pad(bf16[2,16,512]{2,1,0:T(8,128)(2,1)} %param.6, bf16[]{:T(256)} %constant.1.clone.1), padding=0_4x0_0x0_0 | pad | bytes 131074 | tf_op jit(solution)/shard_map/jit(_pad)/pad | solution.py:643
  2.0 0.2 collective-permute-done
  2.3 0.0 copy-start.1
  2.3 0.8 %collective-permute-start.2 = (bf16[5,16,512]{2,1,0:T(8,128)(2,1)S(1)}, bf16[5,16,512]{2,1,0:T(8,128)(2,1)S(1)}, u32[]{:S(2)}, u32[]{:S(2)}) collective-permute-start(bf16[5,16,512]{2,1,0:T(8,128)(2,1)S(1)} %slice.4), channel_id=1, source_target_pairs={{2,4},{4,2},{6,8},{8,6},{10,12},{12,10},{14,16},{16,14},{18,20},{2... | collective-permute-start | bytes 245768 | tf_op jit(solution)/shard_map/ppermute | solution.py:576
  3.1 2.9 %collective-permute-start.5 = (bf16[32,8,128]{2,1,0:T(8,128)(2,1)S(1)}, bf16[32,8,128]{2,1,0:T(8,128)(2,1)S(1)}, u32[]{:S(2)}, u32[]{:S(2)}) collective-permute-start(bf16[32,8,128]{2,1,0:T(8,128)(2,1)S(1)} %copy-done), channel_id=1, source_target_pairs={{0,1},{1,0},{2,3},{3,2},{4,5},{5,4},{6,7},{7,6},{8,9},{9,8},{10,11... | collective-permute-start | bytes 196616 | tf_op jit(solution)/shard_map/ppermute | solution.py:627
  6.0 0.1 collective-permute-start.1
  6.1 0.0 collective-permute-done.2.refs_2_.refs_0_
  6.1 1.9 %collective-permute-start.3 = (bf16[5,16,512]{2,1,0:T(8,128)(2,1)S(1)}, bf16[5,16,512]{2,1,0:T(8,128)(2,1)S(1)}, u32[]{:S(2)}, u32[]{:S(2)}) collective-permute-start(bf16[5,16,512]{2,1,0:T(8,128)(2,1)S(1)} %collective-permute-done.2.refs_2_.refs_0_), channel_id=1, source_target_pairs={{0,1},{1,0},{2,3},{3,2},{4,5},{5,4},{6,7},{7,6},{8,9},{9,8},{10,11... | collective-permute-start | bytes 245768 | tf_op jit(solution)/shard_map/ppermute | solution.py:627
  8.1 0.1 maximum_bitcast_fusion.refs_4_
  8.1 0.3 shard_map.94
  8.5 2.8 %collective-permute-done.1.refs_1_ = bf16[6,16,512]{2,1,0:T(8,128)(2,1)S(1)} collective-permute-done((bf16[6,16,512]{2,1,0:T(8,128)(2,1)S(1)}, bf16[6,16,512]{2,1,0:T(8,128)(2,1)S(1)}, u32[]{:S(2)}, u32[]{:S(2)}) %collective-permute-start.1) | collective-permute-done | bytes 98336 | tf_op jit(solution)/shard_map/ppermute | solution.py:627
  11.3 1.8 %collective-permute-done.3.refs_3_.refs_1_ = bf16[5,16,512]{2,1,0:T(8,128)(2,1)S(1)} collective-permute-done((bf16[5,16,512]{2,1,0:T(8,128)(2,1)S(1)}, bf16[5,16,512]{2,1,0:T(8,128)(2,1)S(1)}, u32[]{:S(2)}, u32[]{:S(2)}) %collective-permute-start.3) | collective-permute-done | bytes 81952 | tf_op jit(solution)/shard_map/ppermute | solution.py:627
  13.0 2.2 %shard_map.95 = (f32[4,16,128]{2,1,0:T(8,128)S(1)}, bf16[80,128]{1,0:T(8,128)(2,1)S(1)}, f32[16,128]{1,0:T(8,128)S(1)}, f32[256,128]{1,0:T(8,128)S(1)}) custom-call(bf16[6,16,512]{2,1,0:T(8,128)(2,1)S(1)} %constant_dynamic-update-slice_fusion.refs_0_, bf16[6,16,512]{2,1,0:T(8,128)(2,1)S(1)} %collective-permute-done.1.refs_1_, ...), custom_call_target="tpu_custom_call" | custom-call | tf_op jit(solution)/shard_map/pallas_call | solution.py:604
  15.2 1.0 %collective-permute-start.4 = (bf16[80,128]{1,0:T(8,128)(2,1)S(1)}, bf16[80,128]{1,0:T(8,128)(2,1)S(1)}, u32[]{:S(2)}, u32[]{:S(2)}) collective-permute-start(bf16[80,128]{1,0:T(8,128)(2,1)S(1)} %get-tuple-element.26), channel_id=1, source_target_pairs={{0,2},{2,0},{4,6},{6,4},{8,10},{10,8},{12,14},{14,12},{16,18},{18,... | collective-permute-start | bytes 61448 | tf_op jit(solution)/shard_map/ppermute | solution.py:576
  16.2 0.0 collective-permute-done.5.refs_1_
  16.2 0.1 shard_map.96.goals_ref
  16.3 0.8 %collective-permute-done.4.pc_ref = bf16[80,128]{1,0:T(8,128)(2,1)S(1)} collective-permute-done((bf16[80,128]{1,0:T(8,128)(2,1)S(1)}, bf16[80,128]{1,0:T(8,128)(2,1)S(1)}, u32[]{:S(2)}, u32[]{:S(2)}) %collective-permute-start.4) | collective-permute-done | bytes 20512 | tf_op jit(solution)/shard_map/ppermute | solution.py:576
  17.1 1.3 %shard_map.97 = f32[16,128]{1,0:T(8,128)S(1)} custom-call(f32[4,16,128]{2,1,0:T(8,128)S(1)} %get-tuple-element.25.pack_ref, bf16[80,128]{1,0:T(8,128)(2,1)S(1)} %collective-permute-done.4.pc_ref, f32[16,128]{1,0:T(8,128)S(1)} %get-tuple-element.27.far_ref, f32[8,32,256]{2,1,0:T(8,128)S(1)} %shard_map.96.goals_ref, f32[256,128]{1,0:T(8,128)S(1)} %get-tuple-element.28.h_ref, ...), custom_call_target="tpu_custom_call" | custom-call | tf_op jit(solution)/shard_map/pallas_call | solution.py:604
  18.3 0.4 %collective-permute-start.6 = (f32[16,128]{1,0:T(8,128)S(1)}, f32[16,128]{1,0:T(8,128)S(1)}, u32[]{:S(2)}, u32[]{:S(2)}) collective-permute-start(f32[16,128]{1,0:T(8,128)S(1)} %shard_map.97), channel_id=1, source_target_pairs={{0,2},{2,0},{4,6},{6,4},{8,10},{10,8},{12,14},{14,12},{16,18},{18,... | collective-permute-start | bytes 24584 | tf_op jit(solution)/shard_map/ppermute | solution.py:591
  18.7 0.8 %collective-permute-done.6 = f32[16,128]{1,0:T(8,128)S(1)} collective-permute-done((f32[16,128]{1,0:T(8,128)S(1)}, f32[16,128]{1,0:T(8,128)S(1)}, u32[]{:S(2)}, u32[]{:S(2)}) %collective-permute-start.6) | collective-permute-done | bytes 8224 | tf_op jit(solution)/shard_map/ppermute | solution.py:591
  19.5 2.8 %collective-permute-start.7 = (f32[16,128]{1,0:T(8,128)S(1)}, f32[16,128]{1,0:T(8,128)S(1)}, u32[]{:S(2)}, u32[]{:S(2)}) collective-permute-start(f32[16,128]{1,0:T(8,128)S(1)} %add.14), channel_id=1, source_target_pairs={{0,4},{2,6},{4,0},{6,2},{8,12},{10,14},{12,8},{14,10},{16,20},{18,... | collective-permute-start | bytes 24584 | tf_op jit(solution)/shard_map/ppermute | solution.py:591
  22.3 1.6 %collective-permute-start.8 = (f32[16,128]{1,0:T(8,128)S(1)}, f32[16,128]{1,0:T(8,128)S(1)}, u32[]{:S(2)}, u32[]{:S(2)}) collective-permute-start(f32[16,128]{1,0:T(8,128)S(1)} %add.14), channel_id=1, source_target_pairs={{0,8},{2,10},{4,12},{6,14},{8,0},{10,2},{12,4},{14,6},{16,24},{18,... | collective-permute-start | bytes 24584 | tf_op jit(solution)/shard_map/ppermute | solution.py:591
  23.9 0.4 %collective-permute-start.9 = (f32[16,128]{1,0:T(8,128)S(1)}, f32[16,128]{1,0:T(8,128)S(1)}, u32[]{:S(2)}, u32[]{:S(2)}) collective-permute-start(f32[16,128]{1,0:T(8,128)S(1)} %add.14), channel_id=1, source_target_pairs={{0,12},{2,14},{4,8},{6,10},{8,4},{10,6},{12,0},{14,2},{16,28},{18,... | collective-permute-start | bytes 24584 | tf_op jit(solution)/shard_map/ppermute | solution.py:591
  24.2 0.0 collective-permute-done.7
  24.2 1.7 %collective-permute-done.8 = f32[16,128]{1,0:T(8,128)S(1)} collective-permute-done((f32[16,128]{1,0:T(8,128)S(1)}, f32[16,128]{1,0:T(8,128)S(1)}, u32[]{:S(2)}, u32[]{:S(2)}) %collective-permute-start.8) | collective-permute-done | bytes 8224 | tf_op jit(solution)/shard_map/ppermute | solution.py:591
  26.0 2.5 %collective-permute-done.9 = f32[16,128]{1,0:T(8,128)S(1)} collective-permute-done((f32[16,128]{1,0:T(8,128)S(1)}, f32[16,128]{1,0:T(8,128)S(1)}, u32[]{:S(2)}, u32[]{:S(2)}) %collective-permute-start.9) | collective-permute-done | bytes 8224 | tf_op jit(solution)/shard_map/ppermute | solution.py:591
  28.4 1.7 %collective-permute-start.10 = (f32[16,128]{1,0:T(8,128)S(1)}, f32[16,128]{1,0:T(8,128)S(1)}, u32[]{:S(2)}, u32[]{:S(2)}) collective-permute-start(f32[16,128]{1,0:T(8,128)S(1)} %add_add_fusion.own_ref), channel_id=1, source_target_pairs={{0,16},{2,18},{4,20},{6,22},{8,24},{10,26},{12,28},{14,30},{16,0},... | collective-permute-start | bytes 24584 | tf_op jit(solution)/shard_map/ppermute | solution.py:596
  30.2 2.8 %collective-permute-done.10.got_ref = f32[16,128]{1,0:T(8,128)S(1)} collective-permute-done((f32[16,128]{1,0:T(8,128)S(1)}, f32[16,128]{1,0:T(8,128)S(1)}, u32[]{:S(2)}, u32[]{:S(2)}) %collective-permute-start.10) | collective-permute-done | bytes 8224 | tf_op jit(solution)/shard_map/ppermute | solution.py:596
  33.0 0.8 %shard_map.98 = (f32[16,256]{1,0:T(8,128)}, f32[32,36]{1,0:T(8,128)}, f32[1,32]{1,0:T(1,128)}, f32[2,128]{1,0:T(2,128)}) custom-call(f32[4,16,128]{2,1,0:T(8,128)S(1)} %get-tuple-element.25.pack_ref, f32[16,128]{1,0:T(8,128)S(1)} %add_add_fusion.own_ref, f32[16,128]{1,0:T(8,128)S(1)} %collective-permute-done.10.got_ref), custom_call_target="tpu_custom_call" | custom-call | tf_op jit(solution)/shard_map/pallas_call | solution.py:604
  (15 shorter events, 0.1 us)
Async XLA Ops:
  0.6 1.3 %copy-start = (bf16[32,8,128]{2,1,0:T(8,128)(2,1)S(1)}, bf16[32,8,128]{2,1,0:T(8,128)(2,1)}, u32[]{:S(2)}) copy-start(bf16[32,8,128]{2,1,0:T(8,128)(2,1)} %refs_0_.1) | copy-start | bytes 196612
  0.6 1.3 %copy-start.2 = (s32[2,2,1,32]{3,2,1,0:T(1,128)S(1)}, s32[2,2,1,32]{3,2,1,0:T(1,128)}, u32[]{:S(2)}) copy-start(s32[2,2,1,32]{3,2,1,0:T(1,128)} %shift_ref.1) | copy-start | bytes 1540
  0.7 1.6 %collective-permute-start = (bf16[2,16,512]{2,1,0:T(8,128)(2,1)}, bf16[2,16,512]{2,1,0:T(8,128)(2,1)S(1)}, u32[]{:S(2)}, u32[]{:S(2)}) collective-permute-start(bf16[2,16,512]{2,1,0:T(8,128)(2,1)} %param.6), channel_id=1, source_target_pairs={{0,2},{2,0},{4,6},{6,4},{8,10},{10,8},{12,14},{14,12},{16,18},{18,... | collective-permute-start | bytes 98312 | tf_op jit(solution)/shard_map/ppermute | solution.py:576
  2.3 3.7 %copy-start.3 = (f32[256]{0:T(256)S(1)}, f32[256]{0:T(256)}, u32[]{:S(2)}) copy-start(f32[256]{0:T(256)} %param.10) | copy-start | bytes 3076
  2.3 5.8 %copy-start.4 = (f32[32]{0:T(128)S(1)}, f32[32]{0:T(128)}, u32[]{:S(2)}) copy-start(f32[32]{0:T(128)} %param.9) | copy-start | bytes 388
  2.3 5.8 %copy-start.1 = (bf16[32,36]{1,0:T(8,128)(2,1)S(1)}, bf16[32,36]{1,0:T(8,128)(2,1)}, u32[]{:S(2)}) copy-start(bf16[32,36]{1,0:T(8,128)(2,1)} %weight_ref.1) | copy-start | bytes 6916
  2.3 3.8 %collective-permute-start.2 = (bf16[5,16,512]{2,1,0:T(8,128)(2,1)S(1)}, bf16[5,16,512]{2,1,0:T(8,128)(2,1)S(1)}, u32[]{:S(2)}, u32[]{:S(2)}) collective-permute-start(bf16[5,16,512]{2,1,0:T(8,128)(2,1)S(1)} %slice.4), channel_id=1, source_target_pairs={{2,4},{4,2},{6,8},{8,6},{10,12},{12,10},{14,16},{16,14},{18,20},{2... | collective-permute-start | bytes 245768 | tf_op jit(solution)/shard_map/ppermute | solution.py:576
  3.1 13.1 %collective-permute-start.5 = (bf16[32,8,128]{2,1,0:T(8,128)(2,1)S(1)}, bf16[32,8,128]{2,1,0:T(8,128)(2,1)S(1)}, u32[]{:S(2)}, u32[]{:S(2)}) collective-permute-start(bf16[32,8,128]{2,1,0:T(8,128)(2,1)S(1)} %copy-done), channel_id=1, source_target_pairs={{0,1},{1,0},{2,3},{3,2},{4,5},{5,4},{6,7},{7,6},{8,9},{9,8},{10,11... | collective-permute-start | bytes 196616 | tf_op jit(solution)/shard_map/ppermute | solution.py:627
  6.0 5.3 %collective-permute-start.1 = (bf16[6,16,512]{2,1,0:T(8,128)(2,1)S(1)}, bf16[6,16,512]{2,1,0:T(8,128)(2,1)S(1)}, u32[]{:S(2)}, u32[]{:S(2)}) collective-permute-start(bf16[6,16,512]{2,1,0:T(8,128)(2,1)S(1)} %constant_dynamic-update-slice_fusion.refs_0_), channel_id=1, source_target_pairs={{0,1},{1,0},{2,3},{3,2},{4,5},{5,4},{6,7},{7,6},{8,9},{9,8},{10,11... | collective-permute-start | bytes 294920 | tf_op jit(solution)/shard_map/ppermute | solution.py:627
  6.1 6.9 %collective-permute-start.3 = (bf16[5,16,512]{2,1,0:T(8,128)(2,1)S(1)}, bf16[5,16,512]{2,1,0:T(8,128)(2,1)S(1)}, u32[]{:S(2)}, u32[]{:S(2)}) collective-permute-start(bf16[5,16,512]{2,1,0:T(8,128)(2,1)S(1)} %collective-permute-done.2.refs_2_.refs_0_), channel_id=1, source_target_pairs={{0,1},{1,0},{2,3},{3,2},{4,5},{5,4},{6,7},{7,6},{8,9},{9,8},{10,11... | collective-permute-start | bytes 245768 | tf_op jit(solution)/shard_map/ppermute | solution.py:627
  15.2 1.8 %collective-permute-start.4 = (bf16[80,128]{1,0:T(8,128)(2,1)S(1)}, bf16[80,128]{1,0:T(8,128)(2,1)S(1)}, u32[]{:S(2)}, u32[]{:S(2)}) collective-permute-start(bf16[80,128]{1,0:T(8,128)(2,1)S(1)} %get-tuple-element.26), channel_id=1, source_target_pairs={{0,2},{2,0},{4,6},{6,4},{8,10},{10,8},{12,14},{14,12},{16,18},{18,... | collective-permute-start | bytes 61448 | tf_op jit(solution)/shard_map/ppermute | solution.py:576
  18.3 1.2 %collective-permute-start.6 = (f32[16,128]{1,0:T(8,128)S(1)}, f32[16,128]{1,0:T(8,128)S(1)}, u32[]{:S(2)}, u32[]{:S(2)}) collective-permute-start(f32[16,128]{1,0:T(8,128)S(1)} %shard_map.97), channel_id=1, source_target_pairs={{0,2},{2,0},{4,6},{6,4},{8,10},{10,8},{12,14},{14,12},{16,18},{18,... | collective-permute-start | bytes 24584 | tf_op jit(solution)/shard_map/ppermute | solution.py:591
  19.5 4.7 %collective-permute-start.7 = (f32[16,128]{1,0:T(8,128)S(1)}, f32[16,128]{1,0:T(8,128)S(1)}, u32[]{:S(2)}, u32[]{:S(2)}) collective-permute-start(f32[16,128]{1,0:T(8,128)S(1)} %add.14), channel_id=1, source_target_pairs={{0,4},{2,6},{4,0},{6,2},{8,12},{10,14},{12,8},{14,10},{16,20},{18,... | collective-permute-start | bytes 24584 | tf_op jit(solution)/shard_map/ppermute | solution.py:591
  22.3 3.7 %collective-permute-start.8 = (f32[16,128]{1,0:T(8,128)S(1)}, f32[16,128]{1,0:T(8,128)S(1)}, u32[]{:S(2)}, u32[]{:S(2)}) collective-permute-start(f32[16,128]{1,0:T(8,128)S(1)} %add.14), channel_id=1, source_target_pairs={{0,8},{2,10},{4,12},{6,14},{8,0},{10,2},{12,4},{14,6},{16,24},{18,... | collective-permute-start | bytes 24584 | tf_op jit(solution)/shard_map/ppermute | solution.py:591
  23.9 4.5 %collective-permute-start.9 = (f32[16,128]{1,0:T(8,128)S(1)}, f32[16,128]{1,0:T(8,128)S(1)}, u32[]{:S(2)}, u32[]{:S(2)}) collective-permute-start(f32[16,128]{1,0:T(8,128)S(1)} %add.14), channel_id=1, source_target_pairs={{0,12},{2,14},{4,8},{6,10},{8,4},{10,6},{12,0},{14,2},{16,28},{18,... | collective-permute-start | bytes 24584 | tf_op jit(solution)/shard_map/ppermute | solution.py:591
  28.4 4.5 %collective-permute-start.10 = (f32[16,128]{1,0:T(8,128)S(1)}, f32[16,128]{1,0:T(8,128)S(1)}, u32[]{:S(2)}, u32[]{:S(2)}) collective-permute-start(f32[16,128]{1,0:T(8,128)S(1)} %add_add_fusion.own_ref), channel_id=1, source_target_pairs={{0,16},{2,18},{4,20},{6,22},{8,24},{10,26},{12,28},{14,30},{16,0},... | collective-permute-start | bytes 24584 | tf_op jit(solution)/shard_map/ppermute | solution.py:596

commit v8 on v7

--- a/solution.py
+++ b/solution.py
@@ -117,10 +117,10 @@
         edge = raw_ref[pl.ds(7 - 7 * odd, 32, stride=8), :]
         core += [edge[:16], edge[16:]]
     words = words_ref[...].astype(F32)
-    blocks = far + [words[16 * k : 16 * k + 16] for k in range(words.shape[0] // 16)]
-    blocks += [jnp.zeros((TILE, LANES), F32)] * (-len(blocks) % G)
-    blocks += core
-    blocks += [jnp.zeros((TILE, LANES), F32)] * (-len(blocks) % G)
+    words = [words[16 * k : 16 * k + 16] for k in range(words.shape[0] // 16)]
+    blocks = []
+    for group in (words + core, far + words):
+        blocks += group + [jnp.zeros((TILE, LANES), F32)] * (-len(group) % G)
     for k, block in enumerate(blocks):
         at = (k % G) * LANES
         side_ref[k // G, :, at : at + LANES] = block.astype(BF16)
@@ -237,9 +237,9 @@
     odd = lax.rem(s, 2)
 
     wb = -(-2 * fl // 16)
-    for group, ref in ((near_refs, own_ref), (far_refs, words_ref)):
+    for group, ref, at in ((near_refs, own_ref, 0), (far_refs, words_ref, 2 * nsc)):
         for j in range(nf):
-            words = [side_block(group[j], 2 * fl, 2 * nsc + k) for k in range(wb)]
+            words = [side_block(group[j], 2 * fl, at + k) for k in range(wb)]
             words = jnp.concatenate(words, axis=0)[: 2 * fl].astype(jnp.int32)
             ref[2 * fl * j : 2 * fl * (j + 1), :] = words
     moves = (
@@ -271,11 +271,10 @@
             for g in range(G):
                 moved = jnp.take_along_axis(row, 8 * g + spot // TILE, axis=1)
                 idx_ref[which, f * G + g] = (moved + spot) & (LANES - 1)
-    first_core = -(-(2 * nsc + wb) // G) * G
     for j in range(nf):
         for k in range(2 * nsc):
             at = 4 * G + (j * 2 * nsc + k) * TILE
-            block = side_block(near_refs[j], 2 * fl, first_core + k)
+            block = side_block(near_refs[j], 2 * fl, wb + k)
             pc_ref[at : at + TILE, :] = block.astype(BF16)
 
     lane = lax.broadcasted_iota(jnp.int32, (TILE, LANES), 1)
@@ -631,19 +630,19 @@
 
     shape = jax.ShapeDtypeStruct
     words = -(-2 * fl // 16)
-    far_planes = -(-(2 * nsc + words) // G)
-    planes = far_planes + -(-2 * nsc // G)
+    planes = -(-(2 * nsc + words) // G)
     raw_core = involution(raw, n_space, 1, 0)
     (side,) = call(
         functools.partial(side_kernel, (fl, nsc, T)),
         [shifts, goal],
-        [shape((planes, TILE, W), BF16)],
+        [shape((2 * planes, TILE, W), BF16)],
         [pltpu.VMEM((256, LANES), F32), pltpu.VMEM((16 * words, LANES), jnp.int32)],
     )
     near = lax.optimization_barrier(jnp.pad(raw, ((0, fl + planes), (0, 0), (0, 0))))
-    near = lax.dynamic_update_slice(near, side, (2 * fl, 0, 0))
+    near = lax.dynamic_update_slice(near, side[:planes], (2 * fl, 0, 0))
     near = lax.dynamic_update_slice(near, raw_core, (fl, 0, 0))
-    far_own = involution(near[: 2 * fl + far_planes], n_space, 1, 1)
+    far_own = jnp.concatenate([near[: 2 * fl], side[planes:]], axis=0)
+    far_own = involution(far_own, n_space, 1, 1)
     nears = pieces(near)
     *tables, big, bigt = call(
         table_kernel,

time: 34 us -> 33.8 us (level)
  waiting for transfers between devices: 13.4 us -> 13 us
    ppermute x3, waiting for transfers between devices: 4.57 us -> 4.22 us  [from_frame(): return lax.ppermute(value, 'frame', [(i, (i - j) % nf) for i in range(nf)])]
where the time goes in v8:
time: 33.8 us; the launch traced here: 33.6 us
  starting transfers between devices  14.3 us (42%)
  waiting for transfers between devices  13 us (38%)
  Pallas kernels  4.63 us (14%)
  local copies, waits for them, and re-layouts  0.81 us (2%)
  between operations  0.74 us (2%)
    ppermute x4, starting transfers between devices, sum_space(): got.append(lax.ppermute(value, 'space', [(i, i ^ m) for i in range(count)]))  5.4 us
    ppermute x4, waiting for transfers between devices, sum_space(): got.append(lax.ppermute(value, 'space', [(i, i ^ m) for i in range(count)]))  4.98 us
    ppermute x3, starting transfers between devices, from_frame(): return lax.ppermute(value, 'frame', [(i, (i - j) % nf) for i in range(nf)])  4.92 us
    pallas_call x6, Pallas kernels, call(): pl.pallas_call(body, out_shape=tuple(outs), in_specs=[vm] * len(args), ou...  4.63 us
    ppermute x3, waiting for transfers between devices, from_frame(): return lax.ppermute(value, 'frame', [(i, (i - j) % nf) for i in range(nf)])  4.22 us
    ppermute x1, waiting for transfers between devices, sum_space(): got = lax.ppermute(value, 'space', [(i, i ^ mask) for i in range(count)])  2.74 us
    ppermute x3, starting transfers between devices, involution(): return lax.ppermute(value, 'space', pairs)  2.22 us
    ppermute x1, starting transfers between devices, sum_space(): got = lax.ppermute(value, 'space', [(i, i ^ mask) for i in range(count)])  1.81 us
  transfers between devices with their start and end apart: 11, of which 8 were waited for; matrix products, arithmetic and copies ran while one was open for 3% of the time, Pallas kernels for 8%

profile of v8, /device:TPU:0, one launch (start us, length us, event | category | flops | bytes accessed | tf_op | source)
XLA Modules:
  0.0 33.6 jit_solution(3992143273979414458)
XLA Ops:
  0.7 0.6 %collective-permute-start = (bf16[2,16,512]{2,1,0:T(8,128)(2,1)}, bf16[2,16,512]{2,1,0:T(8,128)(2,1)S(1)}, u32[]{:S(2)}, u32[]{:S(2)}) collective-permute-start(bf16[2,16,512]{2,1,0:T(8,128)(2,1)} %param.6), channel_id=1, source_target_pairs={{0,2},{2,0},{4,6},{6,4},{8,10},{10,8},{12,14},{14,12},{16,18},{18,... | collective-permute-start | bytes 98312 | tf_op jit(solution)/shard_map/ppermute | solution.py:575
  1.2 0.8 %pad.4 = bf16[5,16,512]{2,1,0:T(8,128)(2,1)S(1)} pad(bf16[2,16,512]{2,1,0:T(8,128)(2,1)} %param.6, bf16[]{:T(256)} %constant.1.clone.1), padding=0_3x0_0x0_0 | pad | bytes 114690 | tf_op jit(solution)/shard_map/jit(_pad)/pad | solution.py:641
  2.0 0.3 collective-permute-done
  2.3 0.0 copy-start.3
  2.3 0.0 copy-start.4
  2.3 0.0 copy-start.1
  2.3 0.7 %collective-permute-start.2 = (bf16[5,16,512]{2,1,0:T(8,128)(2,1)S(1)}, bf16[5,16,512]{2,1,0:T(8,128)(2,1)S(1)}, u32[]{:S(2)}, u32[]{:S(2)}) collective-permute-start(bf16[5,16,512]{2,1,0:T(8,128)(2,1)S(1)} %pad_maximum_fusion), channel_id=1, source_target_pairs={{2,4},{4,2},{6,8},{8,6},{10,12},{12,10},{14,16},{16,14},{18,20},{2... | collective-permute-start | bytes 245768 | tf_op jit(solution)/shard_map/ppermute | solution.py:575
  3.0 2.9 %collective-permute-start.5 = (bf16[32,8,128]{2,1,0:T(8,128)(2,1)S(1)}, bf16[32,8,128]{2,1,0:T(8,128)(2,1)S(1)}, u32[]{:S(2)}, u32[]{:S(2)}) collective-permute-start(bf16[32,8,128]{2,1,0:T(8,128)(2,1)S(1)} %copy-done), channel_id=1, source_target_pairs={{0,1},{1,0},{2,3},{3,2},{4,5},{5,4},{6,7},{7,6},{8,9},{9,8},{10,11... | collective-permute-start | bytes 196616 | tf_op jit(solution)/shard_map/ppermute | solution.py:626
  5.9 0.1 collective-permute-start.1
  6.0 0.0 collective-permute-done.2.refs_2_.refs_0_
  6.0 1.9 %collective-permute-start.3 = (bf16[5,16,512]{2,1,0:T(8,128)(2,1)S(1)}, bf16[5,16,512]{2,1,0:T(8,128)(2,1)S(1)}, u32[]{:S(2)}, u32[]{:S(2)}) collective-permute-start(bf16[5,16,512]{2,1,0:T(8,128)(2,1)S(1)} %collective-permute-done.2.refs_2_.refs_0_), channel_id=1, source_target_pairs={{0,1},{1,0},{2,3},{3,2},{4,5},{5,4},{6,7},{7,6},{8,9},{9,8},{10,11... | collective-permute-start | bytes 245768 | tf_op jit(solution)/shard_map/ppermute | solution.py:626
  8.0 0.1 maximum_bitcast_fusion.refs_4_
  8.0 0.3 shard_map.94
  8.4 2.5 %collective-permute-done.1.refs_1_ = bf16[5,16,512]{2,1,0:T(8,128)(2,1)S(1)} collective-permute-done((bf16[5,16,512]{2,1,0:T(8,128)(2,1)S(1)}, bf16[5,16,512]{2,1,0:T(8,128)(2,1)S(1)}, u32[]{:S(2)}, u32[]{:S(2)}) %collective-permute-start.1) | collective-permute-done | bytes 81952 | tf_op jit(solution)/shard_map/ppermute | solution.py:626
  10.8 1.8 %collective-permute-done.3.refs_3_.refs_1_ = bf16[5,16,512]{2,1,0:T(8,128)(2,1)S(1)} collective-permute-done((bf16[5,16,512]{2,1,0:T(8,128)(2,1)S(1)}, bf16[5,16,512]{2,1,0:T(8,128)(2,1)S(1)}, u32[]{:S(2)}, u32[]{:S(2)}) %collective-permute-start.3) | collective-permute-done | bytes 81952 | tf_op jit(solution)/shard_map/ppermute | solution.py:626
  12.6 2.2 %shard_map.95 = (f32[4,16,128]{2,1,0:T(8,128)S(1)}, bf16[80,128]{1,0:T(8,128)(2,1)S(1)}, f32[16,128]{1,0:T(8,128)S(1)}, f32[256,128]{1,0:T(8,128)S(1)}) custom-call(bf16[5,16,512]{2,1,0:T(8,128)(2,1)S(1)} %constant_dynamic-update-slice_fusion.refs_0_, bf16[5,16,512]{2,1,0:T(8,128)(2,1)S(1)} %collective-permute-done.1.refs_1_, ...), custom_call_target="tpu_custom_call" | custom-call | tf_op jit(solution)/shard_map/pallas_call | solution.py:603
  14.8 1.0 %collective-permute-start.4 = (bf16[80,128]{1,0:T(8,128)(2,1)S(1)}, bf16[80,128]{1,0:T(8,128)(2,1)S(1)}, u32[]{:S(2)}, u32[]{:S(2)}) collective-permute-start(bf16[80,128]{1,0:T(8,128)(2,1)S(1)} %get-tuple-element.26), channel_id=1, source_target_pairs={{0,2},{2,0},{4,6},{6,4},{8,10},{10,8},{12,14},{14,12},{16,18},{18,... | collective-permute-start | bytes 61448 | tf_op jit(solution)/shard_map/ppermute | solution.py:575
  15.8 0.0 collective-permute-done.5.refs_1_
  15.8 0.1 shard_map.96.goals_ref
  15.8 0.8 %collective-permute-done.4.pc_ref = bf16[80,128]{1,0:T(8,128)(2,1)S(1)} collective-permute-done((bf16[80,128]{1,0:T(8,128)(2,1)S(1)}, bf16[80,128]{1,0:T(8,128)(2,1)S(1)}, u32[]{:S(2)}, u32[]{:S(2)}) %collective-permute-start.4) | collective-permute-done | bytes 20512 | tf_op jit(solution)/shard_map/ppermute | solution.py:575
  16.6 1.3 %shard_map.97 = f32[16,128]{1,0:T(8,128)S(1)} custom-call(f32[4,16,128]{2,1,0:T(8,128)S(1)} %get-tuple-element.25.pack_ref, bf16[80,128]{1,0:T(8,128)(2,1)S(1)} %collective-permute-done.4.pc_ref, f32[16,128]{1,0:T(8,128)S(1)} %get-tuple-element.27.far_ref, f32[8,32,256]{2,1,0:T(8,128)S(1)} %shard_map.96.goals_ref, f32[256,128]{1,0:T(8,128)S(1)} %get-tuple-element.28.h_ref, ...), custom_call_target="tpu_custom_call" | custom-call | tf_op jit(solution)/shard_map/pallas_call | solution.py:603
  17.9 0.4 %collective-permute-start.6 = (f32[16,128]{1,0:T(8,128)S(1)}, f32[16,128]{1,0:T(8,128)S(1)}, u32[]{:S(2)}, u32[]{:S(2)}) collective-permute-start(f32[16,128]{1,0:T(8,128)S(1)} %shard_map.97), channel_id=1, source_target_pairs={{0,2},{2,0},{4,6},{6,4},{8,10},{10,8},{12,14},{14,12},{16,18},{18,... | collective-permute-start | bytes 24584 | tf_op jit(solution)/shard_map/ppermute | solution.py:590
  18.3 0.8 %collective-permute-done.6 = f32[16,128]{1,0:T(8,128)S(1)} collective-permute-done((f32[16,128]{1,0:T(8,128)S(1)}, f32[16,128]{1,0:T(8,128)S(1)}, u32[]{:S(2)}, u32[]{:S(2)}) %collective-permute-start.6) | collective-permute-done | bytes 8224 | tf_op jit(solution)/shard_map/ppermute | solution.py:590
  19.1 3.0 %collective-permute-start.7 = (f32[16,128]{1,0:T(8,128)S(1)}, f32[16,128]{1,0:T(8,128)S(1)}, u32[]{:S(2)}, u32[]{:S(2)}) collective-permute-start(f32[16,128]{1,0:T(8,128)S(1)} %add.14), channel_id=1, source_target_pairs={{0,4},{2,6},{4,0},{6,2},{8,12},{10,14},{12,8},{14,10},{16,20},{18,... | collective-permute-start | bytes 24584 | tf_op jit(solution)/shard_map/ppermute | solution.py:590
  22.1 1.6 %collective-permute-start.8 = (f32[16,128]{1,0:T(8,128)S(1)}, f32[16,128]{1,0:T(8,128)S(1)}, u32[]{:S(2)}, u32[]{:S(2)}) collective-permute-start(f32[16,128]{1,0:T(8,128)S(1)} %add.14), channel_id=1, source_target_pairs={{0,8},{2,10},{4,12},{6,14},{8,0},{10,2},{12,4},{14,6},{16,24},{18,... | collective-permute-start | bytes 24584 | tf_op jit(solution)/shard_map/ppermute | solution.py:590
  23.7 0.4 %collective-permute-start.9 = (f32[16,128]{1,0:T(8,128)S(1)}, f32[16,128]{1,0:T(8,128)S(1)}, u32[]{:S(2)}, u32[]{:S(2)}) collective-permute-start(f32[16,128]{1,0:T(8,128)S(1)} %add.14), channel_id=1, source_target_pairs={{0,12},{2,14},{4,8},{6,10},{8,4},{10,6},{12,0},{14,2},{16,28},{18,... | collective-permute-start | bytes 24584 | tf_op jit(solution)/shard_map/ppermute | solution.py:590
  24.1 0.0 collective-permute-done.7
  24.1 1.7 %collective-permute-done.8 = f32[16,128]{1,0:T(8,128)S(1)} collective-permute-done((f32[16,128]{1,0:T(8,128)S(1)}, f32[16,128]{1,0:T(8,128)S(1)}, u32[]{:S(2)}, u32[]{:S(2)}) %collective-permute-start.8) | collective-permute-done | bytes 8224 | tf_op jit(solution)/shard_map/ppermute | solution.py:590
  25.8 2.5 %collective-permute-done.9 = f32[16,128]{1,0:T(8,128)S(1)} collective-permute-done((f32[16,128]{1,0:T(8,128)S(1)}, f32[16,128]{1,0:T(8,128)S(1)}, u32[]{:S(2)}, u32[]{:S(2)}) %collective-permute-start.9) | collective-permute-done | bytes 8224 | tf_op jit(solution)/shard_map/ppermute | solution.py:590
  28.2 1.8 %collective-permute-start.10 = (f32[16,128]{1,0:T(8,128)S(1)}, f32[16,128]{1,0:T(8,128)S(1)}, u32[]{:S(2)}, u32[]{:S(2)}) collective-permute-start(f32[16,128]{1,0:T(8,128)S(1)} %add_add_fusion.own_ref), channel_id=1, source_target_pairs={{0,16},{2,18},{4,20},{6,22},{8,24},{10,26},{12,28},{14,30},{16,0},... | collective-permute-start | bytes 24584 | tf_op jit(solution)/shard_map/ppermute | solution.py:595
  30.1 2.7 %collective-permute-done.10.got_ref = f32[16,128]{1,0:T(8,128)S(1)} collective-permute-done((f32[16,128]{1,0:T(8,128)S(1)}, f32[16,128]{1,0:T(8,128)S(1)}, u32[]{:S(2)}, u32[]{:S(2)}) %collective-permute-start.10) | collective-permute-done | bytes 8224 | tf_op jit(solution)/shard_map/ppermute | solution.py:595
  32.8 0.8 %shard_map.98 = (f32[16,256]{1,0:T(8,128)}, f32[32,36]{1,0:T(8,128)}, f32[1,32]{1,0:T(1,128)}, f32[2,128]{1,0:T(2,128)}) custom-call(f32[4,16,128]{2,1,0:T(8,128)S(1)} %get-tuple-element.25.pack_ref, f32[16,128]{1,0:T(8,128)S(1)} %add_add_fusion.own_ref, f32[16,128]{1,0:T(8,128)S(1)} %collective-permute-done.10.got_ref), custom_call_target="tpu_custom_call" | custom-call | tf_op jit(solution)/shard_map/pallas_call | solution.py:603
  (16 shorter events, 0.1 us)
Async XLA Ops:
  0.6 1.3 %copy-start = (bf16[32,8,128]{2,1,0:T(8,128)(2,1)S(1)}, bf16[32,8,128]{2,1,0:T(8,128)(2,1)}, u32[]{:S(2)}) copy-start(bf16[32,8,128]{2,1,0:T(8,128)(2,1)} %refs_0_.1) | copy-start | bytes 196612
  0.6 1.3 %copy-start.2 = (s32[2,2,1,32]{3,2,1,0:T(1,128)S(1)}, s32[2,2,1,32]{3,2,1,0:T(1,128)}, u32[]{:S(2)}) copy-start(s32[2,2,1,32]{3,2,1,0:T(1,128)} %shift_ref.1) | copy-start | bytes 1540
  0.7 1.6 %collective-permute-start = (bf16[2,16,512]{2,1,0:T(8,128)(2,1)}, bf16[2,16,512]{2,1,0:T(8,128)(2,1)S(1)}, u32[]{:S(2)}, u32[]{:S(2)}) collective-permute-start(bf16[2,16,512]{2,1,0:T(8,128)(2,1)} %param.6), channel_id=1, source_target_pairs={{0,2},{2,0},{4,6},{6,4},{8,10},{10,8},{12,14},{14,12},{16,18},{18,... | collective-permute-start | bytes 98312 | tf_op jit(solution)/shard_map/ppermute | solution.py:575
  2.3 3.6 %copy-start.3 = (f32[256]{0:T(256)S(1)}, f32[256]{0:T(256)}, u32[]{:S(2)}) copy-start(f32[256]{0:T(256)} %param.10) | copy-start | bytes 3076
  2.3 5.7 %copy-start.4 = (f32[32]{0:T(128)S(1)}, f32[32]{0:T(128)}, u32[]{:S(2)}) copy-start(f32[32]{0:T(128)} %param.9) | copy-start | bytes 388
  2.3 5.7 %copy-start.1 = (bf16[32,36]{1,0:T(8,128)(2,1)S(1)}, bf16[32,36]{1,0:T(8,128)(2,1)}, u32[]{:S(2)}) copy-start(bf16[32,36]{1,0:T(8,128)(2,1)} %weight_ref.1) | copy-start | bytes 6916
  2.3 3.7 %collective-permute-start.2 = (bf16[5,16,512]{2,1,0:T(8,128)(2,1)S(1)}, bf16[5,16,512]{2,1,0:T(8,128)(2,1)S(1)}, u32[]{:S(2)}, u32[]{:S(2)}) collective-permute-start(bf16[5,16,512]{2,1,0:T(8,128)(2,1)S(1)} %pad_maximum_fusion), channel_id=1, source_target_pairs={{2,4},{4,2},{6,8},{8,6},{10,12},{12,10},{14,16},{16,14},{18,20},{2... | collective-permute-start | bytes 245768 | tf_op jit(solution)/shard_map/ppermute | solution.py:575
  3.0 12.7 %collective-permute-start.5 = (bf16[32,8,128]{2,1,0:T(8,128)(2,1)S(1)}, bf16[32,8,128]{2,1,0:T(8,128)(2,1)S(1)}, u32[]{:S(2)}, u32[]{:S(2)}) collective-permute-start(bf16[32,8,128]{2,1,0:T(8,128)(2,1)S(1)} %copy-done), channel_id=1, source_target_pairs={{0,1},{1,0},{2,3},{3,2},{4,5},{5,4},{6,7},{7,6},{8,9},{9,8},{10,11... | collective-permute-start | bytes 196616 | tf_op jit(solution)/shard_map/ppermute | solution.py:626
  5.9 4.9 %collective-permute-start.1 = (bf16[5,16,512]{2,1,0:T(8,128)(2,1)S(1)}, bf16[5,16,512]{2,1,0:T(8,128)(2,1)S(1)}, u32[]{:S(2)}, u32[]{:S(2)}) collective-permute-start(bf16[5,16,512]{2,1,0:T(8,128)(2,1)S(1)} %constant_dynamic-update-slice_fusion.refs_0_), channel_id=1, source_target_pairs={{0,1},{1,0},{2,3},{3,2},{4,5},{5,4},{6,7},{7,6},{8,9},{9,8},{10,11... | collective-permute-start | bytes 245768 | tf_op jit(solution)/shard_map/ppermute | solution.py:626
  6.0 6.6 %collective-permute-start.3 = (bf16[5,16,512]{2,1,0:T(8,128)(2,1)S(1)}, bf16[5,16,512]{2,1,0:T(8,128)(2,1)S(1)}, u32[]{:S(2)}, u32[]{:S(2)}) collective-permute-start(bf16[5,16,512]{2,1,0:T(8,128)(2,1)S(1)} %collective-permute-done.2.refs_2_.refs_0_), channel_id=1, source_target_pairs={{0,1},{1,0},{2,3},{3,2},{4,5},{5,4},{6,7},{7,6},{8,9},{9,8},{10,11... | collective-permute-start | bytes 245768 | tf_op jit(solution)/shard_map/ppermute | solution.py:626
  14.8 1.8 %collective-permute-start.4 = (bf16[80,128]{1,0:T(8,128)(2,1)S(1)}, bf16[80,128]{1,0:T(8,128)(2,1)S(1)}, u32[]{:S(2)}, u32[]{:S(2)}) collective-permute-start(bf16[80,128]{1,0:T(8,128)(2,1)S(1)} %get-tuple-element.26), channel_id=1, source_target_pairs={{0,2},{2,0},{4,6},{6,4},{8,10},{10,8},{12,14},{14,12},{16,18},{18,... | collective-permute-start | bytes 61448 | tf_op jit(solution)/shard_map/ppermute | solution.py:575
  17.9 1.2 %collective-permute-start.6 = (f32[16,128]{1,0:T(8,128)S(1)}, f32[16,128]{1,0:T(8,128)S(1)}, u32[]{:S(2)}, u32[]{:S(2)}) collective-permute-start(f32[16,128]{1,0:T(8,128)S(1)} %shard_map.97), channel_id=1, source_target_pairs={{0,2},{2,0},{4,6},{6,4},{8,10},{10,8},{12,14},{14,12},{16,18},{18,... | collective-permute-start | bytes 24584 | tf_op jit(solution)/shard_map/ppermute | solution.py:590
  19.1 5.0 %collective-permute-start.7 = (f32[16,128]{1,0:T(8,128)S(1)}, f32[16,128]{1,0:T(8,128)S(1)}, u32[]{:S(2)}, u32[]{:S(2)}) collective-permute-start(f32[16,128]{1,0:T(8,128)S(1)} %add.14), channel_id=1, source_target_pairs={{0,4},{2,6},{4,0},{6,2},{8,12},{10,14},{12,8},{14,10},{16,20},{18,... | collective-permute-start | bytes 24584 | tf_op jit(solution)/shard_map/ppermute | solution.py:590
  22.1 3.7 %collective-permute-start.8 = (f32[16,128]{1,0:T(8,128)S(1)}, f32[16,128]{1,0:T(8,128)S(1)}, u32[]{:S(2)}, u32[]{:S(2)}) collective-permute-start(f32[16,128]{1,0:T(8,128)S(1)} %add.14), channel_id=1, source_target_pairs={{0,8},{2,10},{4,12},{6,14},{8,0},{10,2},{12,4},{14,6},{16,24},{18,... | collective-permute-start | bytes 24584 | tf_op jit(solution)/shard_map/ppermute | solution.py:590
  23.7 4.5 %collective-permute-start.9 = (f32[16,128]{1,0:T(8,128)S(1)}, f32[16,128]{1,0:T(8,128)S(1)}, u32[]{:S(2)}, u32[]{:S(2)}) collective-permute-start(f32[16,128]{1,0:T(8,128)S(1)} %add.14), channel_id=1, source_target_pairs={{0,12},{2,14},{4,8},{6,10},{8,4},{10,6},{12,0},{14,2},{16,28},{18,... | collective-permute-start | bytes 24584 | tf_op jit(solution)/shard_map/ppermute | solution.py:590
  28.2 4.5 %collective-permute-start.10 = (f32[16,128]{1,0:T(8,128)S(1)}, f32[16,128]{1,0:T(8,128)S(1)}, u32[]{:S(2)}, u32[]{:S(2)}) collective-permute-start(f32[16,128]{1,0:T(8,128)S(1)} %add_add_fusion.own_ref), channel_id=1, source_target_pairs={{0,16},{2,18},{4,20},{6,22},{8,24},{10,26},{12,28},{14,30},{16,0},... | collective-permute-start | bytes 24584 | tf_op jit(solution)/shard_map/ppermute | solution.py:595

commit v9 on v8

--- a/solution.py
+++ b/solution.py
@@ -542,11 +542,14 @@
     out_ref[...] = jnp.concatenate([first, second], axis=0)
 
 
-def last_sum(nf, pack_ref, own_ref, got_ref, merged_ref, weight_ref, bias_ref, noise_ref):
+def store_merged(nf, pack_ref, merged_ref):
     own = pack_ref.shape[0] // nf
     fr = lax.axis_index("frame")
     for k in range(own):
         merged_ref[:, k * LANES : (k + 1) * LANES] = pack_ref[fr * own + k]
+
+
+def last_sum(own_ref, got_ref, weight_ref, bias_ref, noise_ref):
     total = own_ref[...] + got_ref[...]
     first, second = total[:8], total[8:]
     gw = jnp.concatenate(
@@ -707,11 +710,11 @@
             pltpu.VMEM((rows_out * TILE, LANES), F32),
         ],
     )
-    merged, grad_weight, grad_bias, grad_noise = call(
-        functools.partial(last_sum, nf),
-        [pack, *sum_space(partial, n_space)],
+    (merged,) = call(functools.partial(store_merged, nf), [pack], [shape((TILE, W // nf), F32)], [])
+    grad_weight, grad_bias, grad_noise = call(
+        last_sum,
+        sum_space(partial, n_space),
         [
-            shape((TILE, W // nf), F32),
             shape((channels, 36), F32),
             shape((1, channels), F32),
             shape((2, LANES), F32),

time: 33.8 us -> 33.8 us (level)
  waiting for transfers between devices: 13 us -> 12.3 us
  Pallas kernels: 4.63 us -> 5.24 us
    ppermute x1, waiting for transfers between devices: 2.74 us -> 2.13 us  [sum_space(): got = lax.ppermute(value, 'space', [(i, i ^ mask) for i in range(count)])]
    pallas_call x6 -> x7, Pallas kernels: 4.63 us -> 5.24 us  [call(): pl.pallas_call(body, out_shape=tuple(outs), in_specs=[vm] * len(args), ou...]
  transfers between devices with their start and end apart: 11 -> 11, of which waited for: 8 -> 8; matrix products, arithmetic and copies ran while one was open for 3% -> 3% of each run, Pallas kernels for 8% -> 10%
where the time goes in v9:
time: 33.8 us; the launch traced here: 33.6 us
  starting transfers between devices  14.3 us (42%)
  waiting for transfers between devices  12.3 us (36%)
  Pallas kernels  5.24 us (16%)
  local copies, waits for them, and re-layouts  0.81 us (2%)
  between operations  0.74 us (2%)
    ppermute x4, starting transfers between devices, sum_space(): got.append(lax.ppermute(value, 'space', [(i, i ^ m) for i in range(count)]))  5.4 us
    pallas_call x7, Pallas kernels, call(): pl.pallas_call(body, out_shape=tuple(outs), in_specs=[vm] * len(args), ou...  5.24 us
    ppermute x4, waiting for transfers between devices, sum_space(): got.append(lax.ppermute(value, 'space', [(i, i ^ m) for i in range(count)]))  4.98 us
    ppermute x3, starting transfers between devices, from_frame(): return lax.ppermute(value, 'frame', [(i, (i - j) % nf) for i in range(nf)])  4.92 us
    ppermute x3, waiting for transfers between devices, from_frame(): return lax.ppermute(value, 'frame', [(i, (i - j) % nf) for i in range(nf)])  4.22 us
    ppermute x3, starting transfers between devices, involution(): return lax.ppermute(value, 'space', pairs)  2.22 us
    ppermute x1, waiting for transfers between devices, sum_space(): got = lax.ppermute(value, 'space', [(i, i ^ mask) for i in range(count)])  2.13 us
    ppermute x1, starting transfers between devices, sum_space(): got = lax.ppermute(value, 'space', [(i, i ^ mask) for i in range(count)])  1.81 us
  transfers between devices with their start and end apart: 11, of which 8 were waited for; matrix products, arithmetic and copies ran while one was open for 3% of the time, Pallas kernels for 10%

profile of v9, /device:TPU:0, one launch (start us, length us, event | category | flops | bytes accessed | tf_op | source)
XLA Modules:
  0.0 33.6 jit_solution(4982265172354774266)
XLA Ops:
  0.7 0.6 %collective-permute-start = (bf16[2,16,512]{2,1,0:T(8,128)(2,1)}, bf16[2,16,512]{2,1,0:T(8,128)(2,1)S(1)}, u32[]{:S(2)}, u32[]{:S(2)}) collective-permute-start(bf16[2,16,512]{2,1,0:T(8,128)(2,1)} %param.6), channel_id=1, source_target_pairs={{0,2},{2,0},{4,6},{6,4},{8,10},{10,8},{12,14},{14,12},{16,18},{18,... | collective-permute-start | bytes 98312 | tf_op jit(solution)/shard_map/ppermute | solution.py:578
  1.2 0.8 %pad.4 = bf16[5,16,512]{2,1,0:T(8,128)(2,1)S(1)} pad(bf16[2,16,512]{2,1,0:T(8,128)(2,1)} %param.6, bf16[]{:T(256)} %constant.1.clone.1), padding=0_3x0_0x0_0 | pad | bytes 114690 | tf_op jit(solution)/shard_map/jit(_pad)/pad | solution.py:644
  2.0 0.3 collective-permute-done
  2.3 0.0 copy-start.3
  2.3 0.0 copy-start.4
  2.3 0.0 copy-start.1
  2.3 0.7 %collective-permute-start.2 = (bf16[5,16,512]{2,1,0:T(8,128)(2,1)S(1)}, bf16[5,16,512]{2,1,0:T(8,128)(2,1)S(1)}, u32[]{:S(2)}, u32[]{:S(2)}) collective-permute-start(bf16[5,16,512]{2,1,0:T(8,128)(2,1)S(1)} %pad_maximum_fusion), channel_id=1, source_target_pairs={{2,4},{4,2},{6,8},{8,6},{10,12},{12,10},{14,16},{16,14},{18,20},{2... | collective-permute-start | bytes 245768 | tf_op jit(solution)/shard_map/ppermute | solution.py:578
  3.0 2.9 %collective-permute-start.5 = (bf16[32,8,128]{2,1,0:T(8,128)(2,1)S(1)}, bf16[32,8,128]{2,1,0:T(8,128)(2,1)S(1)}, u32[]{:S(2)}, u32[]{:S(2)}) collective-permute-start(bf16[32,8,128]{2,1,0:T(8,128)(2,1)S(1)} %copy-done), channel_id=1, source_target_pairs={{0,1},{1,0},{2,3},{3,2},{4,5},{5,4},{6,7},{7,6},{8,9},{9,8},{10,11... | collective-permute-start | bytes 196616 | tf_op jit(solution)/shard_map/ppermute | solution.py:629
  5.9 0.1 collective-permute-start.1
  6.0 0.0 collective-permute-done.2.refs_2_.refs_0_
  6.0 1.9 %collective-permute-start.3 = (bf16[5,16,512]{2,1,0:T(8,128)(2,1)S(1)}, bf16[5,16,512]{2,1,0:T(8,128)(2,1)S(1)}, u32[]{:S(2)}, u32[]{:S(2)}) collective-permute-start(bf16[5,16,512]{2,1,0:T(8,128)(2,1)S(1)} %collective-permute-done.2.refs_2_.refs_0_), channel_id=1, source_target_pairs={{0,1},{1,0},{2,3},{3,2},{4,5},{5,4},{6,7},{7,6},{8,9},{9,8},{10,11... | collective-permute-start | bytes 245768 | tf_op jit(solution)/shard_map/ppermute | solution.py:629
  8.0 0.1 maximum_bitcast_fusion.refs_4_
  8.0 0.3 shard_map.94
  8.4 2.5 %collective-permute-done.1.refs_1_ = bf16[5,16,512]{2,1,0:T(8,128)(2,1)S(1)} collective-permute-done((bf16[5,16,512]{2,1,0:T(8,128)(2,1)S(1)}, bf16[5,16,512]{2,1,0:T(8,128)(2,1)S(1)}, u32[]{:S(2)}, u32[]{:S(2)}) %collective-permute-start.1) | collective-permute-done | bytes 81952 | tf_op jit(solution)/shard_map/ppermute | solution.py:629
  10.8 1.8 %collective-permute-done.3.refs_3_.refs_1_ = bf16[5,16,512]{2,1,0:T(8,128)(2,1)S(1)} collective-permute-done((bf16[5,16,512]{2,1,0:T(8,128)(2,1)S(1)}, bf16[5,16,512]{2,1,0:T(8,128)(2,1)S(1)}, u32[]{:S(2)}, u32[]{:S(2)}) %collective-permute-start.3) | collective-permute-done | bytes 81952 | tf_op jit(solution)/shard_map/ppermute | solution.py:629
  12.6 2.2 %shard_map.95 = (f32[4,16,128]{2,1,0:T(8,128)S(1)}, bf16[80,128]{1,0:T(8,128)(2,1)S(1)}, f32[16,128]{1,0:T(8,128)S(1)}, f32[256,128]{1,0:T(8,128)S(1)}) custom-call(bf16[5,16,512]{2,1,0:T(8,128)(2,1)S(1)} %constant_dynamic-update-slice_fusion.refs_0_, bf16[5,16,512]{2,1,0:T(8,128)(2,1)S(1)} %collective-permute-done.1.refs_1_, ...), custom_call_target="tpu_custom_call" | custom-call | tf_op jit(solution)/shard_map/pallas_call | solution.py:606
  14.8 1.0 %collective-permute-start.4 = (bf16[80,128]{1,0:T(8,128)(2,1)S(1)}, bf16[80,128]{1,0:T(8,128)(2,1)S(1)}, u32[]{:S(2)}, u32[]{:S(2)}) collective-permute-start(bf16[80,128]{1,0:T(8,128)(2,1)S(1)} %get-tuple-element.25), channel_id=1, source_target_pairs={{0,2},{2,0},{4,6},{6,4},{8,10},{10,8},{12,14},{14,12},{16,18},{18,... | collective-permute-start | bytes 61448 | tf_op jit(solution)/shard_map/ppermute | solution.py:578
  15.8 0.0 collective-permute-done.5.refs_1_
  15.8 0.1 shard_map.97.goals_ref
  15.8 0.8 %collective-permute-done.4.pc_ref = bf16[80,128]{1,0:T(8,128)(2,1)S(1)} collective-permute-done((bf16[80,128]{1,0:T(8,128)(2,1)S(1)}, bf16[80,128]{1,0:T(8,128)(2,1)S(1)}, u32[]{:S(2)}, u32[]{:S(2)}) %collective-permute-start.4) | collective-permute-done | bytes 20512 | tf_op jit(solution)/shard_map/ppermute | solution.py:578
  16.6 1.3 %shard_map.98 = f32[16,128]{1,0:T(8,128)S(1)} custom-call(f32[4,16,128]{2,1,0:T(8,128)S(1)} %get-tuple-element.24.pack_ref, bf16[80,128]{1,0:T(8,128)(2,1)S(1)} %collective-permute-done.4.pc_ref, f32[16,128]{1,0:T(8,128)S(1)} %get-tuple-element.26.far_ref, f32[8,32,256]{2,1,0:T(8,128)S(1)} %shard_map.97.goals_ref, f32[256,128]{1,0:T(8,128)S(1)} %get-tuple-element.27.h_ref, ...), custom_call_target="tpu_custom_call" | custom-call | tf_op jit(solution)/shard_map/pallas_call | solution.py:606
  17.9 0.4 %collective-permute-start.6 = (f32[16,128]{1,0:T(8,128)S(1)}, f32[16,128]{1,0:T(8,128)S(1)}, u32[]{:S(2)}, u32[]{:S(2)}) collective-permute-start(f32[16,128]{1,0:T(8,128)S(1)} %shard_map.98), channel_id=1, source_target_pairs={{0,2},{2,0},{4,6},{6,4},{8,10},{10,8},{12,14},{14,12},{16,18},{18,... | collective-permute-start | bytes 24584 | tf_op jit(solution)/shard_map/ppermute | solution.py:593
  18.3 0.8 %collective-permute-done.6 = f32[16,128]{1,0:T(8,128)S(1)} collective-permute-done((f32[16,128]{1,0:T(8,128)S(1)}, f32[16,128]{1,0:T(8,128)S(1)}, u32[]{:S(2)}, u32[]{:S(2)}) %collective-permute-start.6) | collective-permute-done | bytes 8224 | tf_op jit(solution)/shard_map/ppermute | solution.py:593
  19.1 3.0 %collective-permute-start.7 = (f32[16,128]{1,0:T(8,128)S(1)}, f32[16,128]{1,0:T(8,128)S(1)}, u32[]{:S(2)}, u32[]{:S(2)}) collective-permute-start(f32[16,128]{1,0:T(8,128)S(1)} %add.14), channel_id=1, source_target_pairs={{0,4},{2,6},{4,0},{6,2},{8,12},{10,14},{12,8},{14,10},{16,20},{18,... | collective-permute-start | bytes 24584 | tf_op jit(solution)/shard_map/ppermute | solution.py:593
  22.1 1.6 %collective-permute-start.8 = (f32[16,128]{1,0:T(8,128)S(1)}, f32[16,128]{1,0:T(8,128)S(1)}, u32[]{:S(2)}, u32[]{:S(2)}) collective-permute-start(f32[16,128]{1,0:T(8,128)S(1)} %add.14), channel_id=1, source_target_pairs={{0,8},{2,10},{4,12},{6,14},{8,0},{10,2},{12,4},{14,6},{16,24},{18,... | collective-permute-start | bytes 24584 | tf_op jit(solution)/shard_map/ppermute | solution.py:593
  23.7 0.4 %collective-permute-start.9 = (f32[16,128]{1,0:T(8,128)S(1)}, f32[16,128]{1,0:T(8,128)S(1)}, u32[]{:S(2)}, u32[]{:S(2)}) collective-permute-start(f32[16,128]{1,0:T(8,128)S(1)} %add.14), channel_id=1, source_target_pairs={{0,12},{2,14},{4,8},{6,10},{8,4},{10,6},{12,0},{14,2},{16,28},{18,... | collective-permute-start | bytes 24584 | tf_op jit(solution)/shard_map/ppermute | solution.py:593
  24.1 1.7 %collective-permute-done.8 = f32[16,128]{1,0:T(8,128)S(1)} collective-permute-done((f32[16,128]{1,0:T(8,128)S(1)}, f32[16,128]{1,0:T(8,128)S(1)}, u32[]{:S(2)}, u32[]{:S(2)}) %collective-permute-start.8) | collective-permute-done | bytes 8224 | tf_op jit(solution)/shard_map/ppermute | solution.py:593
  25.8 2.5 %collective-permute-done.9 = f32[16,128]{1,0:T(8,128)S(1)} collective-permute-done((f32[16,128]{1,0:T(8,128)S(1)}, f32[16,128]{1,0:T(8,128)S(1)}, u32[]{:S(2)}, u32[]{:S(2)}) %collective-permute-start.9) | collective-permute-done | bytes 8224 | tf_op jit(solution)/shard_map/ppermute | solution.py:593
  28.2 1.8 %collective-permute-start.10 = (f32[16,128]{1,0:T(8,128)S(1)}, f32[16,128]{1,0:T(8,128)S(1)}, u32[]{:S(2)}, u32[]{:S(2)}) collective-permute-start(f32[16,128]{1,0:T(8,128)S(1)} %add_add_fusion.own_ref), channel_id=1, source_target_pairs={{0,16},{2,18},{4,20},{6,22},{8,24},{10,26},{12,28},{14,30},{16,0},... | collective-permute-start | bytes 24584 | tf_op jit(solution)/shard_map/ppermute | solution.py:598
  30.1 0.6 %shard_map.96 = f32[16,256]{1,0:T(8,128)} custom-call(f32[4,16,128]{2,1,0:T(8,128)S(1)} %get-tuple-element.24.pack_ref), custom_call_target="tpu_custom_call" | custom-call | tf_op jit(solution)/shard_map/pallas_call | solution.py:606
  30.7 2.1 %collective-permute-done.10.got_ref = f32[16,128]{1,0:T(8,128)S(1)} collective-permute-done((f32[16,128]{1,0:T(8,128)S(1)}, f32[16,128]{1,0:T(8,128)S(1)}, u32[]{:S(2)}, u32[]{:S(2)}) %collective-permute-start.10) | collective-permute-done | bytes 8224 | tf_op jit(solution)/shard_map/ppermute | solution.py:598
  32.8 0.8 %shard_map.99 = (f32[32,36]{1,0:T(8,128)}, f32[1,32]{1,0:T(1,128)}, f32[2,128]{1,0:T(2,128)}) custom-call(f32[16,128]{1,0:T(8,128)S(1)} %add_add_fusion.own_ref, f32[16,128]{1,0:T(8,128)S(1)} %collective-permute-done.10.got_ref), custom_call_target="tpu_custom_call" | custom-call | tf_op jit(solution)/shard_map/pallas_call | solution.py:606
  (17 shorter events, 0.1 us)
Async XLA Ops:
  0.6 1.3 %copy-start = (bf16[32,8,128]{2,1,0:T(8,128)(2,1)S(1)}, bf16[32,8,128]{2,1,0:T(8,128)(2,1)}, u32[]{:S(2)}) copy-start(bf16[32,8,128]{2,1,0:T(8,128)(2,1)} %refs_0_.1) | copy-start | bytes 196612
  0.6 1.3 %copy-start.2 = (s32[2,2,1,32]{3,2,1,0:T(1,128)S(1)}, s32[2,2,1,32]{3,2,1,0:T(1,128)}, u32[]{:S(2)}) copy-start(s32[2,2,1,32]{3,2,1,0:T(1,128)} %shift_ref.1) | copy-start | bytes 1540
  0.7 1.6 %collective-permute-start = (bf16[2,16,512]{2,1,0:T(8,128)(2,1)}, bf16[2,16,512]{2,1,0:T(8,128)(2,1)S(1)}, u32[]{:S(2)}, u32[]{:S(2)}) collective-permute-start(bf16[2,16,512]{2,1,0:T(8,128)(2,1)} %param.6), channel_id=1, source_target_pairs={{0,2},{2,0},{4,6},{6,4},{8,10},{10,8},{12,14},{14,12},{16,18},{18,... | collective-permute-start | bytes 98312 | tf_op jit(solution)/shard_map/ppermute | solution.py:578
  2.3 3.6 %copy-start.3 = (f32[256]{0:T(256)S(1)}, f32[256]{0:T(256)}, u32[]{:S(2)}) copy-start(f32[256]{0:T(256)} %param.10) | copy-start | bytes 3076
  2.3 5.7 %copy-start.4 = (f32[32]{0:T(128)S(1)}, f32[32]{0:T(128)}, u32[]{:S(2)}) copy-start(f32[32]{0:T(128)} %param.9) | copy-start | bytes 388
  2.3 5.7 %copy-start.1 = (bf16[32,36]{1,0:T(8,128)(2,1)S(1)}, bf16[32,36]{1,0:T(8,128)(2,1)}, u32[]{:S(2)}) copy-start(bf16[32,36]{1,0:T(8,128)(2,1)} %weight_ref.1) | copy-start | bytes 6916
  2.3 3.7 %collective-permute-start.2 = (bf16[5,16,512]{2,1,0:T(8,128)(2,1)S(1)}, bf16[5,16,512]{2,1,0:T(8,128)(2,1)S(1)}, u32[]{:S(2)}, u32[]{:S(2)}) collective-permute-start(bf16[5,16,512]{2,1,0:T(8,128)(2,1)S(1)} %pad_maximum_fusion), channel_id=1, source_target_pairs={{2,4},{4,2},{6,8},{8,6},{10,12},{12,10},{14,16},{16,14},{18,20},{2... | collective-permute-start | bytes 245768 | tf_op jit(solution)/shard_map/ppermute | solution.py:578
  3.0 12.7 %collective-permute-start.5 = (bf16[32,8,128]{2,1,0:T(8,128)(2,1)S(1)}, bf16[32,8,128]{2,1,0:T(8,128)(2,1)S(1)}, u32[]{:S(2)}, u32[]{:S(2)}) collective-permute-start(bf16[32,8,128]{2,1,0:T(8,128)(2,1)S(1)} %copy-done), channel_id=1, source_target_pairs={{0,1},{1,0},{2,3},{3,2},{4,5},{5,4},{6,7},{7,6},{8,9},{9,8},{10,11... | collective-permute-start | bytes 196616 | tf_op jit(solution)/shard_map/ppermute | solution.py:629
  5.9 4.9 %collective-permute-start.1 = (bf16[5,16,512]{2,1,0:T(8,128)(2,1)S(1)}, bf16[5,16,512]{2,1,0:T(8,128)(2,1)S(1)}, u32[]{:S(2)}, u32[]{:S(2)}) collective-permute-start(bf16[5,16,512]{2,1,0:T(8,128)(2,1)S(1)} %constant_dynamic-update-slice_fusion.refs_0_), channel_id=1, source_target_pairs={{0,1},{1,0},{2,3},{3,2},{4,5},{5,4},{6,7},{7,6},{8,9},{9,8},{10,11... | collective-permute-start | bytes 245768 | tf_op jit(solution)/shard_map/ppermute | solution.py:629
  6.0 6.6 %collective-permute-start.3 = (bf16[5,16,512]{2,1,0:T(8,128)(2,1)S(1)}, bf16[5,16,512]{2,1,0:T(8,128)(2,1)S(1)}, u32[]{:S(2)}, u32[]{:S(2)}) collective-permute-start(bf16[5,16,512]{2,1,0:T(8,128)(2,1)S(1)} %collective-permute-done.2.refs_2_.refs_0_), channel_id=1, source_target_pairs={{0,1},{1,0},{2,3},{3,2},{4,5},{5,4},{6,7},{7,6},{8,9},{9,8},{10,11... | collective-permute-start | bytes 245768 | tf_op jit(solution)/shard_map/ppermute | solution.py:629
  14.8 1.8 %collective-permute-start.4 = (bf16[80,128]{1,0:T(8,128)(2,1)S(1)}, bf16[80,128]{1,0:T(8,128)(2,1)S(1)}, u32[]{:S(2)}, u32[]{:S(2)}) collective-permute-start(bf16[80,128]{1,0:T(8,128)(2,1)S(1)} %get-tuple-element.25), channel_id=1, source_target_pairs={{0,2},{2,0},{4,6},{6,4},{8,10},{10,8},{12,14},{14,12},{16,18},{18,... | collective-permute-start | bytes 61448 | tf_op jit(solution)/shard_map/ppermute | solution.py:578
  17.9 1.2 %collective-permute-start.6 = (f32[16,128]{1,0:T(8,128)S(1)}, f32[16,128]{1,0:T(8,128)S(1)}, u32[]{:S(2)}, u32[]{:S(2)}) collective-permute-start(f32[16,128]{1,0:T(8,128)S(1)} %shard_map.98), channel_id=1, source_target_pairs={{0,2},{2,0},{4,6},{6,4},{8,10},{10,8},{12,14},{14,12},{16,18},{18,... | collective-permute-start | bytes 24584 | tf_op jit(solution)/shard_map/ppermute | solution.py:593
  19.1 5.0 %collective-permute-start.7 = (f32[16,128]{1,0:T(8,128)S(1)}, f32[16,128]{1,0:T(8,128)S(1)}, u32[]{:S(2)}, u32[]{:S(2)}) collective-permute-start(f32[16,128]{1,0:T(8,128)S(1)} %add.14), channel_id=1, source_target_pairs={{0,4},{2,6},{4,0},{6,2},{8,12},{10,14},{12,8},{14,10},{16,20},{18,... | collective-permute-start | bytes 24584 | tf_op jit(solution)/shard_map/ppermute | solution.py:593
  22.1 3.7 %collective-permute-start.8 = (f32[16,128]{1,0:T(8,128)S(1)}, f32[16,128]{1,0:T(8,128)S(1)}, u32[]{:S(2)}, u32[]{:S(2)}) collective-permute-start(f32[16,128]{1,0:T(8,128)S(1)} %add.14), channel_id=1, source_target_pairs={{0,8},{2,10},{4,12},{6,14},{8,0},{10,2},{12,4},{14,6},{16,24},{18,... | collective-permute-start | bytes 24584 | tf_op jit(solution)/shard_map/ppermute | solution.py:593
  23.7 4.5 %collective-permute-start.9 = (f32[16,128]{1,0:T(8,128)S(1)}, f32[16,128]{1,0:T(8,128)S(1)}, u32[]{:S(2)}, u32[]{:S(2)}) collective-permute-start(f32[16,128]{1,0:T(8,128)S(1)} %add.14), channel_id=1, source_target_pairs={{0,12},{2,14},{4,8},{6,10},{8,4},{10,6},{12,0},{14,2},{16,28},{18,... | collective-permute-start | bytes 24584 | tf_op jit(solution)/shard_map/ppermute | solution.py:593
  28.2 4.5 %collective-permute-start.10 = (f32[16,128]{1,0:T(8,128)S(1)}, f32[16,128]{1,0:T(8,128)S(1)}, u32[]{:S(2)}, u32[]{:S(2)}) collective-permute-start(f32[16,128]{1,0:T(8,128)S(1)} %add_add_fusion.own_ref), channel_id=1, source_target_pairs={{0,16},{2,18},{4,20},{6,22},{8,24},{10,26},{12,28},{14,30},{16,0},... | collective-permute-start | bytes 24584 | tf_op jit(solution)/shard_map/ppermute | solution.py:598
